TPU v7x, 32 devices: a whole 2x2x4 slice. The times are simulated.
32 devices in a mesh: term: 8 (over z, x), sector: 4 (over y, core).
Axes of the slice: x: 2, y: 2, z: 4, core: 2. Of those that a mesh axis runs over, the one named last changes fastest.
Arguments:
- psi_start: float32 [4, 384, 384], P('sector'), may hold values from -6 to 6
- diagonal: float32 [4, 384, 384], P('sector'), may hold values from -3 to 3
- left_ops: float32 [128, 384, 384], P(('term', 'sector')), may hold values from -0.3125 to 0.3125
- right_ops: float32 [128, 384, 384], P(('term', 'sector')), may hold values from -0.078125 to 0.078125
- pair_in: int32 [32, 4], P(('term', 'sector')), may hold values from 0 to 3
- pair_out: int32 [32, 4], P(('term', 'sector')), may hold values from 0 to 3
- pair_count: int32 [32], P(('term', 'sector')), may hold values from 1 to 4, as said below
Outputs:
- psi_final: float32 [4, 384, 384], P('sector')
- energies: float32 [2], replicated
Inputs may be any that keep to these rules, and one draw needn't show every extreme that they name: `pair_count`: some device has all 4 slots live in every draw.
All inputs are finite; a program needn't handle non-finite values.
Results may differ from a plain program's by a relative error of at most 0.00013.
Values sent between devices are 32-bit elements; how exact they have to be, the bound alone decides.
No kernel may reach another device: no remote copies, remote signals or barrier semaphores. Data moves between devices by JAX's collectives and lax.ppermute only.
A program may use at most 64 MiB of HBM per device.

v0:
```python
import functools

import jax
import jax.numpy as jnp
from jax import lax
from jax.experimental import pallas as pl
from jax.experimental.pallas import tpu as pltpu
from jax.sharding import PartitionSpec as P


ITERS = 2
AXES = ("term", "sector")
TILE = (8, 128)
CHUNKS = 2

epsilon = 1e-06


VMEM = pl.BlockSpec(memory_space=pltpu.VMEM)
SMEM = pl.BlockSpec(memory_space=pltpu.SMEM)
F32 = jnp.float32
BF16 = jnp.bfloat16

DIMS = (("sector", 1), ("term", 0), ("term", 1))
CORE = ("sector", 0)
ORDERS = ((0, 1, 2), (2, 1, 0))


def matmul_cost(pairs, rows, b):
    return pl.CostEstimate(
        flops=6 * pairs * rows * b * b, bytes_accessed=8 * pairs * b * b, transcendentals=0
    )


def grant(mib):
    return pltpu.CompilerParams(vmem_limit_bytes=mib << 20)


def bit_of(axis, bit):
    return (lax.axis_index(axis) >> bit) & 1


def place(bits, parity, rows):
    return 2 * bits[0] + parity, pl.multiple_of((2 * bits[1] + bits[2]) * rows, 8)


def piece_place(k, parity, rows):
    return place([bit_of(*dim) ^ ((k >> (2 - i)) & 1) for i, dim in enumerate(DIMS)], parity, rows)


def slot_bits(j, order):
    flip = [0, 0, 0]
    for i, dim in enumerate(order):
        flip[dim] = (j >> (2 - i)) & 1
    return flip


def slot_place(j, parity, rows):
    a, b = slot_bits(j, ORDERS[0]), slot_bits(j, ORDERS[1])
    flip = [x if x == y else jnp.where(parity == 0, x, y) for x, y in zip(a, b)]
    return place([bit_of(*dim) ^ f for dim, f in zip(DIMS, flip)], parity, rows)


def split(x):
    high = x.astype(BF16)
    return high, (x - high.astype(F32)).astype(BF16)


def segments(first, rows, shard):
    me = lax.axis_index("sector")
    if first:
        out = [[(h, me ^ side, h * rows, 0, rows) for h in range(CHUNKS)] for side in range(2)]
        out += [[(h, me ^ (2 + side), 0, 0, rows)] for h in range(CHUNKS) for side in range(2)]
        return out
    out = []
    for number in range(16):
        sector, row = piece_place(number >> 1, (me & 1) ^ (number & 1), shard)
        out.append([(h, sector, h * shard, row, shard) for h in range(CHUNKS)])
    return out


def prep_kernel(left_ref, right_ref, psi_ref, diag_ref, left_cat, right_cat, vec_ref, mine_ref):
    b = left_ref.shape[-1]

    def one(p, carry):
        high, low = split(left_ref[p])
        for place, x in enumerate((high, low, high)):
            left_cat[p, :, place * b:(place + 1) * b] = x
        high, low = split(right_ref[p])
        for place, x in enumerate((high, high, low)):
            right_cat[p, :, place * b:(place + 1) * b] = x
        return carry

    lax.fori_loop(0, left_ref.shape[0], one, 0)
    rows = vec_ref.shape[0] // CHUNKS
    for h in range(CHUNKS):
        _, row = piece_place(0, 0, rows)
        at = pl.ds(pl.multiple_of(row + h * 4 * rows, 8), rows)
        vec_ref[h * rows:(h + 1) * rows, :] = psi_ref[0, at, :]
        mine_ref[h * rows:(h + 1) * rows, :] = diag_ref[0, at, :]


def prepare(left_ops, right_ops, psi, diag):
    pairs, b, _ = left_ops.shape
    shard = jax.ShapeDtypeStruct((b // 4, b), F32)
    return pl.pallas_call(
        prep_kernel,
        in_specs=[VMEM] * 4,
        out_specs=[VMEM] * 4,
        out_shape=[jax.ShapeDtypeStruct((pairs, b, 3 * b), BF16)] * 2 + [shard] * 2,
        compiler_params=grant(16),
        cost_estimate=pl.CostEstimate(
            flops=4 * left_ops.size, bytes_accessed=20 * left_ops.size, transcendentals=0
        ),
    )(left_ops, right_ops, psi, diag)


def store_wide(dest, start, x):
    rows = x.shape[0]
    for c in range(x.shape[1] // TILE[1]):
        dest[start + c * rows:start + (c + 1) * rows, :] = x[:, c * TILE[1]:(c + 1) * TILE[1]]


DOT_NT = functools.partial(
    lax.dot_general, dimension_numbers=(((1,), (1,)), ((), ())), preferred_element_type=F32
)
DOT = functools.partial(jnp.dot, preferred_element_type=F32)


def inner_kernel(first, half, cells, pieces, *refs):
    in_ref, count_ref, *refs = refs
    parts = refs[:pieces]
    refs = refs[pieces:]
    if half:
        right, early_h, early_l, squares_ref, cat_ref, inv_ref, vec = refs
    else:
        right, early_h, early_l, squares_ref, vec = refs
    _, rows, _ = vec.shape
    b = right.shape[1]
    shard = rows // 4
    x_bit = bit_of(*DIMS[1])
    side = x_bit ^ half
    total = jnp.zeros((1, b), F32)
    cuts_of = segments(first, rows, shard)
    for piece, cuts in zip(parts, [cuts_of[i] for i in picked(first, half)]):
        for chunk, sector, start, row, size in cuts:
            if first and chunk != half:
                continue
            x = piece[start:start + size, :]
            high, low = split(x)
            total += jnp.sum(x * x, axis=0, keepdims=True)
            if not first:
                row = pl.multiple_of(row - side * 2 * shard + chunk * 2 * shard, 16)
            at = pl.ds(row, size)
            for place, y in enumerate((high, low, high)):
                vec[sector, at, place * b:(place + 1) * b] = y
    total = jnp.broadcast_to(jnp.sum(total, axis=1, keepdims=True), (TILE[0], b))
    if half:
        inv_ref[...] = lax.rsqrt((total + squares_ref[...]) / cells + epsilon)
    else:
        squares_ref[...] = total

    def one_pair(p, carry):
        high, low = split(DOT_NT(vec[in_ref[0, p]], right[p]))
        if not half:
            early_h[p], early_l[p] = high, low
            return carry
        for which, (h, l) in enumerate(((early_h[p], early_l[p]), (high, low))):
            if first:
                moves = [(0, rows, which * rows)]
            else:
                moves = [
                    (c * 2 * shard, 2 * shard, pl.multiple_of(c * rows + (x_bit ^ which) * 2 * shard, 16))
                    for c in range(CHUNKS)
                ]
            for start, size, row in moves:
                for place, y in enumerate((h, h, l)):
                    cat_ref[p, pl.ds(place * b + row, size), :] = y[start:start + size, :]
        return carry

    lax.fori_loop(0, count_ref[0], one_pair, 0)


def picked(first, half):
    if first:
        return [0, 1, 2 + 2 * half, 3 + 2 * half]
    return [number for number in range(16) if (number >> 2) & 1 == half]


def inner(first, half, cells, sectors, pair_in, pair_count, pieces, right, early=()):
    pairs, b, _ = right.shape
    rows = b // 2
    compact = jax.ShapeDtypeStruct((pairs, rows, b), BF16)
    row = jax.ShapeDtypeStruct((TILE[0], b), F32)
    shapes = [jax.ShapeDtypeStruct((pairs, 3 * b, b), BF16), row] if half else [compact, compact, row]
    return pl.pallas_call(
        functools.partial(inner_kernel, first, half, cells, len(pieces)),
        in_specs=[SMEM] * 2 + [VMEM] * (len(pieces) + 1 + len(early)),
        out_specs=[VMEM] * len(shapes),
        out_shape=shapes,
        scratch_shapes=[pltpu.VMEM((sectors, rows, 3 * b), BF16)],
        compiler_params=grant(16),
        cost_estimate=matmul_cost(pairs, rows, b),
    )(pair_in, pair_count, *pieces, right, *early)


def outer_kernel(first, chunk, cells, pieces, *refs):
    out_ref, count_ref, *refs = refs
    parts = refs[:pieces]
    left, cat, inv_ref, before_ref, send_ref, keep_ref, rho_ref, acc = refs[pieces:]
    _, rows, b = acc.shape
    shard = rows // 4
    core = lax.axis_index("sector") & 1
    acc[...] = jnp.zeros_like(acc)
    here = slice(chunk * rows, (chunk + 1) * rows)

    def one_pair(p, carry):
        target = out_ref[0, p]
        acc[target] += DOT(left[p, here, :], cat[p])
        return carry

    lax.fori_loop(0, count_ref[0], one_pair, 0)
    scale = inv_ref[:1, :]
    rho = jnp.zeros((1, b), F32)
    wide = shard * b // TILE[1]
    for piece, cuts in zip(parts, segments(first, rows, shard)):
        for at, sector, start, row, size in cuts:
            if at == chunk:
                x = acc[sector, pl.ds(row, size), :] * piece[start:start + size, :]
                rho += jnp.sum(x, axis=0, keepdims=True)
    for dest, parity in ((send_ref, 1 - core), (keep_ref, core)):
        for j in range(8):
            sector, row = slot_place(j, parity, shard)
            store_wide(dest, j * wide, acc[sector, pl.ds(row, shard), :] * scale)
    rho = jnp.broadcast_to(jnp.sum(rho * scale * scale, axis=1, keepdims=True), TILE) / cells + before_ref[...]
    rho_ref[...] = rho
    if chunk == CHUNKS - 1:
        send_ref[8 * wide:, :] = rho
        keep_ref[8 * wide:, :] = rho


def outer(first, chunk, cells, sectors, pair_out, pair_count, pieces, ops, inv, before):
    pairs, _, b = ops[1].shape
    rows = b // CHUNKS
    extra = TILE[0] if chunk == CHUNKS - 1 else 0
    half = jax.ShapeDtypeStruct((sectors * rows // 2 * b // TILE[1] + extra, TILE[1]), F32)
    return pl.pallas_call(
        functools.partial(outer_kernel, first, chunk, cells, len(pieces)),
        in_specs=[SMEM] * 2 + [VMEM] * (len(pieces) + 4),
        out_specs=[VMEM] * 3,
        out_shape=[half, half, jax.ShapeDtypeStruct(TILE, F32)],
        scratch_shapes=[pltpu.VMEM((sectors, rows, b), F32)],
        compiler_params=grant(20),
        cost_estimate=matmul_cost(pairs, rows, b),
    )(pair_out, pair_count, *pieces, *ops, inv, before)


def combine_kernel(keep_ref, recv_ref, next_ref, send_ref=None):
    extra = 0 if send_ref is None else 2 * next_ref.shape[0] - keep_ref.shape[0]
    rows = next_ref.shape[0] - extra
    next_ref[:rows, :] = keep_ref[:rows, :] + recv_ref[:rows, :]
    if send_ref is None:
        return
    send_ref[:rows, :] = keep_ref[rows:2 * rows, :] + recv_ref[rows:2 * rows, :]
    if extra:
        total = keep_ref[2 * rows:, :] + recv_ref[2 * rows:, :]
        next_ref[rows:, :] = total
        send_ref[rows:, :] = total


def combine(keep, recv, extra):
    shape = jax.ShapeDtypeStruct(((keep.shape[0] - extra) // 2 + extra, TILE[1]), F32)
    return pl.pallas_call(
        combine_kernel,
        in_specs=[VMEM] * 2,
        out_specs=[VMEM] * 2,
        out_shape=[shape] * 2,
        compiler_params=grant(4),
    )(keep, recv)


def total(mine, recv):
    return pl.pallas_call(
        combine_kernel,
        in_specs=[VMEM] * 2,
        out_specs=VMEM,
        out_shape=jax.ShapeDtypeStruct(mine.shape, F32),
        compiler_params=grant(4),
    )(mine, recv)


def update_kernel(*refs):
    sums, (vec_ref, inv_ref, diag_ref, new_ref, energy_ref) = refs[:2 * CHUNKS], refs[2 * CHUNKS:]
    rows, b = new_ref.shape
    shard = rows // CHUNKS
    end = shard * b // TILE[1]
    rho = sums[-2][end:, :] + sums[-1][end:, :]
    energy_ref[...] = rho
    for h in range(CHUNKS):
        mine_ref, recv_ref = sums[2 * h:2 * h + 2]
        at = slice(h * shard, (h + 1) * shard)
        for c in range(b // TILE[1]):
            part = slice(c * shard, (c + 1) * shard)
            lanes = slice(c * TILE[1], (c + 1) * TILE[1])
            normed = vec_ref[at, lanes] * inv_ref[:1, lanes]
            sigma = mine_ref[part, :] + recv_ref[part, :]
            residual = sigma - rho[:1, :] * normed
            gap = jnp.maximum(jnp.abs(diag_ref[at, lanes] - rho[:1, :]), 1.0)
            new_ref[at, lanes] = normed - residual / gap


def update(sums, vec, inv, diag):
    return pl.pallas_call(
        update_kernel,
        in_specs=[VMEM] * (len(sums) + 3),
        out_specs=[VMEM] * 2,
        out_shape=[jax.ShapeDtypeStruct(vec.shape, F32), jax.ShapeDtypeStruct(TILE, F32)],
        compiler_params=grant(4),
    )(*sums, vec, inv, diag)


def zero_tile(tile):
    def kernel(in_ref, out_ref):
        out_ref[...] = jnp.zeros_like(out_ref)

    return pl.pallas_call(
        kernel, in_specs=[VMEM], out_specs=VMEM, out_shape=jax.ShapeDtypeStruct(TILE, F32), compiler_params=grant(4)
    )(tile)


def join_kernel(*refs):
    *parts, out_ref = refs
    rows = parts[0].shape[0] // CHUNKS
    for k, part in enumerate(parts):
        _, row = piece_place(k, 0, rows)
        for h in range(CHUNKS):
            at = pl.ds(pl.multiple_of(row + h * 4 * rows, 8), rows)
            out_ref[0, at, :] = part[h * rows:(h + 1) * rows, :]


def join(parts):
    quarter, b = parts[0].shape
    return pl.pallas_call(
        join_kernel,
        in_specs=[VMEM] * len(parts),
        out_specs=VMEM,
        out_shape=jax.ShapeDtypeStruct((1, 4 * quarter, b), F32),
        compiler_params=grant(4),
    )(*parts)


def flips(mesh_shape, even, odd):
    terms, sectors = mesh_shape
    pairs = []
    for t in range(terms):
        for s in range(sectors):
            u = {"term": t, "sector": s}
            for axis, bit in odd if s & 1 else even:
                u[axis] ^= 1 << bit
            pairs.append((t * sectors + s, u["term"] * sectors + u["sector"]))
    return pairs


def rest_dims(terms):
    return [("term", bit) for bit in range(2, terms.bit_length() - 1)]


def shards(mesh_shape, psi_start, diagonal, left_ops, right_ops, pair_in, pair_out, pair_count):
    terms, sectors = mesh_shape
    b = psi_start.shape[1]
    cells = float(sectors * b * b)

    def swap(x, even, odd=None):
        return lax.ppermute(x, AXES, flips(mesh_shape, even, even if odd is None else odd))

    def dims_of(k):
        return [dim for i, dim in enumerate(DIMS) if (k >> (2 - i)) & 1]

    away = (2, 1, 4, 5, 6, 3, 7)
    rest = rest_dims(terms)

    own = psi_start[0]
    rows = b // CHUNKS
    far = []
    for h in range(CHUNKS):
        far.append(swap(own[h * rows:(h + 1) * rows], [DIMS[0]]))
    beside = swap(own, [CORE])
    left, right, vec, diag = prepare(left_ops, right_ops, psi_start, diagonal)
    far[0], left, right, vec, diag = lax.optimization_barrier((far[0], left, right, vec, diag))
    pieces = [own, beside]
    for x in far:
        pieces += [x, swap(x, [CORE])]
    zero = jnp.zeros(TILE, F32)
    energies = []
    for sweep in range(ITERS):
        first = sweep == 0
        early, late = ([pieces[i] for i in picked(first, half)] for half in range(2))
        early = inner(first, 0, cells, sectors, pair_in, pair_count, early, right)
        cat, inv = inner(first, 1, cells, sectors, pair_in, pair_count, late, right, early)
        rho = zero
        keeps, recvs = [], []
        for h in range(CHUNKS):
            send, keep, rho = outer(
                first, h, cells, sectors, pair_out, pair_count, pieces, (left, cat), inv, rho
            )
            keeps.append(keep)
            recvs.append(swap(send, [CORE]))
        for step in zip(*ORDERS):
            for h in range(CHUNKS):
                extra = TILE[0] if h == CHUNKS - 1 else 0
                keeps[h], send = combine(keeps[h], recvs[h], extra)
                recvs[h] = swap(send, [DIMS[step[0]]], [DIMS[step[1]]])
        for step in rest:
            for h in range(CHUNKS):
                keeps[h] = total(keeps[h], recvs[h])
                recvs[h] = swap(keeps[h], [step])
        sums = [x for pair in zip(keeps, recvs) for x in pair]
        vec, energy = update(sums, vec, inv, diag)
        energies.append(energy[0, 0])
        if sweep < ITERS - 1:
            got = {0: vec}
            zero = zero_tile(energy)
            for k in away:
                got[k] = swap(vec, dims_of(k))
            pieces = []
            for k in range(8):
                pieces += [got[k], swap(got[k], [CORE])]
    got = {k: swap(vec, dims_of(k)) for k in (3, 2, 1)}
    block = join([vec, got[1], got[2], got[3]])
    return block, jnp.stack(energies)


def solution(mesh):
    mesh_shape = (mesh.shape["term"], mesh.shape["sector"])
    return jax.shard_map(
        functools.partial(shards, mesh_shape),
        mesh=mesh,
        in_specs=(
            P("sector", None, None),
            P("sector", None, None),
            P(("term", "sector"), None, None),
            P(("term", "sector"), None, None),
            P(("term", "sector"), None),
            P(("term", "sector"), None),
            P(("term", "sector")),
        ),
        out_specs=(P("sector", None, None), P()),
        check_vma=False,
    )
```

profile of v0, /device:TPU:0, one launch (start us, length us, event | category | flops | bytes accessed | tf_op | source)
XLA Modules:
  0.0 127.7 jit_solution(10421651509836268824)
XLA Ops:
  1.8 3.1 %collective-permute-start.1 = (f32[192,384]{1,0:T(8,128)S(1)}, f32[192,384]{1,0:T(8,128)S(1)}, u32[]{:S(2)}, u32[]{:S(2)}) collective-permute-start(f32[192,384]{1,0:T(8,128)S(1)} %get-tuple-element.117), channel_id=1, source_target_pairs={{0,2},{1,3},{2,0},{3,1},{4,6},{5,7},{6,4},{7,5},{8,10},{9,11},{10,... | collective-permute-start | bytes 884744 | tf_op jit(solution)/shard_map/ppermute | solution.py:374
  12.7 5.5 %collective-permute-done.3.refs_4_.refs_6_ = f32[192,384]{1,0:T(8,128)S(1)} collective-permute-done((f32[192,384]{1,0:T(8,128)S(1)}, f32[192,384]{1,0:T(8,128)S(1)}, u32[]{:S(2)}, u32[]{:S(2)}) %collective-permute-start.3) | collective-permute-done | bytes 294944 | tf_op jit(solution)/shard_map/ppermute | solution.py:374
  18.9 2.9 %shard_map.87 = (bf16[4,192,384]{2,1,0:T(8,128)(2,1)S(1)}, bf16[4,192,384]{2,1,0:T(8,128)(2,1)S(1)}, f32[8,384]{1,0:T(8,128)S(1)}) custom-call(s32[1,4]{1,0:T(1,128)S(1)} %copy-done.5, s32[1]{0:T(128)S(6)} %copy.9.refs_1_, f32[384,384]{1,0:T(8,128)S(1)} %bitcast.8, f32[384,384]{1,0:T(8,128)S(1)} %collective-permute-done.refs_3_, ...), custom_call_target="tpu_custom_call" | custom-call | flops 679477248 | bytes 4718592 | tf_op jit(solution)/shard_map/pallas_call | solution.py:196
  21.8 3.0 %shard_map.88 = (bf16[4,1152,384]{2,1,0:T(8,128)(2,1)S(1)}, f32[8,384]{1,0:T(8,128)S(1)}) custom-call(s32[1,4]{1,0:T(1,128)S(1)} %copy-done.5, s32[1]{0:T(128)S(6)} %copy.9.refs_1_, f32[384,384]{1,0:T(8,128)S(1)} %bitcast.9, f32[384,384]{1,0:T(8,128)S(1)} %collective-permute-done.refs_3_, f32[192,384]{1,0:T(8,128)S(1)} %collective-permute-done.3.refs_4_.refs_6_, ...), custom_call_target="tpu_custom_call" | custom-call | flops 679477248 | bytes 4718592 | tf_op jit(solution)/shard_map/pallas_call | solution.py:196
  24.8 2.5 %shard_map.89 = (f32[1152,128]{1,0:T(8,128)S(1)}, f32[1152,128]{1,0:T(8,128)S(1)}, f32[8,128]{1,0:T(8,128)S(1)}) custom-call(s32[1,4]{1,0:T(1,128)S(1)} %copy-done.6, s32[1]{0:T(128)S(6)} %copy.9.refs_1_, f32[384,384]{1,0:T(8,128)S(1)} %bitcast.10, f32[384,384]{1,0:T(8,128)S(1)} %collective-permute-done.refs_3_, ...), custom_call_target="tpu_custom_call" | custom-call | flops 679477248 | bytes 4718592 | tf_op jit(solution)/shard_map/pallas_call | solution.py:247
  27.3 3.1 %shard_map.94 = (f32[1160,128]{1,0:T(8,128)S(1)}, f32[1160,128]{1,0:T(8,128)S(1)}, f32[8,128]{1,0:T(8,128)}) custom-call(s32[1,4]{1,0:T(1,128)S(1)} %copy-done.6, s32[1]{0:T(128)S(6)} %copy.9.refs_1_, f32[384,384]{1,0:T(8,128)S(1)} %bitcast.11, f32[384,384]{1,0:T(8,128)S(1)} %collective-permute-done.refs_3_, f32[192,384]{1,0:T(8,128)S(1)} %collective-permute-done.1.refs_4_, ...), custom_call_target="tpu_custom_call" | custom-call | flops 679477248 | bytes 4718592 | tf_op jit(solution)/shard_map/pallas_call | solution.py:247
  34.7 4.6 %collective-permute-done.11.recv_ref = f32[584,128]{1,0:T(8,128)S(1)} collective-permute-done((f32[584,128]{1,0:T(8,128)S(1)}, f32[584,128]{1,0:T(8,128)S(1)}, u32[]{:S(2)}, u32[]{:S(2)}) %collective-permute-start.11) | collective-permute-done | bytes 299040 | tf_op jit(solution)/shard_map/ppermute | solution.py:374
  39.4 3.0 %collective-permute-done.6.recv_ref = f32[576,128]{1,0:T(8,128)S(1)} collective-permute-done((f32[576,128]{1,0:T(8,128)S(1)}, f32[576,128]{1,0:T(8,128)S(1)}, u32[]{:S(2)}, u32[]{:S(2)}) %collective-permute-start.6) | collective-permute-done | bytes 294944 | tf_op jit(solution)/shard_map/ppermute | solution.py:374
  42.6 2.5 %collective-permute-done.12.recv_ref = f32[296,128]{1,0:T(8,128)S(1)} collective-permute-done((f32[296,128]{1,0:T(8,128)S(1)}, f32[296,128]{1,0:T(8,128)S(1)}, u32[]{:S(2)}, u32[]{:S(2)}) %collective-permute-start.12) | collective-permute-done | bytes 151584 | tf_op jit(solution)/shard_map/ppermute | solution.py:374
  50.0 2.4 %collective-permute-start.14 = (f32[152,128]{1,0:T(8,128)S(1)}, f32[152,128]{1,0:T(8,128)S(1)}, u32[]{:S(2)}, u32[]{:S(2)}) collective-permute-start(f32[152,128]{1,0:T(8,128)S(1)} %shard_map.98.refs_2_), channel_id=1, source_target_pairs={{0,16},{1,17},{2,18},{3,19},{4,20},{5,21},{6,22},{7,23},{8,24},{9,... | collective-permute-start | bytes 233480 | tf_op jit(solution)/shard_map/ppermute | solution.py:374
  52.6 2.4 %collective-permute-start.9 = (f32[144,128]{1,0:T(8,128)S(1)}, f32[144,128]{1,0:T(8,128)S(1)}, u32[]{:S(2)}, u32[]{:S(2)}) collective-permute-start(f32[144,128]{1,0:T(8,128)S(1)} %shard_map.93.refs_0_), channel_id=1, source_target_pairs={{0,16},{1,17},{2,18},{3,19},{4,20},{5,21},{6,22},{7,23},{8,24},{9,... | collective-permute-start | bytes 221192 | tf_op jit(solution)/shard_map/ppermute | solution.py:374
  55.0 3.4 %collective-permute-done.9.refs_1_ = f32[144,128]{1,0:T(8,128)S(1)} collective-permute-done((f32[144,128]{1,0:T(8,128)S(1)}, f32[144,128]{1,0:T(8,128)S(1)}, u32[]{:S(2)}, u32[]{:S(2)}) %collective-permute-start.9) | collective-permute-done | bytes 73760 | tf_op jit(solution)/shard_map/ppermute | solution.py:374
  65.5 2.3 %collective-permute-start.26 = (f32[96,384]{1,0:T(8,128)S(1)}, f32[96,384]{1,0:T(8,128)S(1)}, u32[]{:S(2)}, u32[]{:S(2)}) collective-permute-start(f32[96,384]{1,0:T(8,128)S(1)} %get-tuple-element.90.refs_2_.refs_4_), channel_id=1, source_target_pairs={{0,6},{1,7},{2,4},{3,5},{4,2},{5,3},{6,0},{7,1},{8,14},{9,15},{10,... | collective-permute-start | bytes 442376 | tf_op jit(solution)/shard_map/ppermute | solution.py:374
  67.8 2.2 %collective-permute-done.18.refs_2_.refs_6_ = f32[96,384]{1,0:T(8,128)S(1)} collective-permute-done((f32[96,384]{1,0:T(8,128)S(1)}, f32[96,384]{1,0:T(8,128)S(1)}, u32[]{:S(2)}, u32[]{:S(2)}) %collective-permute-start.18) | collective-permute-done | bytes 147488 | tf_op jit(solution)/shard_map/ppermute | solution.py:374
  74.1 4.1 %collective-permute-done.26.refs_6_.refs_14_ = f32[96,384]{1,0:T(8,128)S(1)} collective-permute-done((f32[96,384]{1,0:T(8,128)S(1)}, f32[96,384]{1,0:T(8,128)S(1)}, u32[]{:S(2)}, u32[]{:S(2)}) %collective-permute-start.26) | collective-permute-done | bytes 147488 | tf_op jit(solution)/shard_map/ppermute | solution.py:374
  79.2 2.7 %shard_map.100 = (bf16[4,192,384]{2,1,0:T(8,128)(2,1)S(1)}, bf16[4,192,384]{2,1,0:T(8,128)(2,1)S(1)}, f32[8,384]{1,0:T(8,128)S(1)}) custom-call(s32[1,4]{1,0:T(1,128)S(1)} %copy-done.5, s32[1]{0:T(128)S(6)} %copy.9.refs_1_, f32[96,384]{1,0:T(8,128)S(1)} %get-tuple-element.90.refs_2_.refs_4_, f32[96,384]{1,0:T(8,128)S(1)} %collective-permute-done.15.refs_3_, ...), custom_call_target="tpu_custom_call" | custom-call | flops 679477248 | bytes 4718592 | tf_op jit(solution)/shard_map/pallas_call | solution.py:196
  82.0 2.9 %shard_map.101 = (bf16[4,1152,384]{2,1,0:T(8,128)(2,1)S(1)}, f32[8,384]{1,0:T(8,128)S(1)}) custom-call(s32[1,4]{1,0:T(1,128)S(1)} %copy-done.5, s32[1]{0:T(128)S(6)} %copy.9.refs_1_, f32[96,384]{1,0:T(8,128)S(1)} %collective-permute-done.18.refs_2_.refs_6_, f32[96,384]{1,0:T(8,128)S(1)} %collective-permute-done.19.refs_3_.refs_7_, ...), custom_call_target="tpu_custom_call" | custom-call | flops 679477248 | bytes 4718592 | tf_op jit(solution)/shard_map/pallas_call | solution.py:196
  84.9 2.5 %shard_map.103 = (f32[1152,128]{1,0:T(8,128)S(1)}, f32[1152,128]{1,0:T(8,128)S(1)}, f32[8,128]{1,0:T(8,128)S(1)}) custom-call(s32[1,4]{1,0:T(1,128)S(1)} %copy-done.6, s32[1]{0:T(128)S(6)} %copy.9.refs_1_, f32[96,384]{1,0:T(8,128)S(1)} %get-tuple-element.90.refs_2_.refs_4_, f32[96,384]{1,0:T(8,128)S(1)} %collective-permute-done.15.refs_3_, ...), custom_call_target="tpu_custom_call" | custom-call | flops 679477248 | bytes 4718592 | tf_op jit(solution)/shard_map/pallas_call | solution.py:247
  87.4 3.1 %shard_map.108 = (f32[1160,128]{1,0:T(8,128)S(1)}, f32[1160,128]{1,0:T(8,128)S(1)}, f32[8,128]{1,0:T(8,128)}) custom-call(s32[1,4]{1,0:T(1,128)S(1)} %copy-done.6, s32[1]{0:T(128)S(6)} %copy.9.refs_1_, f32[96,384]{1,0:T(8,128)S(1)} %get-tuple-element.90.refs_2_.refs_4_, f32[96,384]{1,0:T(8,128)S(1)} %collective-permute-done.15.refs_3_, ...), custom_call_target="tpu_custom_call" | custom-call | flops 679477248 | bytes 4718592 | tf_op jit(solution)/shard_map/pallas_call | solution.py:247
  94.9 4.6 %collective-permute-done.36.recv_ref = f32[584,128]{1,0:T(8,128)S(1)} collective-permute-done((f32[584,128]{1,0:T(8,128)S(1)}, f32[584,128]{1,0:T(8,128)S(1)}, u32[]{:S(2)}, u32[]{:S(2)}) %collective-permute-start.36) | collective-permute-done | bytes 299040 | tf_op jit(solution)/shard_map/ppermute | solution.py:374
  99.6 3.0 %collective-permute-done.31.recv_ref = f32[576,128]{1,0:T(8,128)S(1)} collective-permute-done((f32[576,128]{1,0:T(8,128)S(1)}, f32[576,128]{1,0:T(8,128)S(1)}, u32[]{:S(2)}, u32[]{:S(2)}) %collective-permute-start.31) | collective-permute-done | bytes 294944 | tf_op jit(solution)/shard_map/ppermute | solution.py:374
  102.7 2.2 %collective-permute-done.37.recv_ref = f32[296,128]{1,0:T(8,128)S(1)} collective-permute-done((f32[296,128]{1,0:T(8,128)S(1)}, f32[296,128]{1,0:T(8,128)S(1)}, u32[]{:S(2)}, u32[]{:S(2)}) %collective-permute-start.37) | collective-permute-done | bytes 151584 | tf_op jit(solution)/shard_map/ppermute | solution.py:374
  109.4 2.3 %collective-permute-start.39 = (f32[152,128]{1,0:T(8,128)S(1)}, f32[152,128]{1,0:T(8,128)S(1)}, u32[]{:S(2)}, u32[]{:S(2)}) collective-permute-start(f32[152,128]{1,0:T(8,128)S(1)} %shard_map.112.refs_2_), channel_id=1, source_target_pairs={{0,16},{1,17},{2,18},{3,19},{4,20},{5,21},{6,22},{7,23},{8,24},{9,... | collective-permute-start | bytes 233480 | tf_op jit(solution)/shard_map/ppermute | solution.py:374
  114.3 3.7 %collective-permute-done.34.refs_1_ = f32[144,128]{1,0:T(8,128)S(1)} collective-permute-done((f32[144,128]{1,0:T(8,128)S(1)}, f32[144,128]{1,0:T(8,128)S(1)}, u32[]{:S(2)}, u32[]{:S(2)}) %collective-permute-start.34) | collective-permute-done | bytes 73760 | tf_op jit(solution)/shard_map/ppermute | solution.py:374
  (110 shorter events, 52.1 us)
Async XLA Ops:
  1.8 10.9 %collective-permute-start.1 = (f32[192,384]{1,0:T(8,128)S(1)}, f32[192,384]{1,0:T(8,128)S(1)}, u32[]{:S(2)}, u32[]{:S(2)}) collective-permute-start(f32[192,384]{1,0:T(8,128)S(1)} %get-tuple-element.117), channel_id=1, source_target_pairs={{0,2},{1,3},{2,0},{3,1},{4,6},{5,7},{6,4},{7,5},{8,10},{9,11},{10,... | collective-permute-start | bytes 884744 | tf_op jit(solution)/shard_map/ppermute | solution.py:374
  4.9 14.0 %collective-permute-start = (f32[384,384]{1,0:T(8,128)}, f32[384,384]{1,0:T(8,128)S(1)}, u32[]{:S(2)}, u32[]{:S(2)}) collective-permute-start(f32[384,384]{1,0:T(8,128)} %bitcast.7), channel_id=1, source_target_pairs={{0,1},{1,0},{2,3},{3,2},{4,5},{5,4},{6,7},{7,6},{8,9},{9,8},{10,11... | collective-permute-start | bytes 1769480 | tf_op jit(solution)/shard_map/ppermute | solution.py:374
  4.9 13.3 %collective-permute-start.3 = (f32[192,384]{1,0:T(8,128)S(1)}, f32[192,384]{1,0:T(8,128)S(1)}, u32[]{:S(2)}, u32[]{:S(2)}) collective-permute-start(f32[192,384]{1,0:T(8,128)S(1)} %get-tuple-element.116), channel_id=1, source_target_pairs={{0,2},{1,3},{2,0},{3,1},{4,6},{5,7},{6,4},{7,5},{8,10},{9,11},{10,... | collective-permute-start | bytes 884744 | tf_op jit(solution)/shard_map/ppermute | solution.py:374
  12.7 6.1 %collective-permute-start.2 = (f32[192,384]{1,0:T(8,128)S(1)}, f32[192,384]{1,0:T(8,128)S(1)}, u32[]{:S(2)}, u32[]{:S(2)}) collective-permute-start(f32[192,384]{1,0:T(8,128)S(1)} %collective-permute-done.1.refs_4_), channel_id=1, source_target_pairs={{0,1},{1,0},{2,3},{3,2},{4,5},{5,4},{6,7},{7,6},{8,9},{9,8},{10,11... | collective-permute-start | bytes 884744 | tf_op jit(solution)/shard_map/ppermute | solution.py:374
  32.5 6.8 %collective-permute-start.11 = (f32[584,128]{1,0:T(8,128)S(1)}, f32[584,128]{1,0:T(8,128)S(1)}, u32[]{:S(2)}, u32[]{:S(2)}) collective-permute-start(f32[584,128]{1,0:T(8,128)S(1)} %get-tuple-element.83), channel_id=1, source_target_pairs={{0,2},{1,9},{2,0},{3,11},{4,6},{5,13},{6,4},{7,15},{8,10},{9,1},{1... | collective-permute-start | bytes 897032 | tf_op jit(solution)/shard_map/ppermute | solution.py:374
  33.3 9.2 %collective-permute-start.6 = (f32[576,128]{1,0:T(8,128)S(1)}, f32[576,128]{1,0:T(8,128)S(1)}, u32[]{:S(2)}, u32[]{:S(2)}) collective-permute-start(f32[576,128]{1,0:T(8,128)S(1)} %get-tuple-element.74), channel_id=1, source_target_pairs={{0,2},{1,9},{2,0},{3,11},{4,6},{5,13},{6,4},{7,15},{8,10},{9,1},{1... | collective-permute-start | bytes 884744 | tf_op jit(solution)/shard_map/ppermute | solution.py:374
  39.3 5.7 %collective-permute-start.12 = (f32[296,128]{1,0:T(8,128)S(1)}, f32[296,128]{1,0:T(8,128)S(1)}, u32[]{:S(2)}, u32[]{:S(2)}) collective-permute-start(f32[296,128]{1,0:T(8,128)S(1)} %get-tuple-element.85), channel_id=1, source_target_pairs={{0,4},{1,5},{2,6},{3,7},{4,0},{5,1},{6,2},{7,3},{8,12},{9,13},{10,... | collective-permute-start | bytes 454664 | tf_op jit(solution)/shard_map/ppermute | solution.py:374
  50.0 8.4 %collective-permute-start.14 = (f32[152,128]{1,0:T(8,128)S(1)}, f32[152,128]{1,0:T(8,128)S(1)}, u32[]{:S(2)}, u32[]{:S(2)}) collective-permute-start(f32[152,128]{1,0:T(8,128)S(1)} %shard_map.98.refs_2_), channel_id=1, source_target_pairs={{0,16},{1,17},{2,18},{3,19},{4,20},{5,21},{6,22},{7,23},{8,24},{9,... | collective-permute-start | bytes 233480 | tf_op jit(solution)/shard_map/ppermute | solution.py:374
  52.6 5.8 %collective-permute-start.9 = (f32[144,128]{1,0:T(8,128)S(1)}, f32[144,128]{1,0:T(8,128)S(1)}, u32[]{:S(2)}, u32[]{:S(2)}) collective-permute-start(f32[144,128]{1,0:T(8,128)S(1)} %shard_map.93.refs_0_), channel_id=1, source_target_pairs={{0,16},{1,17},{2,18},{3,19},{4,20},{5,21},{6,22},{7,23},{8,24},{9,... | collective-permute-start | bytes 221192 | tf_op jit(solution)/shard_map/ppermute | solution.py:374
  58.6 6.9 %collective-permute-start.16 = (f32[96,384]{1,0:T(8,128)S(1)}, f32[96,384]{1,0:T(8,128)S(1)}, u32[]{:S(2)}, u32[]{:S(2)}) collective-permute-start(f32[96,384]{1,0:T(8,128)S(1)} %get-tuple-element.90.refs_2_.refs_4_), channel_id=1, source_target_pairs={{0,8},{1,9},{2,10},{3,11},{4,12},{5,13},{6,14},{7,15},{8,0},{9,1},... | collective-permute-start | bytes 442376 | tf_op jit(solution)/shard_map/ppermute | solution.py:374
  60.5 9.5 %collective-permute-start.18 = (f32[96,384]{1,0:T(8,128)S(1)}, f32[96,384]{1,0:T(8,128)S(1)}, u32[]{:S(2)}, u32[]{:S(2)}) collective-permute-start(f32[96,384]{1,0:T(8,128)S(1)} %get-tuple-element.90.refs_2_.refs_4_), channel_id=1, source_target_pairs={{0,4},{1,5},{2,6},{3,7},{4,0},{5,1},{6,2},{7,3},{8,12},{9,13},{10,... | collective-permute-start | bytes 442376 | tf_op jit(solution)/shard_map/ppermute | solution.py:374
  61.8 10.4 %collective-permute-start.20 = (f32[96,384]{1,0:T(8,128)S(1)}, f32[96,384]{1,0:T(8,128)S(1)}, u32[]{:S(2)}, u32[]{:S(2)}) collective-permute-start(f32[96,384]{1,0:T(8,128)S(1)} %get-tuple-element.90.refs_2_.refs_4_), channel_id=1, source_target_pairs={{0,12},{1,13},{2,14},{3,15},{4,8},{5,9},{6,10},{7,11},{8,4},{9,5},... | collective-permute-start | bytes 442376 | tf_op jit(solution)/shard_map/ppermute | solution.py:374
  62.1 10.0 %collective-permute-start.22 = (f32[96,384]{1,0:T(8,128)S(1)}, f32[96,384]{1,0:T(8,128)S(1)}, u32[]{:S(2)}, u32[]{:S(2)}) collective-permute-start(f32[96,384]{1,0:T(8,128)S(1)} %get-tuple-element.90.refs_2_.refs_4_), channel_id=1, source_target_pairs={{0,2},{1,3},{2,0},{3,1},{4,6},{5,7},{6,4},{7,5},{8,10},{9,11},{10,... | collective-permute-start | bytes 442376 | tf_op jit(solution)/shard_map/ppermute | solution.py:374
  63.5 10.6 %collective-permute-start.24 = (f32[96,384]{1,0:T(8,128)S(1)}, f32[96,384]{1,0:T(8,128)S(1)}, u32[]{:S(2)}, u32[]{:S(2)}) collective-permute-start(f32[96,384]{1,0:T(8,128)S(1)} %get-tuple-element.90.refs_2_.refs_4_), channel_id=1, source_target_pairs={{0,10},{1,11},{2,8},{3,9},{4,14},{5,15},{6,12},{7,13},{8,2},{9,3},... | collective-permute-start | bytes 442376 | tf_op jit(solution)/shard_map/ppermute | solution.py:374
  65.5 12.7 %collective-permute-start.26 = (f32[96,384]{1,0:T(8,128)S(1)}, f32[96,384]{1,0:T(8,128)S(1)}, u32[]{:S(2)}, u32[]{:S(2)}) collective-permute-start(f32[96,384]{1,0:T(8,128)S(1)} %get-tuple-element.90.refs_2_.refs_4_), channel_id=1, source_target_pairs={{0,6},{1,7},{2,4},{3,5},{4,2},{5,3},{6,0},{7,1},{8,14},{9,15},{10,... | collective-permute-start | bytes 442376 | tf_op jit(solution)/shard_map/ppermute | solution.py:374
  70.1 8.1 %collective-permute-start.28 = (f32[96,384]{1,0:T(8,128)S(1)}, f32[96,384]{1,0:T(8,128)S(1)}, u32[]{:S(2)}, u32[]{:S(2)}) collective-permute-start(f32[96,384]{1,0:T(8,128)S(1)} %get-tuple-element.90.refs_2_.refs_4_), channel_id=1, source_target_pairs={{0,14},{1,15},{2,12},{3,13},{4,10},{5,11},{6,8},{7,9},{8,6},{9,7},... | collective-permute-start | bytes 442376 | tf_op jit(solution)/shard_map/ppermute | solution.py:374
  72.1 6.5 %collective-permute-start.17 = (f32[96,384]{1,0:T(8,128)S(1)}, f32[96,384]{1,0:T(8,128)S(1)}, u32[]{:S(2)}, u32[]{:S(2)}) collective-permute-start(f32[96,384]{1,0:T(8,128)S(1)} %collective-permute-done.16.refs_4_), channel_id=1, source_target_pairs={{0,1},{1,0},{2,3},{3,2},{4,5},{5,4},{6,7},{7,6},{8,9},{9,8},{10,11... | collective-permute-start | bytes 442376 | tf_op jit(solution)/shard_map/ppermute | solution.py:374
  72.2 6.6 %collective-permute-start.23 = (f32[96,384]{1,0:T(8,128)S(1)}, f32[96,384]{1,0:T(8,128)S(1)}, u32[]{:S(2)}, u32[]{:S(2)}) collective-permute-start(f32[96,384]{1,0:T(8,128)S(1)} %collective-permute-done.22.refs_6_.refs_10_), channel_id=1, source_target_pairs={{0,1},{1,0},{2,3},{3,2},{4,5},{5,4},{6,7},{7,6},{8,9},{9,8},{10,11... | collective-permute-start | bytes 442376 | tf_op jit(solution)/shard_map/ppermute | solution.py:374
  92.6 6.8 %collective-permute-start.36 = (f32[584,128]{1,0:T(8,128)S(1)}, f32[584,128]{1,0:T(8,128)S(1)}, u32[]{:S(2)}, u32[]{:S(2)}) collective-permute-start(f32[584,128]{1,0:T(8,128)S(1)} %get-tuple-element.109), channel_id=1, source_target_pairs={{0,2},{1,9},{2,0},{3,11},{4,6},{5,13},{6,4},{7,15},{8,10},{9,1},{1... | collective-permute-start | bytes 897032 | tf_op jit(solution)/shard_map/ppermute | solution.py:374
  93.5 9.2 %collective-permute-start.31 = (f32[576,128]{1,0:T(8,128)S(1)}, f32[576,128]{1,0:T(8,128)S(1)}, u32[]{:S(2)}, u32[]{:S(2)}) collective-permute-start(f32[576,128]{1,0:T(8,128)S(1)} %get-tuple-element.100), channel_id=1, source_target_pairs={{0,2},{1,9},{2,0},{3,11},{4,6},{5,13},{6,4},{7,15},{8,10},{9,1},{1... | collective-permute-start | bytes 884744 | tf_op jit(solution)/shard_map/ppermute | solution.py:374
  109.4 8.6 %collective-permute-start.39 = (f32[152,128]{1,0:T(8,128)S(1)}, f32[152,128]{1,0:T(8,128)S(1)}, u32[]{:S(2)}, u32[]{:S(2)}) collective-permute-start(f32[152,128]{1,0:T(8,128)S(1)} %shard_map.112.refs_2_), channel_id=1, source_target_pairs={{0,16},{1,17},{2,18},{3,19},{4,20},{5,21},{6,22},{7,23},{8,24},{9,... | collective-permute-start | bytes 233480 | tf_op jit(solution)/shard_map/ppermute | solution.py:374
  118.1 6.4 %collective-permute-start.40 = (f32[96,384]{1,0:T(8,128)S(1)}, f32[96,384]{1,0:T(8,128)S(1)}, u32[]{:S(2)}, u32[]{:S(2)}) collective-permute-start(f32[96,384]{1,0:T(8,128)S(1)} %get-tuple-element.114.refs_0_), channel_id=1, source_target_pairs={{0,8},{1,9},{2,10},{3,11},{4,12},{5,13},{6,14},{7,15},{8,0},{9,1},... | collective-permute-start | bytes 442376 | tf_op jit(solution)/shard_map/ppermute | solution.py:374
  119.5 5.8 %collective-permute-start.41 = (f32[96,384]{1,0:T(8,128)S(1)}, f32[96,384]{1,0:T(8,128)S(1)}, u32[]{:S(2)}, u32[]{:S(2)}) collective-permute-start(f32[96,384]{1,0:T(8,128)S(1)} %get-tuple-element.114.refs_0_), channel_id=1, source_target_pairs={{0,4},{1,5},{2,6},{3,7},{4,0},{5,1},{6,2},{7,3},{8,12},{9,13},{10,... | collective-permute-start | bytes 442376 | tf_op jit(solution)/shard_map/ppermute | solution.py:374
  120.5 6.3 %collective-permute-start.42 = (f32[96,384]{1,0:T(8,128)S(1)}, f32[96,384]{1,0:T(8,128)S(1)}, u32[]{:S(2)}, u32[]{:S(2)}) collective-permute-start(f32[96,384]{1,0:T(8,128)S(1)} %get-tuple-element.114.refs_0_), channel_id=1, source_target_pairs={{0,12},{1,13},{2,14},{3,15},{4,8},{5,9},{6,10},{7,11},{8,4},{9,5},... | collective-permute-start | bytes 442376 | tf_op jit(solution)/shard_map/ppermute | solution.py:374
  (26 other events, 122.6 us)
where the time goes:
time: 128 us
  waiting for transfers between devices  52.7 us (41%)
  starting transfers between devices  38.7 us (30%)
  Pallas kernels  25.3 us (20%)
  local copies, waits for them, and re-layouts  7.68 us (6%)
  other arithmetic  1.83 us (1%)
  between operations  1.58 us (1%)
    ppermute x43, waiting for transfers between devices, swap(): lax.ppermute(x, AXES, flips(mesh_shape, even, even if odd is None else odd))  52.7 us
    ppermute x43, starting transfers between devices, swap(): lax.ppermute(x, AXES, flips(mesh_shape, even, even if odd is None else odd))  38.7 us
    pallas_call x4, Pallas kernels, inner(): pl.pallas_call(functools.partial(inner_kernel, first, half, cells, len(pi...  11.5 us
    pallas_call x4, Pallas kernels, outer(): pl.pallas_call(functools.partial(outer_kernel, first, chunk, cells, len(p...  11.2 us
    unnamed x14, local copies, waits for them, and re-layouts  5.47 us
  transfers between devices with their start and end apart: 43, of which 24 were waited for; matrix products, arithmetic and copies ran while one was open for 2% of the time, Pallas kernels for 6%

commit v1 on v0

--- a/solution.py
+++ b/solution.py
@@ -131,68 +131,61 @@
     in_ref, count_ref, *refs = refs
     parts = refs[:pieces]
     refs = refs[pieces:]
-    if half:
+    if half == 0:
+        right, early_h, early_l, squares_ref, vec = refs
+    elif half == 1:
         right, early_h, early_l, squares_ref, cat_ref, inv_ref, vec = refs
     else:
-        right, early_h, early_l, squares_ref, vec = refs
-    _, rows, _ = vec.shape
+        right, cat_ref, inv_ref, vec = refs
     b = right.shape[1]
+    rows = b // CHUNKS
     shard = rows // 4
-    x_bit = bit_of(*DIMS[1])
-    side = x_bit ^ half
     total = jnp.zeros((1, b), F32)
     cuts_of = segments(first, rows, shard)
-    for piece, cuts in zip(parts, [cuts_of[i] for i in picked(first, half)]):
+    for piece, cuts in zip(parts, [cuts_of[i] for i in picked(half, len(cuts_of))]):
         for chunk, sector, start, row, size in cuts:
-            if first and chunk != half:
+            if half is not None and chunk != half:
                 continue
             x = piece[start:start + size, :]
             high, low = split(x)
             total += jnp.sum(x * x, axis=0, keepdims=True)
-            if not first:
-                row = pl.multiple_of(row - side * 2 * shard + chunk * 2 * shard, 16)
+            if half is None:
+                row = pl.multiple_of(row + chunk * rows, 16)
             at = pl.ds(row, size)
             for place, y in enumerate((high, low, high)):
                 vec[sector, at, place * b:(place + 1) * b] = y
     total = jnp.broadcast_to(jnp.sum(total, axis=1, keepdims=True), (TILE[0], b))
-    if half:
-        inv_ref[...] = lax.rsqrt((total + squares_ref[...]) / cells + epsilon)
+    if half == 0:
+        squares_ref[...] = total
     else:
-        squares_ref[...] = total
+        if half == 1:
+            total += squares_ref[...]
+        inv_ref[...] = lax.rsqrt(total / cells + epsilon)
 
     def one_pair(p, carry):
         high, low = split(DOT_NT(vec[in_ref[0, p]], right[p]))
-        if not half:
+        if half == 0:
             early_h[p], early_l[p] = high, low
             return carry
-        for which, (h, l) in enumerate(((early_h[p], early_l[p]), (high, low))):
-            if first:
-                moves = [(0, rows, which * rows)]
-            else:
-                moves = [
-                    (c * 2 * shard, 2 * shard, pl.multiple_of(c * rows + (x_bit ^ which) * 2 * shard, 16))
-                    for c in range(CHUNKS)
-                ]
-            for start, size, row in moves:
-                for place, y in enumerate((h, h, l)):
-                    cat_ref[p, pl.ds(place * b + row, size), :] = y[start:start + size, :]
+        moves = [(high, low, 0)] if half is None else [(early_h[p], early_l[p], 0), (high, low, rows)]
+        for h, l, row in moves:
+            for place, y in enumerate((h, h, l)):
+                cat_ref[p, place * b + row:place * b + row + h.shape[0], :] = y
         return carry
 
     lax.fori_loop(0, count_ref[0], one_pair, 0)
 
 
-def picked(first, half):
-    if first:
-        return [0, 1, 2 + 2 * half, 3 + 2 * half]
-    return [number for number in range(16) if (number >> 2) & 1 == half]
+def picked(half, pieces):
+    return list(range(pieces)) if half is None else [0, 1, 2 + 2 * half, 3 + 2 * half]
 
 
 def inner(first, half, cells, sectors, pair_in, pair_count, pieces, right, early=()):
     pairs, b, _ = right.shape
-    rows = b // 2
+    rows = b if half is None else b // CHUNKS
     compact = jax.ShapeDtypeStruct((pairs, rows, b), BF16)
     row = jax.ShapeDtypeStruct((TILE[0], b), F32)
-    shapes = [jax.ShapeDtypeStruct((pairs, 3 * b, b), BF16), row] if half else [compact, compact, row]
+    shapes = [compact, compact, row] if half == 0 else [jax.ShapeDtypeStruct((pairs, 3 * b, b), BF16), row]
     return pl.pallas_call(
         functools.partial(inner_kernel, first, half, cells, len(pieces)),
         in_specs=[SMEM] * 2 + [VMEM] * (len(pieces) + 1 + len(early)),
@@ -376,7 +369,7 @@
     def dims_of(k):
         return [dim for i, dim in enumerate(DIMS) if (k >> (2 - i)) & 1]
 
-    away = (2, 1, 4, 5, 6, 3, 7)
+    away = range(1, 8)
     rest = rest_dims(terms)
 
     own = psi_start[0]
@@ -394,9 +387,13 @@
     energies = []
     for sweep in range(ITERS):
         first = sweep == 0
-        early, late = ([pieces[i] for i in picked(first, half)] for half in range(2))
-        early = inner(first, 0, cells, sectors, pair_in, pair_count, early, right)
-        cat, inv = inner(first, 1, cells, sectors, pair_in, pair_count, late, right, early)
+        args = (cells, sectors, pair_in, pair_count)
+        if first:
+            early, late = ([pieces[i] for i in picked(half, len(pieces))] for half in range(2))
+            early = inner(first, 0, *args, early, right)
+            cat, inv = inner(first, 1, *args, late, right, early)
+        else:
+            cat, inv = inner(first, None, *args, pieces, right)
         rho = zero
         keeps, recvs = [], []
         for h in range(CHUNKS):

time: 128 us -> 128 us (level)
  Pallas kernels: 25.3 us -> 23.5 us
    pallas_call x4 -> x3, Pallas kernels: 11.5 us -> 9.73 us  [inner(): pl.pallas_call(functools.partial(inner_kernel, first, half, cells, len(pi...]
  transfers between devices with their start and end apart: 43 -> 43, of which waited for: 24 -> 27; matrix products, arithmetic and copies ran while one was open for 2% -> 2% of each run, Pallas kernels for 6% -> 3%
where the time goes in v1:
time: 128 us; the launch traced here: 127 us
  waiting for transfers between devices  53.6 us (42%)
  starting transfers between devices  39.1 us (31%)
  Pallas kernels  23.5 us (18%)
  local copies, waits for them, and re-layouts  7.67 us (6%)
  other arithmetic  1.85 us (1%)
  between operations  1.54 us (1%)
    ppermute x43, waiting for transfers between devices, swap(): lax.ppermute(x, AXES, flips(mesh_shape, even, even if odd is None else odd))  53.6 us
    ppermute x43, starting transfers between devices, swap(): lax.ppermute(x, AXES, flips(mesh_shape, even, even if odd is None else odd))  39.1 us
    pallas_call x4, Pallas kernels, outer(): pl.pallas_call(functools.partial(outer_kernel, first, chunk, cells, len(p...  11.2 us
    pallas_call x3, Pallas kernels, inner(): pl.pallas_call(functools.partial(inner_kernel, first, half, cells, len(pi...  9.73 us
    unnamed x14, local copies, waits for them, and re-layouts  5.47 us
  transfers between devices with their start and end apart: 43, of which 27 were waited for; matrix products, arithmetic and copies ran while one was open for 2% of the time, Pallas kernels for 3%

profile of v1, /device:TPU:0, one launch (start us, length us, event | category | flops | bytes accessed | tf_op | source)
XLA Modules:
  0.0 127.3 jit_solution(467949626622166799)
XLA Ops:
  1.8 3.1 %collective-permute-start.1 = (f32[192,384]{1,0:T(8,128)S(1)}, f32[192,384]{1,0:T(8,128)S(1)}, u32[]{:S(2)}, u32[]{:S(2)}) collective-permute-start(f32[192,384]{1,0:T(8,128)S(1)} %get-tuple-element.111), channel_id=1, source_target_pairs={{0,2},{1,3},{2,0},{3,1},{4,6},{5,7},{6,4},{7,5},{8,10},{9,11},{10,... | collective-permute-start | bytes 884744 | tf_op jit(solution)/shard_map/ppermute | solution.py:367
  12.7 5.5 %collective-permute-done.3.refs_4_.refs_6_ = f32[192,384]{1,0:T(8,128)S(1)} collective-permute-done((f32[192,384]{1,0:T(8,128)S(1)}, f32[192,384]{1,0:T(8,128)S(1)}, u32[]{:S(2)}, u32[]{:S(2)}) %collective-permute-start.3) | collective-permute-done | bytes 294944 | tf_op jit(solution)/shard_map/ppermute | solution.py:367
  18.9 2.9 %shard_map.87 = (bf16[4,192,384]{2,1,0:T(8,128)(2,1)S(1)}, bf16[4,192,384]{2,1,0:T(8,128)(2,1)S(1)}, f32[8,384]{1,0:T(8,128)S(1)}) custom-call(s32[1,4]{1,0:T(1,128)S(1)} %copy-done.6, s32[1]{0:T(128)S(6)} %copy.9.refs_1_, f32[384,384]{1,0:T(8,128)S(1)} %bitcast.8, f32[384,384]{1,0:T(8,128)S(1)} %collective-permute-done.refs_3_, ...), custom_call_target="tpu_custom_call" | custom-call | flops 679477248 | bytes 4718592 | tf_op jit(solution)/shard_map/pallas_call | solution.py:189
  21.8 3.0 %shard_map.88 = (bf16[4,1152,384]{2,1,0:T(8,128)(2,1)S(1)}, f32[8,384]{1,0:T(8,128)S(1)}) custom-call(s32[1,4]{1,0:T(1,128)S(1)} %copy-done.6, s32[1]{0:T(128)S(6)} %copy.9.refs_1_, f32[384,384]{1,0:T(8,128)S(1)} %bitcast.9, f32[384,384]{1,0:T(8,128)S(1)} %collective-permute-done.refs_3_, f32[192,384]{1,0:T(8,128)S(1)} %collective-permute-done.3.refs_4_.refs_6_, ...), custom_call_target="tpu_custom_call" | custom-call | flops 679477248 | bytes 4718592 | tf_op jit(solution)/shard_map/pallas_call | solution.py:189
  24.8 2.5 %shard_map.89 = (f32[1152,128]{1,0:T(8,128)S(1)}, f32[1152,128]{1,0:T(8,128)S(1)}, f32[8,128]{1,0:T(8,128)S(1)}) custom-call(s32[1,4]{1,0:T(1,128)S(1)} %copy-done.5, s32[1]{0:T(128)S(6)} %copy.9.refs_1_, f32[384,384]{1,0:T(8,128)S(1)} %bitcast.10, f32[384,384]{1,0:T(8,128)S(1)} %collective-permute-done.refs_3_, ...), custom_call_target="tpu_custom_call" | custom-call | flops 679477248 | bytes 4718592 | tf_op jit(solution)/shard_map/pallas_call | solution.py:240
  27.3 3.1 %shard_map.94 = (f32[1160,128]{1,0:T(8,128)S(1)}, f32[1160,128]{1,0:T(8,128)S(1)}, f32[8,128]{1,0:T(8,128)}) custom-call(s32[1,4]{1,0:T(1,128)S(1)} %copy-done.5, s32[1]{0:T(128)S(6)} %copy.9.refs_1_, f32[384,384]{1,0:T(8,128)S(1)} %bitcast.11, f32[384,384]{1,0:T(8,128)S(1)} %collective-permute-done.refs_3_, f32[192,384]{1,0:T(8,128)S(1)} %collective-permute-done.1.refs_4_, ...), custom_call_target="tpu_custom_call" | custom-call | flops 679477248 | bytes 4718592 | tf_op jit(solution)/shard_map/pallas_call | solution.py:240
  34.7 4.6 %collective-permute-done.11.recv_ref = f32[584,128]{1,0:T(8,128)S(1)} collective-permute-done((f32[584,128]{1,0:T(8,128)S(1)}, f32[584,128]{1,0:T(8,128)S(1)}, u32[]{:S(2)}, u32[]{:S(2)}) %collective-permute-start.11) | collective-permute-done | bytes 299040 | tf_op jit(solution)/shard_map/ppermute | solution.py:367
  39.4 3.0 %collective-permute-done.6.recv_ref = f32[576,128]{1,0:T(8,128)S(1)} collective-permute-done((f32[576,128]{1,0:T(8,128)S(1)}, f32[576,128]{1,0:T(8,128)S(1)}, u32[]{:S(2)}, u32[]{:S(2)}) %collective-permute-start.6) | collective-permute-done | bytes 294944 | tf_op jit(solution)/shard_map/ppermute | solution.py:367
  42.6 2.5 %collective-permute-done.12.recv_ref = f32[296,128]{1,0:T(8,128)S(1)} collective-permute-done((f32[296,128]{1,0:T(8,128)S(1)}, f32[296,128]{1,0:T(8,128)S(1)}, u32[]{:S(2)}, u32[]{:S(2)}) %collective-permute-start.12) | collective-permute-done | bytes 151584 | tf_op jit(solution)/shard_map/ppermute | solution.py:367
  50.0 2.4 %collective-permute-start.14 = (f32[152,128]{1,0:T(8,128)S(1)}, f32[152,128]{1,0:T(8,128)S(1)}, u32[]{:S(2)}, u32[]{:S(2)}) collective-permute-start(f32[152,128]{1,0:T(8,128)S(1)} %shard_map.98.refs_2_), channel_id=1, source_target_pairs={{0,16},{1,17},{2,18},{3,19},{4,20},{5,21},{6,22},{7,23},{8,24},{9,... | collective-permute-start | bytes 233480 | tf_op jit(solution)/shard_map/ppermute | solution.py:367
  52.6 2.4 %collective-permute-start.9 = (f32[144,128]{1,0:T(8,128)S(1)}, f32[144,128]{1,0:T(8,128)S(1)}, u32[]{:S(2)}, u32[]{:S(2)}) collective-permute-start(f32[144,128]{1,0:T(8,128)S(1)} %shard_map.93.refs_0_), channel_id=1, source_target_pairs={{0,16},{1,17},{2,18},{3,19},{4,20},{5,21},{6,22},{7,23},{8,24},{9,... | collective-permute-start | bytes 221192 | tf_op jit(solution)/shard_map/ppermute | solution.py:367
  55.0 3.4 %collective-permute-done.9.refs_1_ = f32[144,128]{1,0:T(8,128)S(1)} collective-permute-done((f32[144,128]{1,0:T(8,128)S(1)}, f32[144,128]{1,0:T(8,128)S(1)}, u32[]{:S(2)}, u32[]{:S(2)}) %collective-permute-start.9) | collective-permute-done | bytes 73760 | tf_op jit(solution)/shard_map/ppermute | solution.py:367
  65.5 2.3 %collective-permute-start.26 = (f32[96,384]{1,0:T(8,128)S(1)}, f32[96,384]{1,0:T(8,128)S(1)}, u32[]{:S(2)}, u32[]{:S(2)}) collective-permute-start(f32[96,384]{1,0:T(8,128)S(1)} %get-tuple-element.87.refs_2_.refs_4_), channel_id=1, source_target_pairs={{0,6},{1,7},{2,4},{3,5},{4,2},{5,3},{6,0},{7,1},{8,14},{9,15},{10,... | collective-permute-start | bytes 442376 | tf_op jit(solution)/shard_map/ppermute | solution.py:367
  67.8 2.2 %collective-permute-done.18.refs_6_ = f32[96,384]{1,0:T(8,128)S(1)} collective-permute-done((f32[96,384]{1,0:T(8,128)S(1)}, f32[96,384]{1,0:T(8,128)S(1)}, u32[]{:S(2)}, u32[]{:S(2)}) %collective-permute-start.18) | collective-permute-done | bytes 147488 | tf_op jit(solution)/shard_map/ppermute | solution.py:367
  74.1 4.1 %collective-permute-done.26.refs_14_ = f32[96,384]{1,0:T(8,128)S(1)} collective-permute-done((f32[96,384]{1,0:T(8,128)S(1)}, f32[96,384]{1,0:T(8,128)S(1)}, u32[]{:S(2)}, u32[]{:S(2)}) %collective-permute-start.26) | collective-permute-done | bytes 147488 | tf_op jit(solution)/shard_map/ppermute | solution.py:367
  80.3 3.9 %shard_map.100 = (bf16[4,1152,384]{2,1,0:T(8,128)(2,1)S(1)}, f32[8,384]{1,0:T(8,128)S(1)}) custom-call(s32[1,4]{1,0:T(1,128)S(1)} %copy-done.6, s32[1]{0:T(128)S(6)} %copy.9.refs_1_, f32[96,384]{1,0:T(8,128)S(1)} %get-tuple-element.87.refs_2_.refs_4_, f32[96,384]{1,0:T(8,128)S(1)} %collective-permute-done.15.refs_3_, ...), custom_call_target="tpu_custom_call" | custom-call | flops 1358954496 | bytes 4718592 | tf_op jit(solution)/shard_map/pallas_call | solution.py:189
  84.2 2.5 %shard_map.102 = (f32[1152,128]{1,0:T(8,128)S(1)}, f32[1152,128]{1,0:T(8,128)S(1)}, f32[8,128]{1,0:T(8,128)S(1)}) custom-call(s32[1,4]{1,0:T(1,128)S(1)} %copy-done.5, s32[1]{0:T(128)S(6)} %copy.9.refs_1_, f32[96,384]{1,0:T(8,128)S(1)} %get-tuple-element.87.refs_2_.refs_4_, f32[96,384]{1,0:T(8,128)S(1)} %collective-permute-done.15.refs_3_, ...), custom_call_target="tpu_custom_call" | custom-call | flops 679477248 | bytes 4718592 | tf_op jit(solution)/shard_map/pallas_call | solution.py:240
  86.7 3.1 %shard_map.107 = (f32[1160,128]{1,0:T(8,128)S(1)}, f32[1160,128]{1,0:T(8,128)S(1)}, f32[8,128]{1,0:T(8,128)}) custom-call(s32[1,4]{1,0:T(1,128)S(1)} %copy-done.5, s32[1]{0:T(128)S(6)} %copy.9.refs_1_, f32[96,384]{1,0:T(8,128)S(1)} %get-tuple-element.87.refs_2_.refs_4_, f32[96,384]{1,0:T(8,128)S(1)} %collective-permute-done.15.refs_3_, ...), custom_call_target="tpu_custom_call" | custom-call | flops 679477248 | bytes 4718592 | tf_op jit(solution)/shard_map/pallas_call | solution.py:240
  94.1 4.6 %collective-permute-done.36.recv_ref = f32[584,128]{1,0:T(8,128)S(1)} collective-permute-done((f32[584,128]{1,0:T(8,128)S(1)}, f32[584,128]{1,0:T(8,128)S(1)}, u32[]{:S(2)}, u32[]{:S(2)}) %collective-permute-start.36) | collective-permute-done | bytes 299040 | tf_op jit(solution)/shard_map/ppermute | solution.py:367
  98.9 3.0 %collective-permute-done.31.recv_ref = f32[576,128]{1,0:T(8,128)S(1)} collective-permute-done((f32[576,128]{1,0:T(8,128)S(1)}, f32[576,128]{1,0:T(8,128)S(1)}, u32[]{:S(2)}, u32[]{:S(2)}) %collective-permute-start.31) | collective-permute-done | bytes 294944 | tf_op jit(solution)/shard_map/ppermute | solution.py:367
  102.0 2.1 %collective-permute-done.37.recv_ref = f32[296,128]{1,0:T(8,128)S(1)} collective-permute-done((f32[296,128]{1,0:T(8,128)S(1)}, f32[296,128]{1,0:T(8,128)S(1)}, u32[]{:S(2)}, u32[]{:S(2)}) %collective-permute-start.37) | collective-permute-done | bytes 151584 | tf_op jit(solution)/shard_map/ppermute | solution.py:367
  108.7 2.3 %collective-permute-start.39 = (f32[152,128]{1,0:T(8,128)S(1)}, f32[152,128]{1,0:T(8,128)S(1)}, u32[]{:S(2)}, u32[]{:S(2)}) collective-permute-start(f32[152,128]{1,0:T(8,128)S(1)} %shard_map.111.refs_2_), channel_id=1, source_target_pairs={{0,16},{1,17},{2,18},{3,19},{4,20},{5,21},{6,22},{7,23},{8,24},{9,... | collective-permute-start | bytes 233480 | tf_op jit(solution)/shard_map/ppermute | solution.py:367
  113.6 3.7 %collective-permute-done.34.refs_1_ = f32[144,128]{1,0:T(8,128)S(1)} collective-permute-done((f32[144,128]{1,0:T(8,128)S(1)}, f32[144,128]{1,0:T(8,128)S(1)}, u32[]{:S(2)}, u32[]{:S(2)}) %collective-permute-start.34) | collective-permute-done | bytes 73760 | tf_op jit(solution)/shard_map/ppermute | solution.py:367
  123.8 2.7 %collective-permute-done.41.refs_2_ = f32[96,384]{1,0:T(8,128)S(1)} collective-permute-done((f32[96,384]{1,0:T(8,128)S(1)}, f32[96,384]{1,0:T(8,128)S(1)}, u32[]{:S(2)}, u32[]{:S(2)}) %collective-permute-start.41) | collective-permute-done | bytes 147488 | tf_op jit(solution)/shard_map/ppermute | solution.py:367
  (109 shorter events, 50.9 us)
Async XLA Ops:
  1.8 10.9 %collective-permute-start.1 = (f32[192,384]{1,0:T(8,128)S(1)}, f32[192,384]{1,0:T(8,128)S(1)}, u32[]{:S(2)}, u32[]{:S(2)}) collective-permute-start(f32[192,384]{1,0:T(8,128)S(1)} %get-tuple-element.111), channel_id=1, source_target_pairs={{0,2},{1,3},{2,0},{3,1},{4,6},{5,7},{6,4},{7,5},{8,10},{9,11},{10,... | collective-permute-start | bytes 884744 | tf_op jit(solution)/shard_map/ppermute | solution.py:367
  4.9 14.0 %collective-permute-start = (f32[384,384]{1,0:T(8,128)}, f32[384,384]{1,0:T(8,128)S(1)}, u32[]{:S(2)}, u32[]{:S(2)}) collective-permute-start(f32[384,384]{1,0:T(8,128)} %bitcast.7), channel_id=1, source_target_pairs={{0,1},{1,0},{2,3},{3,2},{4,5},{5,4},{6,7},{7,6},{8,9},{9,8},{10,11... | collective-permute-start | bytes 1769480 | tf_op jit(solution)/shard_map/ppermute | solution.py:367
  4.9 13.3 %collective-permute-start.3 = (f32[192,384]{1,0:T(8,128)S(1)}, f32[192,384]{1,0:T(8,128)S(1)}, u32[]{:S(2)}, u32[]{:S(2)}) collective-permute-start(f32[192,384]{1,0:T(8,128)S(1)} %get-tuple-element.110), channel_id=1, source_target_pairs={{0,2},{1,3},{2,0},{3,1},{4,6},{5,7},{6,4},{7,5},{8,10},{9,11},{10,... | collective-permute-start | bytes 884744 | tf_op jit(solution)/shard_map/ppermute | solution.py:367
  12.7 6.1 %collective-permute-start.2 = (f32[192,384]{1,0:T(8,128)S(1)}, f32[192,384]{1,0:T(8,128)S(1)}, u32[]{:S(2)}, u32[]{:S(2)}) collective-permute-start(f32[192,384]{1,0:T(8,128)S(1)} %collective-permute-done.1.refs_4_), channel_id=1, source_target_pairs={{0,1},{1,0},{2,3},{3,2},{4,5},{5,4},{6,7},{7,6},{8,9},{9,8},{10,11... | collective-permute-start | bytes 884744 | tf_op jit(solution)/shard_map/ppermute | solution.py:367
  32.5 6.8 %collective-permute-start.11 = (f32[584,128]{1,0:T(8,128)S(1)}, f32[584,128]{1,0:T(8,128)S(1)}, u32[]{:S(2)}, u32[]{:S(2)}) collective-permute-start(f32[584,128]{1,0:T(8,128)S(1)} %get-tuple-element.80), channel_id=1, source_target_pairs={{0,2},{1,9},{2,0},{3,11},{4,6},{5,13},{6,4},{7,15},{8,10},{9,1},{1... | collective-permute-start | bytes 897032 | tf_op jit(solution)/shard_map/ppermute | solution.py:367
  33.3 9.2 %collective-permute-start.6 = (f32[576,128]{1,0:T(8,128)S(1)}, f32[576,128]{1,0:T(8,128)S(1)}, u32[]{:S(2)}, u32[]{:S(2)}) collective-permute-start(f32[576,128]{1,0:T(8,128)S(1)} %get-tuple-element.71), channel_id=1, source_target_pairs={{0,2},{1,9},{2,0},{3,11},{4,6},{5,13},{6,4},{7,15},{8,10},{9,1},{1... | collective-permute-start | bytes 884744 | tf_op jit(solution)/shard_map/ppermute | solution.py:367
  39.3 5.7 %collective-permute-start.12 = (f32[296,128]{1,0:T(8,128)S(1)}, f32[296,128]{1,0:T(8,128)S(1)}, u32[]{:S(2)}, u32[]{:S(2)}) collective-permute-start(f32[296,128]{1,0:T(8,128)S(1)} %get-tuple-element.82), channel_id=1, source_target_pairs={{0,4},{1,5},{2,6},{3,7},{4,0},{5,1},{6,2},{7,3},{8,12},{9,13},{10,... | collective-permute-start | bytes 454664 | tf_op jit(solution)/shard_map/ppermute | solution.py:367
  50.0 8.4 %collective-permute-start.14 = (f32[152,128]{1,0:T(8,128)S(1)}, f32[152,128]{1,0:T(8,128)S(1)}, u32[]{:S(2)}, u32[]{:S(2)}) collective-permute-start(f32[152,128]{1,0:T(8,128)S(1)} %shard_map.98.refs_2_), channel_id=1, source_target_pairs={{0,16},{1,17},{2,18},{3,19},{4,20},{5,21},{6,22},{7,23},{8,24},{9,... | collective-permute-start | bytes 233480 | tf_op jit(solution)/shard_map/ppermute | solution.py:367
  52.6 5.8 %collective-permute-start.9 = (f32[144,128]{1,0:T(8,128)S(1)}, f32[144,128]{1,0:T(8,128)S(1)}, u32[]{:S(2)}, u32[]{:S(2)}) collective-permute-start(f32[144,128]{1,0:T(8,128)S(1)} %shard_map.93.refs_0_), channel_id=1, source_target_pairs={{0,16},{1,17},{2,18},{3,19},{4,20},{5,21},{6,22},{7,23},{8,24},{9,... | collective-permute-start | bytes 221192 | tf_op jit(solution)/shard_map/ppermute | solution.py:367
  58.6 6.9 %collective-permute-start.16 = (f32[96,384]{1,0:T(8,128)S(1)}, f32[96,384]{1,0:T(8,128)S(1)}, u32[]{:S(2)}, u32[]{:S(2)}) collective-permute-start(f32[96,384]{1,0:T(8,128)S(1)} %get-tuple-element.87.refs_2_.refs_4_), channel_id=1, source_target_pairs={{0,8},{1,9},{2,10},{3,11},{4,12},{5,13},{6,14},{7,15},{8,0},{9,1},... | collective-permute-start | bytes 442376 | tf_op jit(solution)/shard_map/ppermute | solution.py:367
  60.5 9.5 %collective-permute-start.18 = (f32[96,384]{1,0:T(8,128)S(1)}, f32[96,384]{1,0:T(8,128)S(1)}, u32[]{:S(2)}, u32[]{:S(2)}) collective-permute-start(f32[96,384]{1,0:T(8,128)S(1)} %get-tuple-element.87.refs_2_.refs_4_), channel_id=1, source_target_pairs={{0,4},{1,5},{2,6},{3,7},{4,0},{5,1},{6,2},{7,3},{8,12},{9,13},{10,... | collective-permute-start | bytes 442376 | tf_op jit(solution)/shard_map/ppermute | solution.py:367
  61.8 10.4 %collective-permute-start.20 = (f32[96,384]{1,0:T(8,128)S(1)}, f32[96,384]{1,0:T(8,128)S(1)}, u32[]{:S(2)}, u32[]{:S(2)}) collective-permute-start(f32[96,384]{1,0:T(8,128)S(1)} %get-tuple-element.87.refs_2_.refs_4_), channel_id=1, source_target_pairs={{0,12},{1,13},{2,14},{3,15},{4,8},{5,9},{6,10},{7,11},{8,4},{9,5},... | collective-permute-start | bytes 442376 | tf_op jit(solution)/shard_map/ppermute | solution.py:367
  62.1 10.0 %collective-permute-start.22 = (f32[96,384]{1,0:T(8,128)S(1)}, f32[96,384]{1,0:T(8,128)S(1)}, u32[]{:S(2)}, u32[]{:S(2)}) collective-permute-start(f32[96,384]{1,0:T(8,128)S(1)} %get-tuple-element.87.refs_2_.refs_4_), channel_id=1, source_target_pairs={{0,2},{1,3},{2,0},{3,1},{4,6},{5,7},{6,4},{7,5},{8,10},{9,11},{10,... | collective-permute-start | bytes 442376 | tf_op jit(solution)/shard_map/ppermute | solution.py:367
  63.5 10.6 %collective-permute-start.24 = (f32[96,384]{1,0:T(8,128)S(1)}, f32[96,384]{1,0:T(8,128)S(1)}, u32[]{:S(2)}, u32[]{:S(2)}) collective-permute-start(f32[96,384]{1,0:T(8,128)S(1)} %get-tuple-element.87.refs_2_.refs_4_), channel_id=1, source_target_pairs={{0,10},{1,11},{2,8},{3,9},{4,14},{5,15},{6,12},{7,13},{8,2},{9,3},... | collective-permute-start | bytes 442376 | tf_op jit(solution)/shard_map/ppermute | solution.py:367
  65.5 12.7 %collective-permute-start.26 = (f32[96,384]{1,0:T(8,128)S(1)}, f32[96,384]{1,0:T(8,128)S(1)}, u32[]{:S(2)}, u32[]{:S(2)}) collective-permute-start(f32[96,384]{1,0:T(8,128)S(1)} %get-tuple-element.87.refs_2_.refs_4_), channel_id=1, source_target_pairs={{0,6},{1,7},{2,4},{3,5},{4,2},{5,3},{6,0},{7,1},{8,14},{9,15},{10,... | collective-permute-start | bytes 442376 | tf_op jit(solution)/shard_map/ppermute | solution.py:367
  70.1 8.1 %collective-permute-start.28 = (f32[96,384]{1,0:T(8,128)S(1)}, f32[96,384]{1,0:T(8,128)S(1)}, u32[]{:S(2)}, u32[]{:S(2)}) collective-permute-start(f32[96,384]{1,0:T(8,128)S(1)} %get-tuple-element.87.refs_2_.refs_4_), channel_id=1, source_target_pairs={{0,14},{1,15},{2,12},{3,13},{4,10},{5,11},{6,8},{7,9},{8,6},{9,7},... | collective-permute-start | bytes 442376 | tf_op jit(solution)/shard_map/ppermute | solution.py:367
  72.1 6.5 %collective-permute-start.17 = (f32[96,384]{1,0:T(8,128)S(1)}, f32[96,384]{1,0:T(8,128)S(1)}, u32[]{:S(2)}, u32[]{:S(2)}) collective-permute-start(f32[96,384]{1,0:T(8,128)S(1)} %collective-permute-done.16.refs_4_), channel_id=1, source_target_pairs={{0,1},{1,0},{2,3},{3,2},{4,5},{5,4},{6,7},{7,6},{8,9},{9,8},{10,11... | collective-permute-start | bytes 442376 | tf_op jit(solution)/shard_map/ppermute | solution.py:367
  72.2 6.6 %collective-permute-start.19 = (f32[96,384]{1,0:T(8,128)S(1)}, f32[96,384]{1,0:T(8,128)S(1)}, u32[]{:S(2)}, u32[]{:S(2)}) collective-permute-start(f32[96,384]{1,0:T(8,128)S(1)} %collective-permute-done.18.refs_6_), channel_id=1, source_target_pairs={{0,1},{1,0},{2,3},{3,2},{4,5},{5,4},{6,7},{7,6},{8,9},{9,8},{10,11... | collective-permute-start | bytes 442376 | tf_op jit(solution)/shard_map/ppermute | solution.py:367
  91.9 6.8 %collective-permute-start.36 = (f32[584,128]{1,0:T(8,128)S(1)}, f32[584,128]{1,0:T(8,128)S(1)}, u32[]{:S(2)}, u32[]{:S(2)}) collective-permute-start(f32[584,128]{1,0:T(8,128)S(1)} %get-tuple-element.103), channel_id=1, source_target_pairs={{0,2},{1,9},{2,0},{3,11},{4,6},{5,13},{6,4},{7,15},{8,10},{9,1},{1... | collective-permute-start | bytes 897032 | tf_op jit(solution)/shard_map/ppermute | solution.py:367
  92.7 9.2 %collective-permute-start.31 = (f32[576,128]{1,0:T(8,128)S(1)}, f32[576,128]{1,0:T(8,128)S(1)}, u32[]{:S(2)}, u32[]{:S(2)}) collective-permute-start(f32[576,128]{1,0:T(8,128)S(1)} %get-tuple-element.94), channel_id=1, source_target_pairs={{0,2},{1,9},{2,0},{3,11},{4,6},{5,13},{6,4},{7,15},{8,10},{9,1},{1... | collective-permute-start | bytes 884744 | tf_op jit(solution)/shard_map/ppermute | solution.py:367
  108.7 8.6 %collective-permute-start.39 = (f32[152,128]{1,0:T(8,128)S(1)}, f32[152,128]{1,0:T(8,128)S(1)}, u32[]{:S(2)}, u32[]{:S(2)}) collective-permute-start(f32[152,128]{1,0:T(8,128)S(1)} %shard_map.111.refs_2_), channel_id=1, source_target_pairs={{0,16},{1,17},{2,18},{3,19},{4,20},{5,21},{6,22},{7,23},{8,24},{9,... | collective-permute-start | bytes 233480 | tf_op jit(solution)/shard_map/ppermute | solution.py:367
  117.3 6.4 %collective-permute-start.40 = (f32[96,384]{1,0:T(8,128)S(1)}, f32[96,384]{1,0:T(8,128)S(1)}, u32[]{:S(2)}, u32[]{:S(2)}) collective-permute-start(f32[96,384]{1,0:T(8,128)S(1)} %get-tuple-element.108.refs_0_), channel_id=1, source_target_pairs={{0,8},{1,9},{2,10},{3,11},{4,12},{5,13},{6,14},{7,15},{8,0},{9,1},... | collective-permute-start | bytes 442376 | tf_op jit(solution)/shard_map/ppermute | solution.py:367
  118.8 7.7 %collective-permute-start.41 = (f32[96,384]{1,0:T(8,128)S(1)}, f32[96,384]{1,0:T(8,128)S(1)}, u32[]{:S(2)}, u32[]{:S(2)}) collective-permute-start(f32[96,384]{1,0:T(8,128)S(1)} %get-tuple-element.108.refs_0_), channel_id=1, source_target_pairs={{0,4},{1,5},{2,6},{3,7},{4,0},{5,1},{6,2},{7,3},{8,12},{9,13},{10,... | collective-permute-start | bytes 442376 | tf_op jit(solution)/shard_map/ppermute | solution.py:367
  119.8 6.7 %collective-permute-start.42 = (f32[96,384]{1,0:T(8,128)S(1)}, f32[96,384]{1,0:T(8,128)S(1)}, u32[]{:S(2)}, u32[]{:S(2)}) collective-permute-start(f32[96,384]{1,0:T(8,128)S(1)} %get-tuple-element.108.refs_0_), channel_id=1, source_target_pairs={{0,12},{1,13},{2,14},{3,15},{4,8},{5,9},{6,10},{7,11},{8,4},{9,5},... | collective-permute-start | bytes 442376 | tf_op jit(solution)/shard_map/ppermute | solution.py:367
  (26 other events, 114.3 us)

commit v2 on v1

--- a/solution.py
+++ b/solution.py
@@ -24,6 +24,7 @@
 DIMS = (("sector", 1), ("term", 0), ("term", 1))
 CORE = ("sector", 0)
 ORDERS = ((0, 1, 2), (2, 1, 0))
+START_ORDER = (4, 2, 1, 6, 5, 3, 7)
 
 
 def matmul_cost(pairs, rows, b):
@@ -48,17 +49,9 @@
     return place([bit_of(*dim) ^ ((k >> (2 - i)) & 1) for i, dim in enumerate(DIMS)], parity, rows)
 
 
-def slot_bits(j, order):
-    flip = [0, 0, 0]
-    for i, dim in enumerate(order):
-        flip[dim] = (j >> (2 - i)) & 1
-    return flip
-
-
-def slot_place(j, parity, rows):
-    a, b = slot_bits(j, ORDERS[0]), slot_bits(j, ORDERS[1])
-    flip = [x if x == y else jnp.where(parity == 0, x, y) for x, y in zip(a, b)]
-    return place([bit_of(*dim) ^ f for dim, f in zip(DIMS, flip)], parity, rows)
+def slot_of(parity, masks):
+    a, b = (sum(masks[dim] << (2 - i) for i, dim in enumerate(order)) for order in ORDERS)
+    return jnp.where(parity == 0, a, b)
 
 
 def split(x):
@@ -118,7 +111,7 @@
 def store_wide(dest, start, x):
     rows = x.shape[0]
     for c in range(x.shape[1] // TILE[1]):
-        dest[start + c * rows:start + (c + 1) * rows, :] = x[:, c * TILE[1]:(c + 1) * TILE[1]]
+        dest[pl.ds(start + c * rows, rows), :] = x[:, c * TILE[1]:(c + 1) * TILE[1]]
 
 
 DOT_NT = functools.partial(
@@ -216,16 +209,24 @@
     scale = inv_ref[:1, :]
     rho = jnp.zeros((1, b), F32)
     wide = shard * b // TILE[1]
-    for piece, cuts in zip(parts, segments(first, rows, shard)):
+    for number, (piece, cuts) in enumerate(zip(parts, segments(first, rows, shard))):
+        side = number & 1
+        dest = send_ref if side else keep_ref
         for at, sector, start, row, size in cuts:
-            if at == chunk:
-                x = acc[sector, pl.ds(row, size), :] * piece[start:start + size, :]
-                rho += jnp.sum(x, axis=0, keepdims=True)
-    for dest, parity in ((send_ref, 1 - core), (keep_ref, core)):
-        for j in range(8):
-            sector, row = slot_place(j, parity, shard)
-            store_wide(dest, j * wide, acc[sector, pl.ds(row, shard), :] * scale)
-    rho = jnp.broadcast_to(jnp.sum(rho * scale * scale, axis=1, keepdims=True), TILE) / cells + before_ref[...]
+            if at != chunk:
+                continue
+            for q in range(size // shard):
+                if first:
+                    masks = (int(number > 1), (q >> 1) ^ bit_of(*DIMS[1]), (q & 1) ^ bit_of(*DIMS[2]))
+                    here = pl.ds(q * shard, shard)
+                else:
+                    masks = tuple((number >> (3 - i)) & 1 for i in range(3))
+                    here = pl.ds(row, shard)
+                x = acc[sector, here, :] * scale
+                slot = slot_of(core ^ side, masks)
+                store_wide(dest, pl.multiple_of(slot * wide, 8), x)
+                rho += jnp.sum(x * piece[start + q * shard:start + (q + 1) * shard, :], axis=0, keepdims=True)
+    rho = jnp.broadcast_to(jnp.sum(rho * scale, axis=1, keepdims=True), TILE) / cells + before_ref[...]
     rho_ref[...] = rho
     if chunk == CHUNKS - 1:
         send_ref[8 * wide:, :] = rho
@@ -369,7 +370,7 @@
     def dims_of(k):
         return [dim for i, dim in enumerate(DIMS) if (k >> (2 - i)) & 1]
 
-    away = range(1, 8)
+    away = START_ORDER
     rest = rest_dims(terms)
 
     own = psi_start[0]
@@ -397,9 +398,7 @@
         rho = zero
         keeps, recvs = [], []
         for h in range(CHUNKS):
-            send, keep, rho = outer(
-                first, h, cells, sectors, pair_out, pair_count, pieces, (left, cat), inv, rho
-            )
+            send, keep, rho = outer(first, h, cells, sectors, pair_out, pair_count, pieces, (left, cat), inv, rho)
             keeps.append(keep)
             recvs.append(swap(send, [CORE]))
         for step in zip(*ORDERS):

time: 128 us -> 127 us (level)
  no operation moved by 1% of the time
where the time goes in v2:
time: 127 us
  waiting for transfers between devices  53.6 us (42%)
  starting transfers between devices  39.2 us (31%)
  Pallas kernels  23.4 us (18%)
  local copies, waits for them, and re-layouts  7.67 us (6%)
  other arithmetic  1.85 us (1%)
  between operations  1.54 us (1%)
    ppermute x43, waiting for transfers between devices, swap(): lax.ppermute(x, AXES, flips(mesh_shape, even, even if odd is None else odd))  53.6 us
    ppermute x43, starting transfers between devices, swap(): lax.ppermute(x, AXES, flips(mesh_shape, even, even if odd is None else odd))  39.2 us
    pallas_call x4, Pallas kernels, outer(): pl.pallas_call(functools.partial(outer_kernel, first, chunk, cells, len(p...  11.1 us
    pallas_call x3, Pallas kernels, inner(): pl.pallas_call(functools.partial(inner_kernel, first, half, cells, len(pi...  9.73 us
    unnamed x14, local copies, waits for them, and re-layouts  5.47 us
  transfers between devices with their start and end apart: 43, of which 27 were waited for; matrix products, arithmetic and copies ran while one was open for 2% of the time, Pallas kernels for 3%

profile of v2, /device:TPU:0, one launch (start us, length us, event | category | flops | bytes accessed | tf_op | source)
XLA Modules:
  0.0 127.1 jit_solution(11638187556106124877)
XLA Ops:
  1.8 3.1 %collective-permute-start.1 = (f32[192,384]{1,0:T(8,128)S(1)}, f32[192,384]{1,0:T(8,128)S(1)}, u32[]{:S(2)}, u32[]{:S(2)}) collective-permute-start(f32[192,384]{1,0:T(8,128)S(1)} %get-tuple-element.111), channel_id=1, source_target_pairs={{0,2},{1,3},{2,0},{3,1},{4,6},{5,7},{6,4},{7,5},{8,10},{9,11},{10,... | collective-permute-start | bytes 884744 | tf_op jit(solution)/shard_map/ppermute | solution.py:368
  12.7 5.5 %collective-permute-done.3.refs_4_.refs_6_ = f32[192,384]{1,0:T(8,128)S(1)} collective-permute-done((f32[192,384]{1,0:T(8,128)S(1)}, f32[192,384]{1,0:T(8,128)S(1)}, u32[]{:S(2)}, u32[]{:S(2)}) %collective-permute-start.3) | collective-permute-done | bytes 294944 | tf_op jit(solution)/shard_map/ppermute | solution.py:368
  18.9 2.9 %shard_map.87 = (bf16[4,192,384]{2,1,0:T(8,128)(2,1)S(1)}, bf16[4,192,384]{2,1,0:T(8,128)(2,1)S(1)}, f32[8,384]{1,0:T(8,128)S(1)}) custom-call(s32[1,4]{1,0:T(1,128)S(1)} %copy-done.6, s32[1]{0:T(128)S(6)} %copy.9.refs_1_, f32[384,384]{1,0:T(8,128)S(1)} %bitcast.8, f32[384,384]{1,0:T(8,128)S(1)} %collective-permute-done.refs_3_, ...), custom_call_target="tpu_custom_call" | custom-call | flops 679477248 | bytes 4718592 | tf_op jit(solution)/shard_map/pallas_call | solution.py:182
  21.8 3.0 %shard_map.88 = (bf16[4,1152,384]{2,1,0:T(8,128)(2,1)S(1)}, f32[8,384]{1,0:T(8,128)S(1)}) custom-call(s32[1,4]{1,0:T(1,128)S(1)} %copy-done.6, s32[1]{0:T(128)S(6)} %copy.9.refs_1_, f32[384,384]{1,0:T(8,128)S(1)} %bitcast.9, f32[384,384]{1,0:T(8,128)S(1)} %collective-permute-done.refs_3_, f32[192,384]{1,0:T(8,128)S(1)} %collective-permute-done.3.refs_4_.refs_6_, ...), custom_call_target="tpu_custom_call" | custom-call | flops 679477248 | bytes 4718592 | tf_op jit(solution)/shard_map/pallas_call | solution.py:182
  24.8 2.5 %shard_map.89 = (f32[1152,128]{1,0:T(8,128)S(1)}, f32[1152,128]{1,0:T(8,128)S(1)}, f32[8,128]{1,0:T(8,128)S(1)}) custom-call(s32[1,4]{1,0:T(1,128)S(1)} %copy-done.5, s32[1]{0:T(128)S(6)} %copy.9.refs_1_, f32[384,384]{1,0:T(8,128)S(1)} %bitcast.10, f32[384,384]{1,0:T(8,128)S(1)} %collective-permute-done.refs_3_, ...), custom_call_target="tpu_custom_call" | custom-call | flops 679477248 | bytes 4718592 | tf_op jit(solution)/shard_map/pallas_call | solution.py:241
  27.3 3.1 %shard_map.94 = (f32[1160,128]{1,0:T(8,128)S(1)}, f32[1160,128]{1,0:T(8,128)S(1)}, f32[8,128]{1,0:T(8,128)}) custom-call(s32[1,4]{1,0:T(1,128)S(1)} %copy-done.5, s32[1]{0:T(128)S(6)} %copy.9.refs_1_, f32[384,384]{1,0:T(8,128)S(1)} %bitcast.11, f32[384,384]{1,0:T(8,128)S(1)} %collective-permute-done.refs_3_, f32[192,384]{1,0:T(8,128)S(1)} %collective-permute-done.1.refs_4_, ...), custom_call_target="tpu_custom_call" | custom-call | flops 679477248 | bytes 4718592 | tf_op jit(solution)/shard_map/pallas_call | solution.py:241
  34.6 4.6 %collective-permute-done.11.recv_ref = f32[584,128]{1,0:T(8,128)S(1)} collective-permute-done((f32[584,128]{1,0:T(8,128)S(1)}, f32[584,128]{1,0:T(8,128)S(1)}, u32[]{:S(2)}, u32[]{:S(2)}) %collective-permute-start.11) | collective-permute-done | bytes 299040 | tf_op jit(solution)/shard_map/ppermute | solution.py:368
  39.4 3.0 %collective-permute-done.6.recv_ref = f32[576,128]{1,0:T(8,128)S(1)} collective-permute-done((f32[576,128]{1,0:T(8,128)S(1)}, f32[576,128]{1,0:T(8,128)S(1)}, u32[]{:S(2)}, u32[]{:S(2)}) %collective-permute-start.6) | collective-permute-done | bytes 294944 | tf_op jit(solution)/shard_map/ppermute | solution.py:368
  42.5 2.5 %collective-permute-done.12.recv_ref = f32[296,128]{1,0:T(8,128)S(1)} collective-permute-done((f32[296,128]{1,0:T(8,128)S(1)}, f32[296,128]{1,0:T(8,128)S(1)}, u32[]{:S(2)}, u32[]{:S(2)}) %collective-permute-start.12) | collective-permute-done | bytes 151584 | tf_op jit(solution)/shard_map/ppermute | solution.py:368
  49.9 2.4 %collective-permute-start.14 = (f32[152,128]{1,0:T(8,128)S(1)}, f32[152,128]{1,0:T(8,128)S(1)}, u32[]{:S(2)}, u32[]{:S(2)}) collective-permute-start(f32[152,128]{1,0:T(8,128)S(1)} %shard_map.98.refs_2_), channel_id=1, source_target_pairs={{0,16},{1,17},{2,18},{3,19},{4,20},{5,21},{6,22},{7,23},{8,24},{9,... | collective-permute-start | bytes 233480 | tf_op jit(solution)/shard_map/ppermute | solution.py:368
  52.5 2.4 %collective-permute-start.9 = (f32[144,128]{1,0:T(8,128)S(1)}, f32[144,128]{1,0:T(8,128)S(1)}, u32[]{:S(2)}, u32[]{:S(2)}) collective-permute-start(f32[144,128]{1,0:T(8,128)S(1)} %shard_map.93.refs_0_), channel_id=1, source_target_pairs={{0,16},{1,17},{2,18},{3,19},{4,20},{5,21},{6,22},{7,23},{8,24},{9,... | collective-permute-start | bytes 221192 | tf_op jit(solution)/shard_map/ppermute | solution.py:368
  54.9 3.4 %collective-permute-done.9.refs_1_ = f32[144,128]{1,0:T(8,128)S(1)} collective-permute-done((f32[144,128]{1,0:T(8,128)S(1)}, f32[144,128]{1,0:T(8,128)S(1)}, u32[]{:S(2)}, u32[]{:S(2)}) %collective-permute-start.9) | collective-permute-done | bytes 73760 | tf_op jit(solution)/shard_map/ppermute | solution.py:368
  65.4 2.3 %collective-permute-start.26 = (f32[96,384]{1,0:T(8,128)S(1)}, f32[96,384]{1,0:T(8,128)S(1)}, u32[]{:S(2)}, u32[]{:S(2)}) collective-permute-start(f32[96,384]{1,0:T(8,128)S(1)} %get-tuple-element.87.refs_2_.refs_4_), channel_id=1, source_target_pairs={{0,6},{1,7},{2,4},{3,5},{4,2},{5,3},{6,0},{7,1},{8,14},{9,15},{10,... | collective-permute-start | bytes 442376 | tf_op jit(solution)/shard_map/ppermute | solution.py:368
  67.8 2.2 %collective-permute-done.18.refs_6_ = f32[96,384]{1,0:T(8,128)S(1)} collective-permute-done((f32[96,384]{1,0:T(8,128)S(1)}, f32[96,384]{1,0:T(8,128)S(1)}, u32[]{:S(2)}, u32[]{:S(2)}) %collective-permute-start.18) | collective-permute-done | bytes 147488 | tf_op jit(solution)/shard_map/ppermute | solution.py:368
  74.1 4.1 %collective-permute-done.26.refs_14_ = f32[96,384]{1,0:T(8,128)S(1)} collective-permute-done((f32[96,384]{1,0:T(8,128)S(1)}, f32[96,384]{1,0:T(8,128)S(1)}, u32[]{:S(2)}, u32[]{:S(2)}) %collective-permute-start.26) | collective-permute-done | bytes 147488 | tf_op jit(solution)/shard_map/ppermute | solution.py:368
  80.2 3.9 %shard_map.100 = (bf16[4,1152,384]{2,1,0:T(8,128)(2,1)S(1)}, f32[8,384]{1,0:T(8,128)S(1)}) custom-call(s32[1,4]{1,0:T(1,128)S(1)} %copy-done.6, s32[1]{0:T(128)S(6)} %copy.9.refs_1_, f32[96,384]{1,0:T(8,128)S(1)} %get-tuple-element.87.refs_2_.refs_4_, f32[96,384]{1,0:T(8,128)S(1)} %collective-permute-done.15.refs_3_, ...), custom_call_target="tpu_custom_call" | custom-call | flops 1358954496 | bytes 4718592 | tf_op jit(solution)/shard_map/pallas_call | solution.py:182
  84.1 2.5 %shard_map.102 = (f32[1152,128]{1,0:T(8,128)S(1)}, f32[1152,128]{1,0:T(8,128)S(1)}, f32[8,128]{1,0:T(8,128)S(1)}) custom-call(s32[1,4]{1,0:T(1,128)S(1)} %copy-done.5, s32[1]{0:T(128)S(6)} %copy.9.refs_1_, f32[96,384]{1,0:T(8,128)S(1)} %get-tuple-element.87.refs_2_.refs_4_, f32[96,384]{1,0:T(8,128)S(1)} %collective-permute-done.15.refs_3_, ...), custom_call_target="tpu_custom_call" | custom-call | flops 679477248 | bytes 4718592 | tf_op jit(solution)/shard_map/pallas_call | solution.py:241
  86.6 3.1 %shard_map.107 = (f32[1160,128]{1,0:T(8,128)S(1)}, f32[1160,128]{1,0:T(8,128)S(1)}, f32[8,128]{1,0:T(8,128)}) custom-call(s32[1,4]{1,0:T(1,128)S(1)} %copy-done.5, s32[1]{0:T(128)S(6)} %copy.9.refs_1_, f32[96,384]{1,0:T(8,128)S(1)} %get-tuple-element.87.refs_2_.refs_4_, f32[96,384]{1,0:T(8,128)S(1)} %collective-permute-done.15.refs_3_, ...), custom_call_target="tpu_custom_call" | custom-call | flops 679477248 | bytes 4718592 | tf_op jit(solution)/shard_map/pallas_call | solution.py:241
  94.0 4.6 %collective-permute-done.36.recv_ref = f32[584,128]{1,0:T(8,128)S(1)} collective-permute-done((f32[584,128]{1,0:T(8,128)S(1)}, f32[584,128]{1,0:T(8,128)S(1)}, u32[]{:S(2)}, u32[]{:S(2)}) %collective-permute-start.36) | collective-permute-done | bytes 299040 | tf_op jit(solution)/shard_map/ppermute | solution.py:368
  98.7 3.0 %collective-permute-done.31.recv_ref = f32[576,128]{1,0:T(8,128)S(1)} collective-permute-done((f32[576,128]{1,0:T(8,128)S(1)}, f32[576,128]{1,0:T(8,128)S(1)}, u32[]{:S(2)}, u32[]{:S(2)}) %collective-permute-start.31) | collective-permute-done | bytes 294944 | tf_op jit(solution)/shard_map/ppermute | solution.py:368
  101.9 2.1 %collective-permute-done.37.recv_ref = f32[296,128]{1,0:T(8,128)S(1)} collective-permute-done((f32[296,128]{1,0:T(8,128)S(1)}, f32[296,128]{1,0:T(8,128)S(1)}, u32[]{:S(2)}, u32[]{:S(2)}) %collective-permute-start.37) | collective-permute-done | bytes 151584 | tf_op jit(solution)/shard_map/ppermute | solution.py:368
  108.5 2.3 %collective-permute-start.39 = (f32[152,128]{1,0:T(8,128)S(1)}, f32[152,128]{1,0:T(8,128)S(1)}, u32[]{:S(2)}, u32[]{:S(2)}) collective-permute-start(f32[152,128]{1,0:T(8,128)S(1)} %shard_map.111.refs_2_), channel_id=1, source_target_pairs={{0,16},{1,17},{2,18},{3,19},{4,20},{5,21},{6,22},{7,23},{8,24},{9,... | collective-permute-start | bytes 233480 | tf_op jit(solution)/shard_map/ppermute | solution.py:368
  113.4 3.7 %collective-permute-done.34.refs_1_ = f32[144,128]{1,0:T(8,128)S(1)} collective-permute-done((f32[144,128]{1,0:T(8,128)S(1)}, f32[144,128]{1,0:T(8,128)S(1)}, u32[]{:S(2)}, u32[]{:S(2)}) %collective-permute-start.34) | collective-permute-done | bytes 73760 | tf_op jit(solution)/shard_map/ppermute | solution.py:368
  123.6 2.7 %collective-permute-done.41.refs_2_ = f32[96,384]{1,0:T(8,128)S(1)} collective-permute-done((f32[96,384]{1,0:T(8,128)S(1)}, f32[96,384]{1,0:T(8,128)S(1)}, u32[]{:S(2)}, u32[]{:S(2)}) %collective-permute-start.41) | collective-permute-done | bytes 147488 | tf_op jit(solution)/shard_map/ppermute | solution.py:368
  (109 shorter events, 50.9 us)
Async XLA Ops:
  1.8 10.9 %collective-permute-start.1 = (f32[192,384]{1,0:T(8,128)S(1)}, f32[192,384]{1,0:T(8,128)S(1)}, u32[]{:S(2)}, u32[]{:S(2)}) collective-permute-start(f32[192,384]{1,0:T(8,128)S(1)} %get-tuple-element.111), channel_id=1, source_target_pairs={{0,2},{1,3},{2,0},{3,1},{4,6},{5,7},{6,4},{7,5},{8,10},{9,11},{10,... | collective-permute-start | bytes 884744 | tf_op jit(solution)/shard_map/ppermute | solution.py:368
  4.9 14.0 %collective-permute-start = (f32[384,384]{1,0:T(8,128)}, f32[384,384]{1,0:T(8,128)S(1)}, u32[]{:S(2)}, u32[]{:S(2)}) collective-permute-start(f32[384,384]{1,0:T(8,128)} %bitcast.7), channel_id=1, source_target_pairs={{0,1},{1,0},{2,3},{3,2},{4,5},{5,4},{6,7},{7,6},{8,9},{9,8},{10,11... | collective-permute-start | bytes 1769480 | tf_op jit(solution)/shard_map/ppermute | solution.py:368
  4.9 13.3 %collective-permute-start.3 = (f32[192,384]{1,0:T(8,128)S(1)}, f32[192,384]{1,0:T(8,128)S(1)}, u32[]{:S(2)}, u32[]{:S(2)}) collective-permute-start(f32[192,384]{1,0:T(8,128)S(1)} %get-tuple-element.110), channel_id=1, source_target_pairs={{0,2},{1,3},{2,0},{3,1},{4,6},{5,7},{6,4},{7,5},{8,10},{9,11},{10,... | collective-permute-start | bytes 884744 | tf_op jit(solution)/shard_map/ppermute | solution.py:368
  12.7 6.1 %collective-permute-start.2 = (f32[192,384]{1,0:T(8,128)S(1)}, f32[192,384]{1,0:T(8,128)S(1)}, u32[]{:S(2)}, u32[]{:S(2)}) collective-permute-start(f32[192,384]{1,0:T(8,128)S(1)} %collective-permute-done.1.refs_4_), channel_id=1, source_target_pairs={{0,1},{1,0},{2,3},{3,2},{4,5},{5,4},{6,7},{7,6},{8,9},{9,8},{10,11... | collective-permute-start | bytes 884744 | tf_op jit(solution)/shard_map/ppermute | solution.py:368
  32.4 6.8 %collective-permute-start.11 = (f32[584,128]{1,0:T(8,128)S(1)}, f32[584,128]{1,0:T(8,128)S(1)}, u32[]{:S(2)}, u32[]{:S(2)}) collective-permute-start(f32[584,128]{1,0:T(8,128)S(1)} %get-tuple-element.80), channel_id=1, source_target_pairs={{0,2},{1,9},{2,0},{3,11},{4,6},{5,13},{6,4},{7,15},{8,10},{9,1},{1... | collective-permute-start | bytes 897032 | tf_op jit(solution)/shard_map/ppermute | solution.py:368
  33.2 9.2 %collective-permute-start.6 = (f32[576,128]{1,0:T(8,128)S(1)}, f32[576,128]{1,0:T(8,128)S(1)}, u32[]{:S(2)}, u32[]{:S(2)}) collective-permute-start(f32[576,128]{1,0:T(8,128)S(1)} %get-tuple-element.71), channel_id=1, source_target_pairs={{0,2},{1,9},{2,0},{3,11},{4,6},{5,13},{6,4},{7,15},{8,10},{9,1},{1... | collective-permute-start | bytes 884744 | tf_op jit(solution)/shard_map/ppermute | solution.py:368
  39.3 5.7 %collective-permute-start.12 = (f32[296,128]{1,0:T(8,128)S(1)}, f32[296,128]{1,0:T(8,128)S(1)}, u32[]{:S(2)}, u32[]{:S(2)}) collective-permute-start(f32[296,128]{1,0:T(8,128)S(1)} %get-tuple-element.82), channel_id=1, source_target_pairs={{0,4},{1,5},{2,6},{3,7},{4,0},{5,1},{6,2},{7,3},{8,12},{9,13},{10,... | collective-permute-start | bytes 454664 | tf_op jit(solution)/shard_map/ppermute | solution.py:368
  49.9 8.4 %collective-permute-start.14 = (f32[152,128]{1,0:T(8,128)S(1)}, f32[152,128]{1,0:T(8,128)S(1)}, u32[]{:S(2)}, u32[]{:S(2)}) collective-permute-start(f32[152,128]{1,0:T(8,128)S(1)} %shard_map.98.refs_2_), channel_id=1, source_target_pairs={{0,16},{1,17},{2,18},{3,19},{4,20},{5,21},{6,22},{7,23},{8,24},{9,... | collective-permute-start | bytes 233480 | tf_op jit(solution)/shard_map/ppermute | solution.py:368
  52.5 5.8 %collective-permute-start.9 = (f32[144,128]{1,0:T(8,128)S(1)}, f32[144,128]{1,0:T(8,128)S(1)}, u32[]{:S(2)}, u32[]{:S(2)}) collective-permute-start(f32[144,128]{1,0:T(8,128)S(1)} %shard_map.93.refs_0_), channel_id=1, source_target_pairs={{0,16},{1,17},{2,18},{3,19},{4,20},{5,21},{6,22},{7,23},{8,24},{9,... | collective-permute-start | bytes 221192 | tf_op jit(solution)/shard_map/ppermute | solution.py:368
  58.5 7.0 %collective-permute-start.16 = (f32[96,384]{1,0:T(8,128)S(1)}, f32[96,384]{1,0:T(8,128)S(1)}, u32[]{:S(2)}, u32[]{:S(2)}) collective-permute-start(f32[96,384]{1,0:T(8,128)S(1)} %get-tuple-element.87.refs_2_.refs_4_), channel_id=1, source_target_pairs={{0,8},{1,9},{2,10},{3,11},{4,12},{5,13},{6,14},{7,15},{8,0},{9,1},... | collective-permute-start | bytes 442376 | tf_op jit(solution)/shard_map/ppermute | solution.py:368
  60.5 9.5 %collective-permute-start.18 = (f32[96,384]{1,0:T(8,128)S(1)}, f32[96,384]{1,0:T(8,128)S(1)}, u32[]{:S(2)}, u32[]{:S(2)}) collective-permute-start(f32[96,384]{1,0:T(8,128)S(1)} %get-tuple-element.87.refs_2_.refs_4_), channel_id=1, source_target_pairs={{0,4},{1,5},{2,6},{3,7},{4,0},{5,1},{6,2},{7,3},{8,12},{9,13},{10,... | collective-permute-start | bytes 442376 | tf_op jit(solution)/shard_map/ppermute | solution.py:368
  61.8 10.3 %collective-permute-start.20 = (f32[96,384]{1,0:T(8,128)S(1)}, f32[96,384]{1,0:T(8,128)S(1)}, u32[]{:S(2)}, u32[]{:S(2)}) collective-permute-start(f32[96,384]{1,0:T(8,128)S(1)} %get-tuple-element.87.refs_2_.refs_4_), channel_id=1, source_target_pairs={{0,12},{1,13},{2,14},{3,15},{4,8},{5,9},{6,10},{7,11},{8,4},{9,5},... | collective-permute-start | bytes 442376 | tf_op jit(solution)/shard_map/ppermute | solution.py:368
  62.0 10.0 %collective-permute-start.22 = (f32[96,384]{1,0:T(8,128)S(1)}, f32[96,384]{1,0:T(8,128)S(1)}, u32[]{:S(2)}, u32[]{:S(2)}) collective-permute-start(f32[96,384]{1,0:T(8,128)S(1)} %get-tuple-element.87.refs_2_.refs_4_), channel_id=1, source_target_pairs={{0,2},{1,3},{2,0},{3,1},{4,6},{5,7},{6,4},{7,5},{8,10},{9,11},{10,... | collective-permute-start | bytes 442376 | tf_op jit(solution)/shard_map/ppermute | solution.py:368
  63.4 10.7 %collective-permute-start.24 = (f32[96,384]{1,0:T(8,128)S(1)}, f32[96,384]{1,0:T(8,128)S(1)}, u32[]{:S(2)}, u32[]{:S(2)}) collective-permute-start(f32[96,384]{1,0:T(8,128)S(1)} %get-tuple-element.87.refs_2_.refs_4_), channel_id=1, source_target_pairs={{0,10},{1,11},{2,8},{3,9},{4,14},{5,15},{6,12},{7,13},{8,2},{9,3},... | collective-permute-start | bytes 442376 | tf_op jit(solution)/shard_map/ppermute | solution.py:368
  65.4 12.7 %collective-permute-start.26 = (f32[96,384]{1,0:T(8,128)S(1)}, f32[96,384]{1,0:T(8,128)S(1)}, u32[]{:S(2)}, u32[]{:S(2)}) collective-permute-start(f32[96,384]{1,0:T(8,128)S(1)} %get-tuple-element.87.refs_2_.refs_4_), channel_id=1, source_target_pairs={{0,6},{1,7},{2,4},{3,5},{4,2},{5,3},{6,0},{7,1},{8,14},{9,15},{10,... | collective-permute-start | bytes 442376 | tf_op jit(solution)/shard_map/ppermute | solution.py:368
  70.0 8.1 %collective-permute-start.28 = (f32[96,384]{1,0:T(8,128)S(1)}, f32[96,384]{1,0:T(8,128)S(1)}, u32[]{:S(2)}, u32[]{:S(2)}) collective-permute-start(f32[96,384]{1,0:T(8,128)S(1)} %get-tuple-element.87.refs_2_.refs_4_), channel_id=1, source_target_pairs={{0,14},{1,15},{2,12},{3,13},{4,10},{5,11},{6,8},{7,9},{8,6},{9,7},... | collective-permute-start | bytes 442376 | tf_op jit(solution)/shard_map/ppermute | solution.py:368
  72.1 6.6 %collective-permute-start.17 = (f32[96,384]{1,0:T(8,128)S(1)}, f32[96,384]{1,0:T(8,128)S(1)}, u32[]{:S(2)}, u32[]{:S(2)}) collective-permute-start(f32[96,384]{1,0:T(8,128)S(1)} %collective-permute-done.16.refs_4_), channel_id=1, source_target_pairs={{0,1},{1,0},{2,3},{3,2},{4,5},{5,4},{6,7},{7,6},{8,9},{9,8},{10,11... | collective-permute-start | bytes 442376 | tf_op jit(solution)/shard_map/ppermute | solution.py:368
  72.1 6.6 %collective-permute-start.19 = (f32[96,384]{1,0:T(8,128)S(1)}, f32[96,384]{1,0:T(8,128)S(1)}, u32[]{:S(2)}, u32[]{:S(2)}) collective-permute-start(f32[96,384]{1,0:T(8,128)S(1)} %collective-permute-done.18.refs_6_), channel_id=1, source_target_pairs={{0,1},{1,0},{2,3},{3,2},{4,5},{5,4},{6,7},{7,6},{8,9},{9,8},{10,11... | collective-permute-start | bytes 442376 | tf_op jit(solution)/shard_map/ppermute | solution.py:368
  91.8 6.8 %collective-permute-start.36 = (f32[584,128]{1,0:T(8,128)S(1)}, f32[584,128]{1,0:T(8,128)S(1)}, u32[]{:S(2)}, u32[]{:S(2)}) collective-permute-start(f32[584,128]{1,0:T(8,128)S(1)} %get-tuple-element.103), channel_id=1, source_target_pairs={{0,2},{1,9},{2,0},{3,11},{4,6},{5,13},{6,4},{7,15},{8,10},{9,1},{1... | collective-permute-start | bytes 897032 | tf_op jit(solution)/shard_map/ppermute | solution.py:368
  92.6 9.2 %collective-permute-start.31 = (f32[576,128]{1,0:T(8,128)S(1)}, f32[576,128]{1,0:T(8,128)S(1)}, u32[]{:S(2)}, u32[]{:S(2)}) collective-permute-start(f32[576,128]{1,0:T(8,128)S(1)} %get-tuple-element.94), channel_id=1, source_target_pairs={{0,2},{1,9},{2,0},{3,11},{4,6},{5,13},{6,4},{7,15},{8,10},{9,1},{1... | collective-permute-start | bytes 884744 | tf_op jit(solution)/shard_map/ppermute | solution.py:368
  108.5 8.6 %collective-permute-start.39 = (f32[152,128]{1,0:T(8,128)S(1)}, f32[152,128]{1,0:T(8,128)S(1)}, u32[]{:S(2)}, u32[]{:S(2)}) collective-permute-start(f32[152,128]{1,0:T(8,128)S(1)} %shard_map.111.refs_2_), channel_id=1, source_target_pairs={{0,16},{1,17},{2,18},{3,19},{4,20},{5,21},{6,22},{7,23},{8,24},{9,... | collective-permute-start | bytes 233480 | tf_op jit(solution)/shard_map/ppermute | solution.py:368
  117.2 6.4 %collective-permute-start.40 = (f32[96,384]{1,0:T(8,128)S(1)}, f32[96,384]{1,0:T(8,128)S(1)}, u32[]{:S(2)}, u32[]{:S(2)}) collective-permute-start(f32[96,384]{1,0:T(8,128)S(1)} %get-tuple-element.108.refs_0_), channel_id=1, source_target_pairs={{0,8},{1,9},{2,10},{3,11},{4,12},{5,13},{6,14},{7,15},{8,0},{9,1},... | collective-permute-start | bytes 442376 | tf_op jit(solution)/shard_map/ppermute | solution.py:368
  118.6 7.7 %collective-permute-start.41 = (f32[96,384]{1,0:T(8,128)S(1)}, f32[96,384]{1,0:T(8,128)S(1)}, u32[]{:S(2)}, u32[]{:S(2)}) collective-permute-start(f32[96,384]{1,0:T(8,128)S(1)} %get-tuple-element.108.refs_0_), channel_id=1, source_target_pairs={{0,4},{1,5},{2,6},{3,7},{4,0},{5,1},{6,2},{7,3},{8,12},{9,13},{10,... | collective-permute-start | bytes 442376 | tf_op jit(solution)/shard_map/ppermute | solution.py:368
  119.6 6.7 %collective-permute-start.42 = (f32[96,384]{1,0:T(8,128)S(1)}, f32[96,384]{1,0:T(8,128)S(1)}, u32[]{:S(2)}, u32[]{:S(2)}) collective-permute-start(f32[96,384]{1,0:T(8,128)S(1)} %get-tuple-element.108.refs_0_), channel_id=1, source_target_pairs={{0,12},{1,13},{2,14},{3,15},{4,8},{5,9},{6,10},{7,11},{8,4},{9,5},... | collective-permute-start | bytes 442376 | tf_op jit(solution)/shard_map/ppermute | solution.py:368
  (26 other events, 114.3 us)

commit v3 on v2

--- a/solution.py
+++ b/solution.py
@@ -249,38 +249,42 @@
     )(pair_out, pair_count, *pieces, *ops, inv, before)
 
 
-def combine_kernel(keep_ref, recv_ref, next_ref, send_ref=None):
-    extra = 0 if send_ref is None else 2 * next_ref.shape[0] - keep_ref.shape[0]
-    rows = next_ref.shape[0] - extra
-    next_ref[:rows, :] = keep_ref[:rows, :] + recv_ref[:rows, :]
-    if send_ref is None:
-        return
-    send_ref[:rows, :] = keep_ref[rows:2 * rows, :] + recv_ref[rows:2 * rows, :]
-    if extra:
-        total = keep_ref[2 * rows:, :] + recv_ref[2 * rows:, :]
-        next_ref[rows:, :] = total
-        send_ref[rows:, :] = total
-
-
-def combine(keep, recv, extra):
-    shape = jax.ShapeDtypeStruct(((keep.shape[0] - extra) // 2 + extra, TILE[1]), F32)
-    return pl.pallas_call(
-        combine_kernel,
+def cut_kernel(extra, keep_ref, recv_ref, *slots):
+    rows = slots[0].shape[0] - extra
+    end = len(slots) * rows
+    for k, slot in enumerate(slots):
+        slot[:rows, :] = keep_ref[k * rows:(k + 1) * rows, :] + recv_ref[k * rows:(k + 1) * rows, :]
+        if extra:
+            slot[rows:, :] = keep_ref[end:, :] + recv_ref[end:, :]
+
+
+def cut(keep, recv, extra, ways):
+    shape = jax.ShapeDtypeStruct(((recv.shape[0] - extra) // ways + extra, TILE[1]), F32)
+    return pl.pallas_call(
+        functools.partial(cut_kernel, extra),
         in_specs=[VMEM] * 2,
-        out_specs=[VMEM] * 2,
-        out_shape=[shape] * 2,
+        out_specs=[VMEM] * ways,
+        out_shape=[shape] * ways,
         compiler_params=grant(4),
     )(keep, recv)
 
 
-def total(mine, recv):
-    return pl.pallas_call(
-        combine_kernel,
-        in_specs=[VMEM] * 2,
+def sum_kernel(*refs):
+    *parts, out_ref = refs
+    total = parts[0][...]
+    for part in parts[1:]:
+        total += part[...]
+    out_ref[...] = total
+
+
+def sum_of(parts):
+    return pl.pallas_call(
+        sum_kernel,
+        in_specs=[VMEM] * len(parts),
         out_specs=VMEM,
-        out_shape=jax.ShapeDtypeStruct(mine.shape, F32),
+        out_shape=jax.ShapeDtypeStruct(parts[0].shape, F32),
         compiler_params=grant(4),
-    )(mine, recv)
+    )(*parts)
 
 
 def update_kernel(*refs):
@@ -401,14 +405,22 @@
             send, keep, rho = outer(first, h, cells, sectors, pair_out, pair_count, pieces, (left, cat), inv, rho)
             keeps.append(keep)
             recvs.append(swap(send, [CORE]))
-        for step in zip(*ORDERS):
+        first_dims, second, third = ([[DIMS[dim]] for dim in step] for step in zip(*ORDERS))
+        for h in range(CHUNKS):
+            extra = TILE[0] if h == CHUNKS - 1 else 0
+            keeps[h], send = cut(keeps[h], recvs[h], extra, 2)
+            recvs[h] = swap(send, *first_dims)
+        both = [a + b for a, b in zip(second, third)]
+        for h in range(CHUNKS):
+            extra = TILE[0] if h == CHUNKS - 1 else 0
+            slots = cut(keeps[h], recvs[h], extra, 4)
+            parts = [slots[0]]
+            for k, dims in ((3, both), (2, second), (1, third)):
+                parts.append(swap(slots[k], *dims))
+            keeps[h] = parts
+        for number, step in enumerate(rest):
             for h in range(CHUNKS):
-                extra = TILE[0] if h == CHUNKS - 1 else 0
-                keeps[h], send = combine(keeps[h], recvs[h], extra)
-                recvs[h] = swap(send, [DIMS[step[0]]], [DIMS[step[1]]])
-        for step in rest:
-            for h in range(CHUNKS):
-                keeps[h] = total(keeps[h], recvs[h])
+                keeps[h] = sum_of([keeps[h], recvs[h]] if number else keeps[h])
                 recvs[h] = swap(keeps[h], [step])
         sums = [x for pair in zip(keeps, recvs) for x in pair]
         vec, energy = update(sums, vec, inv, diag)

time: 127 us -> 123 us (0.969)
  waiting for transfers between devices: 53.6 us -> 41.4 us
  starting transfers between devices: 39.2 us -> 46.9 us
    ppermute x43 -> x47, waiting for transfers between devices: 53.6 us -> 41.4 us  [swap(): lax.ppermute(x, AXES, flips(mesh_shape, even, even if odd is None else odd))]
    ppermute x43 -> x47, starting transfers between devices: 39.2 us -> 46.9 us  [swap(): lax.ppermute(x, AXES, flips(mesh_shape, even, even if odd is None else odd))]
  transfers between devices with their start and end apart: 43 -> 47, of which waited for: 27 -> 24; matrix products, arithmetic and copies ran while one was open for 2% -> 2% of each run, Pallas kernels for 3% -> 4%
where the time goes in v3:
time: 123 us
  starting transfers between devices  46.9 us (38%)
  waiting for transfers between devices  41.4 us (34%)
  Pallas kernels  23.3 us (19%)
  local copies, waits for them, and re-layouts  7.67 us (6%)
  other arithmetic  1.85 us (2%)
  between operations  1.51 us (1%)
    ppermute x47, starting transfers between devices, swap(): lax.ppermute(x, AXES, flips(mesh_shape, even, even if odd is None else odd))  46.9 us
    ppermute x47, waiting for transfers between devices, swap(): lax.ppermute(x, AXES, flips(mesh_shape, even, even if odd is None else odd))  41.4 us
    pallas_call x4, Pallas kernels, outer(): pl.pallas_call(functools.partial(outer_kernel, first, chunk, cells, len(p...  11.1 us
    pallas_call x3, Pallas kernels, inner(): pl.pallas_call(functools.partial(inner_kernel, first, half, cells, len(pi...  9.73 us
    unnamed x14, local copies, waits for them, and re-layouts  5.47 us
  transfers between devices with their start and end apart: 47, of which 24 were waited for; matrix products, arithmetic and copies ran while one was open for 2% of the time, Pallas kernels for 4%

profile of v3, /device:TPU:0, one launch (start us, length us, event | category | flops | bytes accessed | tf_op | source)
XLA Modules:
  0.0 122.7 jit_solution(1378792023123017363)
XLA Ops:
  1.8 3.1 %collective-permute-start.1 = (f32[192,384]{1,0:T(8,128)S(1)}, f32[192,384]{1,0:T(8,128)S(1)}, u32[]{:S(2)}, u32[]{:S(2)}) collective-permute-start(f32[192,384]{1,0:T(8,128)S(1)} %get-tuple-element.111), channel_id=1, source_target_pairs={{0,2},{1,3},{2,0},{3,1},{4,6},{5,7},{6,4},{7,5},{8,10},{9,11},{10,... | collective-permute-start | bytes 884744 | tf_op jit(solution)/shard_map/ppermute | solution.py:372
  12.7 5.5 %collective-permute-done.3.refs_4_.refs_6_ = f32[192,384]{1,0:T(8,128)S(1)} collective-permute-done((f32[192,384]{1,0:T(8,128)S(1)}, f32[192,384]{1,0:T(8,128)S(1)}, u32[]{:S(2)}, u32[]{:S(2)}) %collective-permute-start.3) | collective-permute-done | bytes 294944 | tf_op jit(solution)/shard_map/ppermute | solution.py:372
  18.9 2.9 %shard_map.87 = (bf16[4,192,384]{2,1,0:T(8,128)(2,1)S(1)}, bf16[4,192,384]{2,1,0:T(8,128)(2,1)S(1)}, f32[8,384]{1,0:T(8,128)S(1)}) custom-call(s32[1,4]{1,0:T(1,128)S(1)} %copy-done.6, s32[1]{0:T(128)S(6)} %copy.9.refs_1_, f32[384,384]{1,0:T(8,128)S(1)} %bitcast.8, f32[384,384]{1,0:T(8,128)S(1)} %collective-permute-done.refs_3_, ...), custom_call_target="tpu_custom_call" | custom-call | flops 679477248 | bytes 4718592 | tf_op jit(solution)/shard_map/pallas_call | solution.py:182
  21.8 3.0 %shard_map.88 = (bf16[4,1152,384]{2,1,0:T(8,128)(2,1)S(1)}, f32[8,384]{1,0:T(8,128)S(1)}) custom-call(s32[1,4]{1,0:T(1,128)S(1)} %copy-done.6, s32[1]{0:T(128)S(6)} %copy.9.refs_1_, f32[384,384]{1,0:T(8,128)S(1)} %bitcast.9, f32[384,384]{1,0:T(8,128)S(1)} %collective-permute-done.refs_3_, f32[192,384]{1,0:T(8,128)S(1)} %collective-permute-done.3.refs_4_.refs_6_, ...), custom_call_target="tpu_custom_call" | custom-call | flops 679477248 | bytes 4718592 | tf_op jit(solution)/shard_map/pallas_call | solution.py:182
  24.8 2.5 %shard_map.89 = (f32[1152,128]{1,0:T(8,128)S(1)}, f32[1152,128]{1,0:T(8,128)S(1)}, f32[8,128]{1,0:T(8,128)S(1)}) custom-call(s32[1,4]{1,0:T(1,128)S(1)} %copy-done.5, s32[1]{0:T(128)S(6)} %copy.9.refs_1_, f32[384,384]{1,0:T(8,128)S(1)} %bitcast.10, f32[384,384]{1,0:T(8,128)S(1)} %collective-permute-done.refs_3_, ...), custom_call_target="tpu_custom_call" | custom-call | flops 679477248 | bytes 4718592 | tf_op jit(solution)/shard_map/pallas_call | solution.py:241
  27.3 3.1 %shard_map.93 = (f32[1160,128]{1,0:T(8,128)S(1)}, f32[1160,128]{1,0:T(8,128)S(1)}, f32[8,128]{1,0:T(8,128)}) custom-call(s32[1,4]{1,0:T(1,128)S(1)} %copy-done.5, s32[1]{0:T(128)S(6)} %copy.9.refs_1_, f32[384,384]{1,0:T(8,128)S(1)} %bitcast.11, f32[384,384]{1,0:T(8,128)S(1)} %collective-permute-done.refs_3_, f32[192,384]{1,0:T(8,128)S(1)} %collective-permute-done.1.refs_4_, ...), custom_call_target="tpu_custom_call" | custom-call | flops 679477248 | bytes 4718592 | tf_op jit(solution)/shard_map/pallas_call | solution.py:241
  34.6 4.6 %collective-permute-done.12.recv_ref = f32[584,128]{1,0:T(8,128)S(1)} collective-permute-done((f32[584,128]{1,0:T(8,128)S(1)}, f32[584,128]{1,0:T(8,128)S(1)}, u32[]{:S(2)}, u32[]{:S(2)}) %collective-permute-start.12) | collective-permute-done | bytes 299040 | tf_op jit(solution)/shard_map/ppermute | solution.py:372
  39.3 2.9 %collective-permute-start.13 = (f32[152,128]{1,0:T(8,128)S(1)}, f32[152,128]{1,0:T(8,128)S(1)}, u32[]{:S(2)}, u32[]{:S(2)}) collective-permute-start(f32[152,128]{1,0:T(8,128)S(1)} %get-tuple-element.82), channel_id=1, source_target_pairs={{0,12},{1,7},{2,14},{3,5},{4,8},{5,3},{6,10},{7,1},{8,4},{9,15},{1... | collective-permute-start | bytes 233480 | tf_op jit(solution)/shard_map/ppermute | solution.py:372
  42.9 2.9 %collective-permute-start.7 = (f32[144,128]{1,0:T(8,128)S(1)}, f32[144,128]{1,0:T(8,128)S(1)}, u32[]{:S(2)}, u32[]{:S(2)}) collective-permute-start(f32[144,128]{1,0:T(8,128)S(1)} %get-tuple-element.73), channel_id=1, source_target_pairs={{0,12},{1,7},{2,14},{3,5},{4,8},{5,3},{6,10},{7,1},{8,4},{9,15},{1... | collective-permute-start | bytes 221192 | tf_op jit(solution)/shard_map/ppermute | solution.py:372
  47.5 2.5 %collective-permute-start.16 = (f32[152,128]{1,0:T(8,128)S(1)}, f32[152,128]{1,0:T(8,128)S(1)}, u32[]{:S(2)}, u32[]{:S(2)}) collective-permute-start(f32[152,128]{1,0:T(8,128)S(1)} %shard_map.96.refs_2_), channel_id=1, source_target_pairs={{0,16},{1,17},{2,18},{3,19},{4,20},{5,21},{6,22},{7,23},{8,24},{9,... | collective-permute-start | bytes 233480 | tf_op jit(solution)/shard_map/ppermute | solution.py:372
  50.7 3.5 %collective-permute-start.10 = (f32[144,128]{1,0:T(8,128)S(1)}, f32[144,128]{1,0:T(8,128)S(1)}, u32[]{:S(2)}, u32[]{:S(2)}) collective-permute-start(f32[144,128]{1,0:T(8,128)S(1)} %shard_map.92.refs_0_), channel_id=1, source_target_pairs={{0,16},{1,17},{2,18},{3,19},{4,20},{5,21},{6,22},{7,23},{8,24},{9,... | collective-permute-start | bytes 221192 | tf_op jit(solution)/shard_map/ppermute | solution.py:372
  54.3 3.0 %collective-permute-done.10.refs_1_ = f32[144,128]{1,0:T(8,128)S(1)} collective-permute-done((f32[144,128]{1,0:T(8,128)S(1)}, f32[144,128]{1,0:T(8,128)S(1)}, u32[]{:S(2)}, u32[]{:S(2)}) %collective-permute-start.10) | collective-permute-done | bytes 73760 | tf_op jit(solution)/shard_map/ppermute | solution.py:372
  58.8 2.2 %collective-permute-start.22 = (f32[96,384]{1,0:T(8,128)S(1)}, f32[96,384]{1,0:T(8,128)S(1)}, u32[]{:S(2)}, u32[]{:S(2)}) collective-permute-start(f32[96,384]{1,0:T(8,128)S(1)} %get-tuple-element.87.refs_2_.refs_4_), channel_id=1, source_target_pairs={{0,12},{1,13},{2,14},{3,15},{4,8},{5,9},{6,10},{7,11},{8,4},{9,5},... | collective-permute-start | bytes 442376 | tf_op jit(solution)/shard_map/ppermute | solution.py:372
  64.9 4.5 %collective-permute-start.30 = (f32[96,384]{1,0:T(8,128)S(1)}, f32[96,384]{1,0:T(8,128)S(1)}, u32[]{:S(2)}, u32[]{:S(2)}) collective-permute-start(f32[96,384]{1,0:T(8,128)S(1)} %get-tuple-element.87.refs_2_.refs_4_), channel_id=1, source_target_pairs={{0,14},{1,15},{2,12},{3,13},{4,10},{5,11},{6,8},{7,9},{8,6},{9,7},... | collective-permute-start | bytes 442376 | tf_op jit(solution)/shard_map/ppermute | solution.py:372
  70.0 4.0 %collective-permute-done.26.refs_12_ = f32[96,384]{1,0:T(8,128)S(1)} collective-permute-done((f32[96,384]{1,0:T(8,128)S(1)}, f32[96,384]{1,0:T(8,128)S(1)}, u32[]{:S(2)}, u32[]{:S(2)}) %collective-permute-start.26) | collective-permute-done | bytes 147488 | tf_op jit(solution)/shard_map/ppermute | solution.py:372
  73.9 2.9 %collective-permute-done.28.refs_14_ = f32[96,384]{1,0:T(8,128)S(1)} collective-permute-done((f32[96,384]{1,0:T(8,128)S(1)}, f32[96,384]{1,0:T(8,128)S(1)}, u32[]{:S(2)}, u32[]{:S(2)}) %collective-permute-start.28) | collective-permute-done | bytes 147488 | tf_op jit(solution)/shard_map/ppermute | solution.py:372
  78.9 3.9 %shard_map.98 = (bf16[4,1152,384]{2,1,0:T(8,128)(2,1)S(1)}, f32[8,384]{1,0:T(8,128)S(1)}) custom-call(s32[1,4]{1,0:T(1,128)S(1)} %copy-done.6, s32[1]{0:T(128)S(6)} %copy.9.refs_1_, f32[96,384]{1,0:T(8,128)S(1)} %get-tuple-element.87.refs_2_.refs_4_, f32[96,384]{1,0:T(8,128)S(1)} %collective-permute-done.17.refs_3_, ...), custom_call_target="tpu_custom_call" | custom-call | flops 1358954496 | bytes 4718592 | tf_op jit(solution)/shard_map/pallas_call | solution.py:182
  82.8 2.5 %shard_map.100 = (f32[1152,128]{1,0:T(8,128)S(1)}, f32[1152,128]{1,0:T(8,128)S(1)}, f32[8,128]{1,0:T(8,128)S(1)}) custom-call(s32[1,4]{1,0:T(1,128)S(1)} %copy-done.5, s32[1]{0:T(128)S(6)} %copy.9.refs_1_, f32[96,384]{1,0:T(8,128)S(1)} %get-tuple-element.87.refs_2_.refs_4_, f32[96,384]{1,0:T(8,128)S(1)} %collective-permute-done.17.refs_3_, ...), custom_call_target="tpu_custom_call" | custom-call | flops 679477248 | bytes 4718592 | tf_op jit(solution)/shard_map/pallas_call | solution.py:241
  85.3 3.1 %shard_map.104 = (f32[1160,128]{1,0:T(8,128)S(1)}, f32[1160,128]{1,0:T(8,128)S(1)}, f32[8,128]{1,0:T(8,128)}) custom-call(s32[1,4]{1,0:T(1,128)S(1)} %copy-done.5, s32[1]{0:T(128)S(6)} %copy.9.refs_1_, f32[96,384]{1,0:T(8,128)S(1)} %get-tuple-element.87.refs_2_.refs_4_, f32[96,384]{1,0:T(8,128)S(1)} %collective-permute-done.17.refs_3_, ...), custom_call_target="tpu_custom_call" | custom-call | flops 679477248 | bytes 4718592 | tf_op jit(solution)/shard_map/pallas_call | solution.py:241
  92.7 4.6 %collective-permute-done.39.recv_ref = f32[584,128]{1,0:T(8,128)S(1)} collective-permute-done((f32[584,128]{1,0:T(8,128)S(1)}, f32[584,128]{1,0:T(8,128)S(1)}, u32[]{:S(2)}, u32[]{:S(2)}) %collective-permute-start.39) | collective-permute-done | bytes 299040 | tf_op jit(solution)/shard_map/ppermute | solution.py:372
  103.2 1.9 %collective-permute-start.36 = (f32[144,128]{1,0:T(8,128)S(1)}, f32[144,128]{1,0:T(8,128)S(1)}, u32[]{:S(2)}, u32[]{:S(2)}) collective-permute-start(f32[144,128]{1,0:T(8,128)S(1)} %get-tuple-element.98), channel_id=1, source_target_pairs={{0,8},{1,3},{2,10},{3,1},{4,12},{5,7},{6,14},{7,5},{8,0},{9,11},{1... | collective-permute-start | bytes 221192 | tf_op jit(solution)/shard_map/ppermute | solution.py:372
  107.7 2.0 %collective-permute-start.37 = (f32[144,128]{1,0:T(8,128)S(1)}, f32[144,128]{1,0:T(8,128)S(1)}, u32[]{:S(2)}, u32[]{:S(2)}) collective-permute-start(f32[144,128]{1,0:T(8,128)S(1)} %shard_map.103.refs_0_), channel_id=1, source_target_pairs={{0,16},{1,17},{2,18},{3,19},{4,20},{5,21},{6,22},{7,23},{8,24},{9,... | collective-permute-start | bytes 221192 | tf_op jit(solution)/shard_map/ppermute | solution.py:372
  109.6 3.3 %collective-permute-done.37.refs_1_ = f32[144,128]{1,0:T(8,128)S(1)} collective-permute-done((f32[144,128]{1,0:T(8,128)S(1)}, f32[144,128]{1,0:T(8,128)S(1)}, u32[]{:S(2)}, u32[]{:S(2)}) %collective-permute-start.37) | collective-permute-done | bytes 73760 | tf_op jit(solution)/shard_map/ppermute | solution.py:372
  118.1 1.8 %pad_maximum_fusion = f32[2]{0:T(128)} fusion(f32[1]{0:T(128)} %bitcast.4, f32[1]{0:T(128)} %bitcast.3), kind=kLoop, calls=%fused_computation.2 | loop fusion | flops 2 | bytes 16 | tf_op jit(solution)/shard_map/stack | solution.py:438
  (113 shorter events, 45.2 us)
Async XLA Ops:
  1.8 10.9 %collective-permute-start.1 = (f32[192,384]{1,0:T(8,128)S(1)}, f32[192,384]{1,0:T(8,128)S(1)}, u32[]{:S(2)}, u32[]{:S(2)}) collective-permute-start(f32[192,384]{1,0:T(8,128)S(1)} %get-tuple-element.111), channel_id=1, source_target_pairs={{0,2},{1,3},{2,0},{3,1},{4,6},{5,7},{6,4},{7,5},{8,10},{9,11},{10,... | collective-permute-start | bytes 884744 | tf_op jit(solution)/shard_map/ppermute | solution.py:372
  4.9 14.0 %collective-permute-start = (f32[384,384]{1,0:T(8,128)}, f32[384,384]{1,0:T(8,128)S(1)}, u32[]{:S(2)}, u32[]{:S(2)}) collective-permute-start(f32[384,384]{1,0:T(8,128)} %bitcast.7), channel_id=1, source_target_pairs={{0,1},{1,0},{2,3},{3,2},{4,5},{5,4},{6,7},{7,6},{8,9},{9,8},{10,11... | collective-permute-start | bytes 1769480 | tf_op jit(solution)/shard_map/ppermute | solution.py:372
  4.9 13.3 %collective-permute-start.3 = (f32[192,384]{1,0:T(8,128)S(1)}, f32[192,384]{1,0:T(8,128)S(1)}, u32[]{:S(2)}, u32[]{:S(2)}) collective-permute-start(f32[192,384]{1,0:T(8,128)S(1)} %get-tuple-element.110), channel_id=1, source_target_pairs={{0,2},{1,3},{2,0},{3,1},{4,6},{5,7},{6,4},{7,5},{8,10},{9,11},{10,... | collective-permute-start | bytes 884744 | tf_op jit(solution)/shard_map/ppermute | solution.py:372
  32.4 6.8 %collective-permute-start.12 = (f32[584,128]{1,0:T(8,128)S(1)}, f32[584,128]{1,0:T(8,128)S(1)}, u32[]{:S(2)}, u32[]{:S(2)}) collective-permute-start(f32[584,128]{1,0:T(8,128)S(1)} %get-tuple-element.80), channel_id=1, source_target_pairs={{0,2},{1,9},{2,0},{3,11},{4,6},{5,13},{6,4},{7,15},{8,10},{9,1},{1... | collective-permute-start | bytes 897032 | tf_op jit(solution)/shard_map/ppermute | solution.py:372
  33.2 9.6 %collective-permute-start.6 = (f32[576,128]{1,0:T(8,128)S(1)}, f32[576,128]{1,0:T(8,128)S(1)}, u32[]{:S(2)}, u32[]{:S(2)}) collective-permute-start(f32[576,128]{1,0:T(8,128)S(1)} %get-tuple-element.71), channel_id=1, source_target_pairs={{0,2},{1,9},{2,0},{3,11},{4,6},{5,13},{6,4},{7,15},{8,10},{9,1},{1... | collective-permute-start | bytes 884744 | tf_op jit(solution)/shard_map/ppermute | solution.py:372
  39.3 7.1 %collective-permute-start.13 = (f32[152,128]{1,0:T(8,128)S(1)}, f32[152,128]{1,0:T(8,128)S(1)}, u32[]{:S(2)}, u32[]{:S(2)}) collective-permute-start(f32[152,128]{1,0:T(8,128)S(1)} %get-tuple-element.82), channel_id=1, source_target_pairs={{0,12},{1,7},{2,14},{3,5},{4,8},{5,3},{6,10},{7,1},{8,4},{9,15},{1... | collective-permute-start | bytes 233480 | tf_op jit(solution)/shard_map/ppermute | solution.py:372
  42.9 7.1 %collective-permute-start.7 = (f32[144,128]{1,0:T(8,128)S(1)}, f32[144,128]{1,0:T(8,128)S(1)}, u32[]{:S(2)}, u32[]{:S(2)}) collective-permute-start(f32[144,128]{1,0:T(8,128)S(1)} %get-tuple-element.73), channel_id=1, source_target_pairs={{0,12},{1,7},{2,14},{3,5},{4,8},{5,3},{6,10},{7,1},{8,4},{9,15},{1... | collective-permute-start | bytes 221192 | tf_op jit(solution)/shard_map/ppermute | solution.py:372
  47.5 9.8 %collective-permute-start.16 = (f32[152,128]{1,0:T(8,128)S(1)}, f32[152,128]{1,0:T(8,128)S(1)}, u32[]{:S(2)}, u32[]{:S(2)}) collective-permute-start(f32[152,128]{1,0:T(8,128)S(1)} %shard_map.96.refs_2_), channel_id=1, source_target_pairs={{0,16},{1,17},{2,18},{3,19},{4,20},{5,21},{6,22},{7,23},{8,24},{9,... | collective-permute-start | bytes 233480 | tf_op jit(solution)/shard_map/ppermute | solution.py:372
  50.7 6.5 %collective-permute-start.10 = (f32[144,128]{1,0:T(8,128)S(1)}, f32[144,128]{1,0:T(8,128)S(1)}, u32[]{:S(2)}, u32[]{:S(2)}) collective-permute-start(f32[144,128]{1,0:T(8,128)S(1)} %shard_map.92.refs_0_), channel_id=1, source_target_pairs={{0,16},{1,17},{2,18},{3,19},{4,20},{5,21},{6,22},{7,23},{8,24},{9,... | collective-permute-start | bytes 221192 | tf_op jit(solution)/shard_map/ppermute | solution.py:372
  57.4 6.8 %collective-permute-start.18 = (f32[96,384]{1,0:T(8,128)S(1)}, f32[96,384]{1,0:T(8,128)S(1)}, u32[]{:S(2)}, u32[]{:S(2)}) collective-permute-start(f32[96,384]{1,0:T(8,128)S(1)} %get-tuple-element.87.refs_2_.refs_4_), channel_id=1, source_target_pairs={{0,8},{1,9},{2,10},{3,11},{4,12},{5,13},{6,14},{7,15},{8,0},{9,1},... | collective-permute-start | bytes 442376 | tf_op jit(solution)/shard_map/ppermute | solution.py:372
  57.5 7.4 %collective-permute-start.20 = (f32[96,384]{1,0:T(8,128)S(1)}, f32[96,384]{1,0:T(8,128)S(1)}, u32[]{:S(2)}, u32[]{:S(2)}) collective-permute-start(f32[96,384]{1,0:T(8,128)S(1)} %get-tuple-element.87.refs_2_.refs_4_), channel_id=1, source_target_pairs={{0,4},{1,5},{2,6},{3,7},{4,0},{5,1},{6,2},{7,3},{8,12},{9,13},{10,... | collective-permute-start | bytes 442376 | tf_op jit(solution)/shard_map/ppermute | solution.py:372
  58.8 10.7 %collective-permute-start.22 = (f32[96,384]{1,0:T(8,128)S(1)}, f32[96,384]{1,0:T(8,128)S(1)}, u32[]{:S(2)}, u32[]{:S(2)}) collective-permute-start(f32[96,384]{1,0:T(8,128)S(1)} %get-tuple-element.87.refs_2_.refs_4_), channel_id=1, source_target_pairs={{0,12},{1,13},{2,14},{3,15},{4,8},{5,9},{6,10},{7,11},{8,4},{9,5},... | collective-permute-start | bytes 442376 | tf_op jit(solution)/shard_map/ppermute | solution.py:372
  61.0 8.5 %collective-permute-start.24 = (f32[96,384]{1,0:T(8,128)S(1)}, f32[96,384]{1,0:T(8,128)S(1)}, u32[]{:S(2)}, u32[]{:S(2)}) collective-permute-start(f32[96,384]{1,0:T(8,128)S(1)} %get-tuple-element.87.refs_2_.refs_4_), channel_id=1, source_target_pairs={{0,2},{1,3},{2,0},{3,1},{4,6},{5,7},{6,4},{7,5},{8,10},{9,11},{10,... | collective-permute-start | bytes 442376 | tf_op jit(solution)/shard_map/ppermute | solution.py:372
  62.6 11.3 %collective-permute-start.26 = (f32[96,384]{1,0:T(8,128)S(1)}, f32[96,384]{1,0:T(8,128)S(1)}, u32[]{:S(2)}, u32[]{:S(2)}) collective-permute-start(f32[96,384]{1,0:T(8,128)S(1)} %get-tuple-element.87.refs_2_.refs_4_), channel_id=1, source_target_pairs={{0,10},{1,11},{2,8},{3,9},{4,14},{5,15},{6,12},{7,13},{8,2},{9,3},... | collective-permute-start | bytes 442376 | tf_op jit(solution)/shard_map/ppermute | solution.py:372
  64.2 12.6 %collective-permute-start.28 = (f32[96,384]{1,0:T(8,128)S(1)}, f32[96,384]{1,0:T(8,128)S(1)}, u32[]{:S(2)}, u32[]{:S(2)}) collective-permute-start(f32[96,384]{1,0:T(8,128)S(1)} %get-tuple-element.87.refs_2_.refs_4_), channel_id=1, source_target_pairs={{0,6},{1,7},{2,4},{3,5},{4,2},{5,3},{6,0},{7,1},{8,14},{9,15},{10,... | collective-permute-start | bytes 442376 | tf_op jit(solution)/shard_map/ppermute | solution.py:372
  64.9 11.9 %collective-permute-start.30 = (f32[96,384]{1,0:T(8,128)S(1)}, f32[96,384]{1,0:T(8,128)S(1)}, u32[]{:S(2)}, u32[]{:S(2)}) collective-permute-start(f32[96,384]{1,0:T(8,128)S(1)} %get-tuple-element.87.refs_2_.refs_4_), channel_id=1, source_target_pairs={{0,14},{1,15},{2,12},{3,13},{4,10},{5,11},{6,8},{7,9},{8,6},{9,7},... | collective-permute-start | bytes 442376 | tf_op jit(solution)/shard_map/ppermute | solution.py:372
  69.5 7.9 %collective-permute-start.19 = (f32[96,384]{1,0:T(8,128)S(1)}, f32[96,384]{1,0:T(8,128)S(1)}, u32[]{:S(2)}, u32[]{:S(2)}) collective-permute-start(f32[96,384]{1,0:T(8,128)S(1)} %collective-permute-done.18.refs_4_), channel_id=1, source_target_pairs={{0,1},{1,0},{2,3},{3,2},{4,5},{5,4},{6,7},{7,6},{8,9},{9,8},{10,11... | collective-permute-start | bytes 442376 | tf_op jit(solution)/shard_map/ppermute | solution.py:372
  69.5 7.9 %collective-permute-start.21 = (f32[96,384]{1,0:T(8,128)S(1)}, f32[96,384]{1,0:T(8,128)S(1)}, u32[]{:S(2)}, u32[]{:S(2)}) collective-permute-start(f32[96,384]{1,0:T(8,128)S(1)} %collective-permute-done.20.refs_6_), channel_id=1, source_target_pairs={{0,1},{1,0},{2,3},{3,2},{4,5},{5,4},{6,7},{7,6},{8,9},{9,8},{10,11... | collective-permute-start | bytes 442376 | tf_op jit(solution)/shard_map/ppermute | solution.py:372
  90.4 6.8 %collective-permute-start.39 = (f32[584,128]{1,0:T(8,128)S(1)}, f32[584,128]{1,0:T(8,128)S(1)}, u32[]{:S(2)}, u32[]{:S(2)}) collective-permute-start(f32[584,128]{1,0:T(8,128)S(1)} %get-tuple-element.103), channel_id=1, source_target_pairs={{0,2},{1,9},{2,0},{3,11},{4,6},{5,13},{6,4},{7,15},{8,10},{9,1},{1... | collective-permute-start | bytes 897032 | tf_op jit(solution)/shard_map/ppermute | solution.py:372
  91.3 10.2 %collective-permute-start.33 = (f32[576,128]{1,0:T(8,128)S(1)}, f32[576,128]{1,0:T(8,128)S(1)}, u32[]{:S(2)}, u32[]{:S(2)}) collective-permute-start(f32[576,128]{1,0:T(8,128)S(1)} %get-tuple-element.94), channel_id=1, source_target_pairs={{0,2},{1,9},{2,0},{3,11},{4,6},{5,13},{6,4},{7,15},{8,10},{9,1},{1... | collective-permute-start | bytes 884744 | tf_op jit(solution)/shard_map/ppermute | solution.py:372
  98.6 6.5 %collective-permute-start.41 = (f32[152,128]{1,0:T(8,128)S(1)}, f32[152,128]{1,0:T(8,128)S(1)}, u32[]{:S(2)}, u32[]{:S(2)}) collective-permute-start(f32[152,128]{1,0:T(8,128)S(1)} %get-tuple-element.106), channel_id=1, source_target_pairs={{0,4},{1,5},{2,6},{3,7},{4,0},{5,1},{6,2},{7,3},{8,12},{9,13},{10,... | collective-permute-start | bytes 233480 | tf_op jit(solution)/shard_map/ppermute | solution.py:372
  101.5 6.2 %collective-permute-start.34 = (f32[144,128]{1,0:T(8,128)S(1)}, f32[144,128]{1,0:T(8,128)S(1)}, u32[]{:S(2)}, u32[]{:S(2)}) collective-permute-start(f32[144,128]{1,0:T(8,128)S(1)} %get-tuple-element.96), channel_id=1, source_target_pairs={{0,12},{1,7},{2,14},{3,5},{4,8},{5,3},{6,10},{7,1},{8,4},{9,15},{1... | collective-permute-start | bytes 221192 | tf_op jit(solution)/shard_map/ppermute | solution.py:372
  105.1 7.9 %collective-permute-start.43 = (f32[152,128]{1,0:T(8,128)S(1)}, f32[152,128]{1,0:T(8,128)S(1)}, u32[]{:S(2)}, u32[]{:S(2)}) collective-permute-start(f32[152,128]{1,0:T(8,128)S(1)} %shard_map.107.refs_2_), channel_id=1, source_target_pairs={{0,16},{1,17},{2,18},{3,19},{4,20},{5,21},{6,22},{7,23},{8,24},{9,... | collective-permute-start | bytes 233480 | tf_op jit(solution)/shard_map/ppermute | solution.py:372
  113.1 6.9 %collective-permute-start.44 = (f32[96,384]{1,0:T(8,128)S(1)}, f32[96,384]{1,0:T(8,128)S(1)}, u32[]{:S(2)}, u32[]{:S(2)}) collective-permute-start(f32[96,384]{1,0:T(8,128)S(1)} %get-tuple-element.108.refs_0_), channel_id=1, source_target_pairs={{0,8},{1,9},{2,10},{3,11},{4,12},{5,13},{6,14},{7,15},{8,0},{9,1},... | collective-permute-start | bytes 442376 | tf_op jit(solution)/shard_map/ppermute | solution.py:372
  (30 other events, 135.9 us)

commit v4 on v3

--- a/solution.py
+++ b/solution.py
@@ -23,7 +23,7 @@
 
 DIMS = (("sector", 1), ("term", 0), ("term", 1))
 CORE = ("sector", 0)
-ORDERS = ((0, 1, 2), (2, 1, 0))
+ORDERS = (((0, 1, 2), (2, 1, 0)), ((1, 0, 2), (1, 0, 2)))
 START_ORDER = (4, 2, 1, 6, 5, 3, 7)
 
 
@@ -37,6 +37,10 @@
     return pltpu.CompilerParams(vmem_limit_bytes=mib << 20)
 
 
+def chunks_of(size):
+    return ((0, size // 3 * 2), (size // 3 * 2, size // 3))
+
+
 def bit_of(axis, bit):
     return (lax.axis_index(axis) >> bit) & 1
 
@@ -49,8 +53,8 @@
     return place([bit_of(*dim) ^ ((k >> (2 - i)) & 1) for i, dim in enumerate(DIMS)], parity, rows)
 
 
-def slot_of(parity, masks):
-    a, b = (sum(masks[dim] << (2 - i) for i, dim in enumerate(order)) for order in ORDERS)
+def slot_of(chunk, parity, masks):
+    a, b = (sum(masks[dim] << (2 - i) for i, dim in enumerate(order)) for order in ORDERS[chunk])
     return jnp.where(parity == 0, a, b)
 
 
@@ -59,17 +63,29 @@
     return high, (x - high.astype(F32)).astype(BF16)
 
 
-def segments(first, rows, shard):
+def segments(first, b):
     me = lax.axis_index("sector")
+    whole, shard = chunks_of(b), chunks_of(b // 4)
     if first:
-        out = [[(h, me ^ side, h * rows, 0, rows) for h in range(CHUNKS)] for side in range(2)]
-        out += [[(h, me ^ (2 + side), 0, 0, rows)] for h in range(CHUNKS) for side in range(2)]
+        out = [[(h, me ^ side, start, 0, size) for h, (start, size) in enumerate(whole)] for side in range(2)]
+        out += [[(h, me ^ (2 + side), 0, 0, size)] for h, (_, size) in enumerate(whole) for side in range(2)]
         return out
     out = []
     for number in range(16):
-        sector, row = piece_place(number >> 1, (me & 1) ^ (number & 1), shard)
-        out.append([(h, sector, h * shard, row, shard) for h in range(CHUNKS)])
+        parity = (me & 1) ^ (number & 1)
+        out.append([(h, *rows_of(number >> 1, parity, start, size)) for h, (start, size) in enumerate(shard)])
     return out
+
+
+def rows_of(k, parity, start, size):
+    sector, row = piece_place(k, parity, size)
+    return sector, start, row, size
+
+
+def each_chunk(k, b):
+    for (whole, _), (start, size) in zip(chunks_of(b), chunks_of(b // 4)):
+        _, row = piece_place(k, 0, size)
+        yield slice(start, start + size), pl.ds(pl.multiple_of(row + whole, 8), size)
 
 
 def prep_kernel(left_ref, right_ref, psi_ref, diag_ref, left_cat, right_cat, vec_ref, mine_ref):
@@ -85,12 +101,9 @@
         return carry
 
     lax.fori_loop(0, left_ref.shape[0], one, 0)
-    rows = vec_ref.shape[0] // CHUNKS
-    for h in range(CHUNKS):
-        _, row = piece_place(0, 0, rows)
-        at = pl.ds(pl.multiple_of(row + h * 4 * rows, 8), rows)
-        vec_ref[h * rows:(h + 1) * rows, :] = psi_ref[0, at, :]
-        mine_ref[h * rows:(h + 1) * rows, :] = diag_ref[0, at, :]
+    for here, there in each_chunk(0, b):
+        vec_ref[here, :] = psi_ref[0, there, :]
+        mine_ref[here, :] = diag_ref[0, there, :]
 
 
 def prepare(left_ops, right_ops, psi, diag):
@@ -131,10 +144,9 @@
     else:
         right, cat_ref, inv_ref, vec = refs
     b = right.shape[1]
-    rows = b // CHUNKS
-    shard = rows // 4
+    whole = chunks_of(b)
     total = jnp.zeros((1, b), F32)
-    cuts_of = segments(first, rows, shard)
+    cuts_of = segments(first, b)
     for piece, cuts in zip(parts, [cuts_of[i] for i in picked(half, len(cuts_of))]):
         for chunk, sector, start, row, size in cuts:
             if half is not None and chunk != half:
@@ -143,7 +155,7 @@
             high, low = split(x)
             total += jnp.sum(x * x, axis=0, keepdims=True)
             if half is None:
-                row = pl.multiple_of(row + chunk * rows, 16)
+                row = pl.multiple_of(row + whole[chunk][0], 16)
             at = pl.ds(row, size)
             for place, y in enumerate((high, low, high)):
                 vec[sector, at, place * b:(place + 1) * b] = y
@@ -160,7 +172,7 @@
         if half == 0:
             early_h[p], early_l[p] = high, low
             return carry
-        moves = [(high, low, 0)] if half is None else [(early_h[p], early_l[p], 0), (high, low, rows)]
+        moves = [(high, low, 0)] if half is None else [(early_h[p], early_l[p], 0), (high, low, whole[1][0])]
         for h, l, row in moves:
             for place, y in enumerate((h, h, l)):
                 cat_ref[p, place * b + row:place * b + row + h.shape[0], :] = y
@@ -175,7 +187,7 @@
 
 def inner(first, half, cells, sectors, pair_in, pair_count, pieces, right, early=()):
     pairs, b, _ = right.shape
-    rows = b if half is None else b // CHUNKS
+    rows = b if half is None else chunks_of(b)[half][1]
     compact = jax.ShapeDtypeStruct((pairs, rows, b), BF16)
     row = jax.ShapeDtypeStruct((TILE[0], b), F32)
     shapes = [compact, compact, row] if half == 0 else [jax.ShapeDtypeStruct((pairs, 3 * b, b), BF16), row]
@@ -198,7 +210,8 @@
     shard = rows // 4
     core = lax.axis_index("sector") & 1
     acc[...] = jnp.zeros_like(acc)
-    here = slice(chunk * rows, (chunk + 1) * rows)
+    first_row = chunks_of(b)[chunk][0]
+    here = slice(first_row, first_row + rows)
 
     def one_pair(p, carry):
         target = out_ref[0, p]
@@ -209,7 +222,7 @@
     scale = inv_ref[:1, :]
     rho = jnp.zeros((1, b), F32)
     wide = shard * b // TILE[1]
-    for number, (piece, cuts) in enumerate(zip(parts, segments(first, rows, shard))):
+    for number, (piece, cuts) in enumerate(zip(parts, segments(first, b))):
         side = number & 1
         dest = send_ref if side else keep_ref
         for at, sector, start, row, size in cuts:
@@ -223,7 +236,7 @@
                     masks = tuple((number >> (3 - i)) & 1 for i in range(3))
                     here = pl.ds(row, shard)
                 x = acc[sector, here, :] * scale
-                slot = slot_of(core ^ side, masks)
+                slot = slot_of(chunk, core ^ side, masks)
                 store_wide(dest, pl.multiple_of(slot * wide, 8), x)
                 rho += jnp.sum(x * piece[start + q * shard:start + (q + 1) * shard, :], axis=0, keepdims=True)
     rho = jnp.broadcast_to(jnp.sum(rho * scale, axis=1, keepdims=True), TILE) / cells + before_ref[...]
@@ -235,7 +248,7 @@
 
 def outer(first, chunk, cells, sectors, pair_out, pair_count, pieces, ops, inv, before):
     pairs, _, b = ops[1].shape
-    rows = b // CHUNKS
+    rows = chunks_of(b)[chunk][1]
     extra = TILE[0] if chunk == CHUNKS - 1 else 0
     half = jax.ShapeDtypeStruct((sectors * rows // 2 * b // TILE[1] + extra, TILE[1]), F32)
     return pl.pallas_call(
@@ -290,15 +303,14 @@
 def update_kernel(*refs):
     sums, (vec_ref, inv_ref, diag_ref, new_ref, energy_ref) = refs[:2 * CHUNKS], refs[2 * CHUNKS:]
     rows, b = new_ref.shape
-    shard = rows // CHUNKS
-    end = shard * b // TILE[1]
+    end = sums[-1].shape[0] - TILE[0]
     rho = sums[-2][end:, :] + sums[-1][end:, :]
     energy_ref[...] = rho
-    for h in range(CHUNKS):
+    for h, (start, size) in enumerate(chunks_of(rows)):
         mine_ref, recv_ref = sums[2 * h:2 * h + 2]
-        at = slice(h * shard, (h + 1) * shard)
+        at = slice(start, start + size)
         for c in range(b // TILE[1]):
-            part = slice(c * shard, (c + 1) * shard)
+            part = slice(c * size, (c + 1) * size)
             lanes = slice(c * TILE[1], (c + 1) * TILE[1])
             normed = vec_ref[at, lanes] * inv_ref[:1, lanes]
             sigma = mine_ref[part, :] + recv_ref[part, :]
@@ -328,12 +340,9 @@
 
 def join_kernel(*refs):
     *parts, out_ref = refs
-    rows = parts[0].shape[0] // CHUNKS
     for k, part in enumerate(parts):
-        _, row = piece_place(k, 0, rows)
-        for h in range(CHUNKS):
-            at = pl.ds(pl.multiple_of(row + h * 4 * rows, 8), rows)
-            out_ref[0, at, :] = part[h * rows:(h + 1) * rows, :]
+        for here, there in each_chunk(k, out_ref.shape[-1]):
+            out_ref[0, there, :] = part[here, :]
 
 
 def join(parts):
@@ -378,10 +387,9 @@
     rest = rest_dims(terms)
 
     own = psi_start[0]
-    rows = b // CHUNKS
     far = []
-    for h in range(CHUNKS):
-        far.append(swap(own[h * rows:(h + 1) * rows], [DIMS[0]]))
+    for start, size in chunks_of(b):
+        far.append(swap(own[start:start + size], [DIMS[0]]))
     beside = swap(own, [CORE])
     left, right, vec, diag = prepare(left_ops, right_ops, psi_start, diagonal)
     far[0], left, right, vec, diag = lax.optimization_barrier((far[0], left, right, vec, diag))
@@ -405,16 +413,17 @@
             send, keep, rho = outer(first, h, cells, sectors, pair_out, pair_count, pieces, (left, cat), inv, rho)
             keeps.append(keep)
             recvs.append(swap(send, [CORE]))
-        first_dims, second, third = ([[DIMS[dim]] for dim in step] for step in zip(*ORDERS))
+        orders = [[[[DIMS[dim]] for dim in step] for step in zip(*order)] for order in ORDERS]
         for h in range(CHUNKS):
             extra = TILE[0] if h == CHUNKS - 1 else 0
             keeps[h], send = cut(keeps[h], recvs[h], extra, 2)
-            recvs[h] = swap(send, *first_dims)
-        both = [a + b for a, b in zip(second, third)]
+            recvs[h] = swap(send, *orders[h][0])
         for h in range(CHUNKS):
             extra = TILE[0] if h == CHUNKS - 1 else 0
             slots = cut(keeps[h], recvs[h], extra, 4)
             parts = [slots[0]]
+            _, second, third = orders[h]
+            both = [a + b for a, b in zip(second, third)]
             for k, dims in ((3, both), (2, second), (1, third)):
                 parts.append(swap(slots[k], *dims))
             keeps[h] = parts

time: 123 us -> 124 us (level)
  waiting for transfers between devices: 41.4 us -> 44.7 us
  starting transfers between devices: 46.9 us -> 44.9 us
    ppermute x47, waiting for transfers between devices: 41.4 us -> 44.7 us  [swap(): lax.ppermute(x, AXES, flips(mesh_shape, even, even if odd is None else odd))]
    ppermute x47, starting transfers between devices: 46.9 us -> 44.9 us  [swap(): lax.ppermute(x, AXES, flips(mesh_shape, even, even if odd is None else odd))]
  transfers between devices with their start and end apart: 47 -> 47, of which waited for: 24 -> 21; matrix products, arithmetic and copies ran while one was open for 2% -> 2% of each run, Pallas kernels for 4% -> 8%
where the time goes in v4:
time: 124 us
  starting transfers between devices  44.9 us (36%)
  waiting for transfers between devices  44.7 us (36%)
  Pallas kernels  23.5 us (19%)
  local copies, waits for them, and re-layouts  7.66 us (6%)
  other arithmetic  1.85 us (1%)
  between operations  1.54 us (1%)
    ppermute x47, starting transfers between devices, swap(): lax.ppermute(x, AXES, flips(mesh_shape, even, even if odd is None else odd))  44.9 us
    ppermute x47, waiting for transfers between devices, swap(): lax.ppermute(x, AXES, flips(mesh_shape, even, even if odd is None else odd))  44.7 us
    pallas_call x4, Pallas kernels, outer(): pl.pallas_call(functools.partial(outer_kernel, first, chunk, cells, len(p...  11.1 us
    pallas_call x3, Pallas kernels, inner(): pl.pallas_call(functools.partial(inner_kernel, first, half, cells, len(pi...  9.83 us
    unnamed x14, local copies, waits for them, and re-layouts  5.47 us
  transfers between devices with their start and end apart: 47, of which 21 were waited for; matrix products, arithmetic and copies ran while one was open for 2% of the time, Pallas kernels for 8%

profile of v4, /device:TPU:0, one launch (start us, length us, event | category | flops | bytes accessed | tf_op | source)
XLA Modules:
  0.0 124.1 jit_solution(13350902680197212864)
XLA Ops:
  1.7 3.1 %collective-permute-start.1 = (f32[256,384]{1,0:T(8,128)S(1)}, f32[256,384]{1,0:T(8,128)S(1)}, u32[]{:S(2)}, u32[]{:S(2)}) collective-permute-start(f32[256,384]{1,0:T(8,128)S(1)} %slice_bitcast_fusion), channel_id=1, source_target_pairs={{0,2},{1,3},{2,0},{3,1},{4,6},{5,7},{6,4},{7,5},{8,10},{9,11},{10,... | collective-permute-start | bytes 1179656 | tf_op jit(solution)/shard_map/ppermute | solution.py:381
  11.3 2.6 %collective-permute-done.1.refs_4_ = f32[256,384]{1,0:T(8,128)S(1)} collective-permute-done((f32[256,384]{1,0:T(8,128)S(1)}, f32[256,384]{1,0:T(8,128)S(1)}, u32[]{:S(2)}, u32[]{:S(2)}) %collective-permute-start.1) | collective-permute-done | bytes 393248 | tf_op jit(solution)/shard_map/ppermute | solution.py:381
  15.7 5.6 %collective-permute-done.3.refs_4_.refs_6_ = f32[128,384]{1,0:T(8,128)S(1)} collective-permute-done((f32[128,384]{1,0:T(8,128)S(1)}, f32[128,384]{1,0:T(8,128)S(1)}, u32[]{:S(2)}, u32[]{:S(2)}) %collective-permute-start.3) | collective-permute-done | bytes 196640 | tf_op jit(solution)/shard_map/ppermute | solution.py:381
  22.0 3.2 %shard_map.87 = (bf16[4,256,384]{2,1,0:T(8,128)(2,1)S(1)}, bf16[4,256,384]{2,1,0:T(8,128)(2,1)S(1)}, f32[8,384]{1,0:T(8,128)S(1)}) custom-call(s32[1,4]{1,0:T(1,128)S(1)} %copy-done.6, s32[1]{0:T(128)S(6)} %copy.9.refs_1_, f32[384,384]{1,0:T(8,128)S(1)} %bitcast.8, f32[384,384]{1,0:T(8,128)S(1)} %collective-permute-done.refs_3_, ...), custom_call_target="tpu_custom_call" | custom-call | flops 905969664 | bytes 4718592 | tf_op jit(solution)/shard_map/pallas_call | solution.py:194
  25.3 2.7 %shard_map.88 = (bf16[4,1152,384]{2,1,0:T(8,128)(2,1)S(1)}, f32[8,384]{1,0:T(8,128)S(1)}) custom-call(s32[1,4]{1,0:T(1,128)S(1)} %copy-done.6, s32[1]{0:T(128)S(6)} %copy.9.refs_1_, f32[384,384]{1,0:T(8,128)S(1)} %bitcast.9, f32[384,384]{1,0:T(8,128)S(1)} %collective-permute-done.refs_3_, f32[128,384]{1,0:T(8,128)S(1)} %collective-permute-done.3.refs_4_.refs_6_, ...), custom_call_target="tpu_custom_call" | custom-call | flops 452984832 | bytes 4718592 | tf_op jit(solution)/shard_map/pallas_call | solution.py:194
  28.0 2.9 %shard_map.89 = (f32[1536,128]{1,0:T(8,128)S(1)}, f32[1536,128]{1,0:T(8,128)S(1)}, f32[8,128]{1,0:T(8,128)S(1)}) custom-call(s32[1,4]{1,0:T(1,128)S(1)} %copy-done.5, s32[1]{0:T(128)S(6)} %copy.9.refs_1_, f32[384,384]{1,0:T(8,128)S(1)} %bitcast.10, f32[384,384]{1,0:T(8,128)S(1)} %collective-permute-done.refs_3_, ...), custom_call_target="tpu_custom_call" | custom-call | flops 905969664 | bytes 4718592 | tf_op jit(solution)/shard_map/pallas_call | solution.py:254
  30.8 2.7 %shard_map.93 = (f32[776,128]{1,0:T(8,128)S(1)}, f32[776,128]{1,0:T(8,128)S(1)}, f32[8,128]{1,0:T(8,128)}) custom-call(s32[1,4]{1,0:T(1,128)S(1)} %copy-done.5, s32[1]{0:T(128)S(6)} %copy.9.refs_1_, f32[384,384]{1,0:T(8,128)S(1)} %bitcast.11, f32[384,384]{1,0:T(8,128)S(1)} %collective-permute-done.refs_3_, f32[256,384]{1,0:T(8,128)S(1)} %collective-permute-done.1.refs_4_, ...), custom_call_target="tpu_custom_call" | custom-call | flops 452984832 | bytes 4718592 | tf_op jit(solution)/shard_map/pallas_call | solution.py:254
  35.4 6.3 %collective-permute-done.6.recv_ref = f32[768,128]{1,0:T(8,128)S(1)} collective-permute-done((f32[768,128]{1,0:T(8,128)S(1)}, f32[768,128]{1,0:T(8,128)S(1)}, u32[]{:S(2)}, u32[]{:S(2)}) %collective-permute-start.6) | collective-permute-done | bytes 393248 | tf_op jit(solution)/shard_map/ppermute | solution.py:381
  41.7 3.1 %collective-permute-start.7 = (f32[192,128]{1,0:T(8,128)S(1)}, f32[192,128]{1,0:T(8,128)S(1)}, u32[]{:S(2)}, u32[]{:S(2)}) collective-permute-start(f32[192,128]{1,0:T(8,128)S(1)} %get-tuple-element.73), channel_id=1, source_target_pairs={{0,12},{1,7},{2,14},{3,5},{4,8},{5,3},{6,10},{7,1},{8,4},{9,15},{1... | collective-permute-start | bytes 294920 | tf_op jit(solution)/shard_map/ppermute | solution.py:381
  45.4 2.6 %collective-permute-start.13 = (f32[104,128]{1,0:T(8,128)S(1)}, f32[104,128]{1,0:T(8,128)S(1)}, u32[]{:S(2)}, u32[]{:S(2)}) collective-permute-start(f32[104,128]{1,0:T(8,128)S(1)} %get-tuple-element.82), channel_id=1, source_target_pairs={{0,10},{1,11},{2,8},{3,9},{4,14},{5,15},{6,12},{7,13},{8,2},{9,3},... | collective-permute-start | bytes 159752 | tf_op jit(solution)/shard_map/ppermute | solution.py:381
  50.5 1.8 %collective-permute-start.10 = (f32[192,128]{1,0:T(8,128)S(1)}, f32[192,128]{1,0:T(8,128)S(1)}, u32[]{:S(2)}, u32[]{:S(2)}) collective-permute-start(f32[192,128]{1,0:T(8,128)S(1)} %shard_map.92.refs_0_), channel_id=1, source_target_pairs={{0,16},{1,17},{2,18},{3,19},{4,20},{5,21},{6,22},{7,23},{8,24},{9,... | collective-permute-start | bytes 294920 | tf_op jit(solution)/shard_map/ppermute | solution.py:381
  53.6 2.3 %collective-permute-start.16 = (f32[104,128]{1,0:T(8,128)S(1)}, f32[104,128]{1,0:T(8,128)S(1)}, u32[]{:S(2)}, u32[]{:S(2)}) collective-permute-start(f32[104,128]{1,0:T(8,128)S(1)} %shard_map.96.refs_2_), channel_id=1, source_target_pairs={{0,16},{1,17},{2,18},{3,19},{4,20},{5,21},{6,22},{7,23},{8,24},{9,... | collective-permute-start | bytes 159752 | tf_op jit(solution)/shard_map/ppermute | solution.py:381
  56.0 3.5 %collective-permute-done.16.refs_3_ = f32[104,128]{1,0:T(8,128)S(1)} collective-permute-done((f32[104,128]{1,0:T(8,128)S(1)}, f32[104,128]{1,0:T(8,128)S(1)}, u32[]{:S(2)}, u32[]{:S(2)}) %collective-permute-start.16) | collective-permute-done | bytes 53280 | tf_op jit(solution)/shard_map/ppermute | solution.py:381
  61.2 2.0 %collective-permute-start.22 = (f32[96,384]{1,0:T(8,128)S(1)}, f32[96,384]{1,0:T(8,128)S(1)}, u32[]{:S(2)}, u32[]{:S(2)}) collective-permute-start(f32[96,384]{1,0:T(8,128)S(1)} %get-tuple-element.87.refs_2_.refs_4_), channel_id=1, source_target_pairs={{0,12},{1,13},{2,14},{3,15},{4,8},{5,9},{6,10},{7,11},{8,4},{9,5},... | collective-permute-start | bytes 442376 | tf_op jit(solution)/shard_map/ppermute | solution.py:381
  68.2 4.6 %collective-permute-start.30 = (f32[96,384]{1,0:T(8,128)S(1)}, f32[96,384]{1,0:T(8,128)S(1)}, u32[]{:S(2)}, u32[]{:S(2)}) collective-permute-start(f32[96,384]{1,0:T(8,128)S(1)} %get-tuple-element.87.refs_2_.refs_4_), channel_id=1, source_target_pairs={{0,14},{1,15},{2,12},{3,13},{4,10},{5,11},{6,8},{7,9},{8,6},{9,7},... | collective-permute-start | bytes 442376 | tf_op jit(solution)/shard_map/ppermute | solution.py:381
  72.8 5.2 %collective-permute-done.24.refs_10_ = f32[96,384]{1,0:T(8,128)S(1)} collective-permute-done((f32[96,384]{1,0:T(8,128)S(1)}, f32[96,384]{1,0:T(8,128)S(1)}, u32[]{:S(2)}, u32[]{:S(2)}) %collective-permute-start.24) | collective-permute-done | bytes 147488 | tf_op jit(solution)/shard_map/ppermute | solution.py:381
  80.7 3.9 %shard_map.98 = (bf16[4,1152,384]{2,1,0:T(8,128)(2,1)S(1)}, f32[8,384]{1,0:T(8,128)S(1)}) custom-call(s32[1,4]{1,0:T(1,128)S(1)} %copy-done.6, s32[1]{0:T(128)S(6)} %copy.9.refs_1_, f32[96,384]{1,0:T(8,128)S(1)} %get-tuple-element.87.refs_2_.refs_4_, f32[96,384]{1,0:T(8,128)S(1)} %collective-permute-done.17.refs_3_, ...), custom_call_target="tpu_custom_call" | custom-call | flops 1358954496 | bytes 4718592 | tf_op jit(solution)/shard_map/pallas_call | solution.py:194
  84.7 2.9 %shard_map.100 = (f32[1536,128]{1,0:T(8,128)S(1)}, f32[1536,128]{1,0:T(8,128)S(1)}, f32[8,128]{1,0:T(8,128)S(1)}) custom-call(s32[1,4]{1,0:T(1,128)S(1)} %copy-done.5, s32[1]{0:T(128)S(6)} %copy.9.refs_1_, f32[96,384]{1,0:T(8,128)S(1)} %get-tuple-element.87.refs_2_.refs_4_, f32[96,384]{1,0:T(8,128)S(1)} %collective-permute-done.17.refs_3_, ...), custom_call_target="tpu_custom_call" | custom-call | flops 905969664 | bytes 4718592 | tf_op jit(solution)/shard_map/pallas_call | solution.py:254
  87.6 2.7 %shard_map.104 = (f32[776,128]{1,0:T(8,128)S(1)}, f32[776,128]{1,0:T(8,128)S(1)}, f32[8,128]{1,0:T(8,128)}) custom-call(s32[1,4]{1,0:T(1,128)S(1)} %copy-done.5, s32[1]{0:T(128)S(6)} %copy.9.refs_1_, f32[96,384]{1,0:T(8,128)S(1)} %get-tuple-element.87.refs_2_.refs_4_, f32[96,384]{1,0:T(8,128)S(1)} %collective-permute-done.17.refs_3_, ...), custom_call_target="tpu_custom_call" | custom-call | flops 452984832 | bytes 4718592 | tf_op jit(solution)/shard_map/pallas_call | solution.py:254
  92.2 6.2 %collective-permute-done.33.recv_ref = f32[768,128]{1,0:T(8,128)S(1)} collective-permute-done((f32[768,128]{1,0:T(8,128)S(1)}, f32[768,128]{1,0:T(8,128)S(1)}, u32[]{:S(2)}, u32[]{:S(2)}) %collective-permute-start.33) | collective-permute-done | bytes 393248 | tf_op jit(solution)/shard_map/ppermute | solution.py:381
  105.6 2.3 %collective-permute-start.37 = (f32[192,128]{1,0:T(8,128)S(1)}, f32[192,128]{1,0:T(8,128)S(1)}, u32[]{:S(2)}, u32[]{:S(2)}) collective-permute-start(f32[192,128]{1,0:T(8,128)S(1)} %shard_map.103.refs_0_), channel_id=1, source_target_pairs={{0,16},{1,17},{2,18},{3,19},{4,20},{5,21},{6,22},{7,23},{8,24},{9,... | collective-permute-start | bytes 294920 | tf_op jit(solution)/shard_map/ppermute | solution.py:381
  111.0 3.9 %collective-permute-done.43.refs_3_ = f32[104,128]{1,0:T(8,128)S(1)} collective-permute-done((f32[104,128]{1,0:T(8,128)S(1)}, f32[104,128]{1,0:T(8,128)S(1)}, u32[]{:S(2)}, u32[]{:S(2)}) %collective-permute-start.43) | collective-permute-done | bytes 53280 | tf_op jit(solution)/shard_map/ppermute | solution.py:381
  116.5 2.0 %collective-permute-start.46 = (f32[96,384]{1,0:T(8,128)S(1)}, f32[96,384]{1,0:T(8,128)S(1)}, u32[]{:S(2)}, u32[]{:S(2)}) collective-permute-start(f32[96,384]{1,0:T(8,128)S(1)} %get-tuple-element.108.refs_0_), channel_id=1, source_target_pairs={{0,12},{1,13},{2,14},{3,15},{4,8},{5,9},{6,10},{7,11},{8,4},{9,5},... | collective-permute-start | bytes 442376 | tf_op jit(solution)/shard_map/ppermute | solution.py:381
  119.6 1.8 %pad_maximum_fusion = f32[2]{0:T(128)} fusion(f32[1]{0:T(128)} %bitcast.4, f32[1]{0:T(128)} %bitcast.3), kind=kLoop, calls=%fused_computation.2 | loop fusion | flops 2 | bytes 16 | tf_op jit(solution)/shard_map/stack | solution.py:447
  (114 shorter events, 42.6 us)
Async XLA Ops:
  1.7 12.2 %collective-permute-start.1 = (f32[256,384]{1,0:T(8,128)S(1)}, f32[256,384]{1,0:T(8,128)S(1)}, u32[]{:S(2)}, u32[]{:S(2)}) collective-permute-start(f32[256,384]{1,0:T(8,128)S(1)} %slice_bitcast_fusion), channel_id=1, source_target_pairs={{0,2},{1,3},{2,0},{3,1},{4,6},{5,7},{6,4},{7,5},{8,10},{9,11},{10,... | collective-permute-start | bytes 1179656 | tf_op jit(solution)/shard_map/ppermute | solution.py:381
  4.8 17.2 %collective-permute-start = (f32[384,384]{1,0:T(8,128)}, f32[384,384]{1,0:T(8,128)S(1)}, u32[]{:S(2)}, u32[]{:S(2)}) collective-permute-start(f32[384,384]{1,0:T(8,128)} %bitcast.7), channel_id=1, source_target_pairs={{0,1},{1,0},{2,3},{3,2},{4,5},{5,4},{6,7},{7,6},{8,9},{9,8},{10,11... | collective-permute-start | bytes 1769480 | tf_op jit(solution)/shard_map/ppermute | solution.py:381
  13.9 8.1 %collective-permute-start.2 = (f32[256,384]{1,0:T(8,128)S(1)}, f32[256,384]{1,0:T(8,128)S(1)}, u32[]{:S(2)}, u32[]{:S(2)}) collective-permute-start(f32[256,384]{1,0:T(8,128)S(1)} %collective-permute-done.1.refs_4_), channel_id=1, source_target_pairs={{0,1},{1,0},{2,3},{3,2},{4,5},{5,4},{6,7},{7,6},{8,9},{9,8},{10,11... | collective-permute-start | bytes 1179656 | tf_op jit(solution)/shard_map/ppermute | solution.py:381
  13.9 7.4 %collective-permute-start.3 = (f32[128,384]{1,0:T(8,128)S(1)}, f32[128,384]{1,0:T(8,128)S(1)}, u32[]{:S(2)}, u32[]{:S(2)}) collective-permute-start(f32[128,384]{1,0:T(8,128)S(1)} %slice_bitcast_fusion.1), channel_id=1, source_target_pairs={{0,2},{1,3},{2,0},{3,1},{4,6},{5,7},{6,4},{7,5},{8,10},{9,11},{10,... | collective-permute-start | bytes 589832 | tf_op jit(solution)/shard_map/ppermute | solution.py:381
  33.8 7.8 %collective-permute-start.6 = (f32[768,128]{1,0:T(8,128)S(1)}, f32[768,128]{1,0:T(8,128)S(1)}, u32[]{:S(2)}, u32[]{:S(2)}) collective-permute-start(f32[768,128]{1,0:T(8,128)S(1)} %get-tuple-element.71), channel_id=1, source_target_pairs={{0,2},{1,9},{2,0},{3,11},{4,6},{5,13},{6,4},{7,15},{8,10},{9,1},{1... | collective-permute-start | bytes 1179656 | tf_op jit(solution)/shard_map/ppermute | solution.py:381
  35.3 10.1 %collective-permute-start.12 = (f32[392,128]{1,0:T(8,128)S(1)}, f32[392,128]{1,0:T(8,128)S(1)}, u32[]{:S(2)}, u32[]{:S(2)}) collective-permute-start(f32[392,128]{1,0:T(8,128)S(1)} %get-tuple-element.80), channel_id=1, source_target_pairs={{0,4},{1,5},{2,6},{3,7},{4,0},{5,1},{6,2},{7,3},{8,12},{9,13},{10,... | collective-permute-start | bytes 602120 | tf_op jit(solution)/shard_map/ppermute | solution.py:381
  41.7 7.2 %collective-permute-start.7 = (f32[192,128]{1,0:T(8,128)S(1)}, f32[192,128]{1,0:T(8,128)S(1)}, u32[]{:S(2)}, u32[]{:S(2)}) collective-permute-start(f32[192,128]{1,0:T(8,128)S(1)} %get-tuple-element.73), channel_id=1, source_target_pairs={{0,12},{1,7},{2,14},{3,5},{4,8},{5,3},{6,10},{7,1},{8,4},{9,15},{1... | collective-permute-start | bytes 294920 | tf_op jit(solution)/shard_map/ppermute | solution.py:381
  45.4 6.9 %collective-permute-start.13 = (f32[104,128]{1,0:T(8,128)S(1)}, f32[104,128]{1,0:T(8,128)S(1)}, u32[]{:S(2)}, u32[]{:S(2)}) collective-permute-start(f32[104,128]{1,0:T(8,128)S(1)} %get-tuple-element.82), channel_id=1, source_target_pairs={{0,10},{1,11},{2,8},{3,9},{4,14},{5,15},{6,12},{7,13},{8,2},{9,3},... | collective-permute-start | bytes 159752 | tf_op jit(solution)/shard_map/ppermute | solution.py:381
  50.5 9.0 %collective-permute-start.10 = (f32[192,128]{1,0:T(8,128)S(1)}, f32[192,128]{1,0:T(8,128)S(1)}, u32[]{:S(2)}, u32[]{:S(2)}) collective-permute-start(f32[192,128]{1,0:T(8,128)S(1)} %shard_map.92.refs_0_), channel_id=1, source_target_pairs={{0,16},{1,17},{2,18},{3,19},{4,20},{5,21},{6,22},{7,23},{8,24},{9,... | collective-permute-start | bytes 294920 | tf_op jit(solution)/shard_map/ppermute | solution.py:381
  59.6 6.8 %collective-permute-start.18 = (f32[96,384]{1,0:T(8,128)S(1)}, f32[96,384]{1,0:T(8,128)S(1)}, u32[]{:S(2)}, u32[]{:S(2)}) collective-permute-start(f32[96,384]{1,0:T(8,128)S(1)} %get-tuple-element.87.refs_2_.refs_4_), channel_id=1, source_target_pairs={{0,8},{1,9},{2,10},{3,11},{4,12},{5,13},{6,14},{7,15},{8,0},{9,1},... | collective-permute-start | bytes 442376 | tf_op jit(solution)/shard_map/ppermute | solution.py:381
  59.7 8.5 %collective-permute-start.20 = (f32[96,384]{1,0:T(8,128)S(1)}, f32[96,384]{1,0:T(8,128)S(1)}, u32[]{:S(2)}, u32[]{:S(2)}) collective-permute-start(f32[96,384]{1,0:T(8,128)S(1)} %get-tuple-element.87.refs_2_.refs_4_), channel_id=1, source_target_pairs={{0,4},{1,5},{2,6},{3,7},{4,0},{5,1},{6,2},{7,3},{8,12},{9,13},{10,... | collective-permute-start | bytes 442376 | tf_op jit(solution)/shard_map/ppermute | solution.py:381
  61.2 11.6 %collective-permute-start.22 = (f32[96,384]{1,0:T(8,128)S(1)}, f32[96,384]{1,0:T(8,128)S(1)}, u32[]{:S(2)}, u32[]{:S(2)}) collective-permute-start(f32[96,384]{1,0:T(8,128)S(1)} %get-tuple-element.87.refs_2_.refs_4_), channel_id=1, source_target_pairs={{0,12},{1,13},{2,14},{3,15},{4,8},{5,9},{6,10},{7,11},{8,4},{9,5},... | collective-permute-start | bytes 442376 | tf_op jit(solution)/shard_map/ppermute | solution.py:381
  63.2 14.8 %collective-permute-start.24 = (f32[96,384]{1,0:T(8,128)S(1)}, f32[96,384]{1,0:T(8,128)S(1)}, u32[]{:S(2)}, u32[]{:S(2)}) collective-permute-start(f32[96,384]{1,0:T(8,128)S(1)} %get-tuple-element.87.refs_2_.refs_4_), channel_id=1, source_target_pairs={{0,2},{1,3},{2,0},{3,1},{4,6},{5,7},{6,4},{7,5},{8,10},{9,11},{10,... | collective-permute-start | bytes 442376 | tf_op jit(solution)/shard_map/ppermute | solution.py:381
  63.5 14.5 %collective-permute-start.26 = (f32[96,384]{1,0:T(8,128)S(1)}, f32[96,384]{1,0:T(8,128)S(1)}, u32[]{:S(2)}, u32[]{:S(2)}) collective-permute-start(f32[96,384]{1,0:T(8,128)S(1)} %get-tuple-element.87.refs_2_.refs_4_), channel_id=1, source_target_pairs={{0,10},{1,11},{2,8},{3,9},{4,14},{5,15},{6,12},{7,13},{8,2},{9,3},... | collective-permute-start | bytes 442376 | tf_op jit(solution)/shard_map/ppermute | solution.py:381
  66.4 12.1 %collective-permute-start.28 = (f32[96,384]{1,0:T(8,128)S(1)}, f32[96,384]{1,0:T(8,128)S(1)}, u32[]{:S(2)}, u32[]{:S(2)}) collective-permute-start(f32[96,384]{1,0:T(8,128)S(1)} %get-tuple-element.87.refs_2_.refs_4_), channel_id=1, source_target_pairs={{0,6},{1,7},{2,4},{3,5},{4,2},{5,3},{6,0},{7,1},{8,14},{9,15},{10,... | collective-permute-start | bytes 442376 | tf_op jit(solution)/shard_map/ppermute | solution.py:381
  68.2 10.4 %collective-permute-start.30 = (f32[96,384]{1,0:T(8,128)S(1)}, f32[96,384]{1,0:T(8,128)S(1)}, u32[]{:S(2)}, u32[]{:S(2)}) collective-permute-start(f32[96,384]{1,0:T(8,128)S(1)} %get-tuple-element.87.refs_2_.refs_4_), channel_id=1, source_target_pairs={{0,14},{1,15},{2,12},{3,13},{4,10},{5,11},{6,8},{7,9},{8,6},{9,7},... | collective-permute-start | bytes 442376 | tf_op jit(solution)/shard_map/ppermute | solution.py:381
  72.8 6.3 %collective-permute-start.19 = (f32[96,384]{1,0:T(8,128)S(1)}, f32[96,384]{1,0:T(8,128)S(1)}, u32[]{:S(2)}, u32[]{:S(2)}) collective-permute-start(f32[96,384]{1,0:T(8,128)S(1)} %collective-permute-done.18.refs_4_), channel_id=1, source_target_pairs={{0,1},{1,0},{2,3},{3,2},{4,5},{5,4},{6,7},{7,6},{8,9},{9,8},{10,11... | collective-permute-start | bytes 442376 | tf_op jit(solution)/shard_map/ppermute | solution.py:381
  90.5 7.8 %collective-permute-start.33 = (f32[768,128]{1,0:T(8,128)S(1)}, f32[768,128]{1,0:T(8,128)S(1)}, u32[]{:S(2)}, u32[]{:S(2)}) collective-permute-start(f32[768,128]{1,0:T(8,128)S(1)} %get-tuple-element.94), channel_id=1, source_target_pairs={{0,2},{1,9},{2,0},{3,11},{4,6},{5,13},{6,4},{7,15},{8,10},{9,1},{1... | collective-permute-start | bytes 1179656 | tf_op jit(solution)/shard_map/ppermute | solution.py:381
  92.1 9.9 %collective-permute-start.39 = (f32[392,128]{1,0:T(8,128)S(1)}, f32[392,128]{1,0:T(8,128)S(1)}, u32[]{:S(2)}, u32[]{:S(2)}) collective-permute-start(f32[392,128]{1,0:T(8,128)S(1)} %get-tuple-element.103), channel_id=1, source_target_pairs={{0,4},{1,5},{2,6},{3,7},{4,0},{5,1},{6,2},{7,3},{8,12},{9,13},{10,... | collective-permute-start | bytes 602120 | tf_op jit(solution)/shard_map/ppermute | solution.py:381
  98.4 6.2 %collective-permute-start.34 = (f32[192,128]{1,0:T(8,128)S(1)}, f32[192,128]{1,0:T(8,128)S(1)}, u32[]{:S(2)}, u32[]{:S(2)}) collective-permute-start(f32[192,128]{1,0:T(8,128)S(1)} %get-tuple-element.96), channel_id=1, source_target_pairs={{0,12},{1,7},{2,14},{3,5},{4,8},{5,3},{6,10},{7,1},{8,4},{9,15},{1... | collective-permute-start | bytes 294920 | tf_op jit(solution)/shard_map/ppermute | solution.py:381
  105.6 9.3 %collective-permute-start.37 = (f32[192,128]{1,0:T(8,128)S(1)}, f32[192,128]{1,0:T(8,128)S(1)}, u32[]{:S(2)}, u32[]{:S(2)}) collective-permute-start(f32[192,128]{1,0:T(8,128)S(1)} %shard_map.103.refs_0_), channel_id=1, source_target_pairs={{0,16},{1,17},{2,18},{3,19},{4,20},{5,21},{6,22},{7,23},{8,24},{9,... | collective-permute-start | bytes 294920 | tf_op jit(solution)/shard_map/ppermute | solution.py:381
  114.9 6.5 %collective-permute-start.44 = (f32[96,384]{1,0:T(8,128)S(1)}, f32[96,384]{1,0:T(8,128)S(1)}, u32[]{:S(2)}, u32[]{:S(2)}) collective-permute-start(f32[96,384]{1,0:T(8,128)S(1)} %get-tuple-element.108.refs_0_), channel_id=1, source_target_pairs={{0,8},{1,9},{2,10},{3,11},{4,12},{5,13},{6,14},{7,15},{8,0},{9,1},... | collective-permute-start | bytes 442376 | tf_op jit(solution)/shard_map/ppermute | solution.py:381
  115.4 6.2 %collective-permute-start.45 = (f32[96,384]{1,0:T(8,128)S(1)}, f32[96,384]{1,0:T(8,128)S(1)}, u32[]{:S(2)}, u32[]{:S(2)}) collective-permute-start(f32[96,384]{1,0:T(8,128)S(1)} %get-tuple-element.108.refs_0_), channel_id=1, source_target_pairs={{0,4},{1,5},{2,6},{3,7},{4,0},{5,1},{6,2},{7,3},{8,12},{9,13},{10,... | collective-permute-start | bytes 442376 | tf_op jit(solution)/shard_map/ppermute | solution.py:381
  116.5 6.7 %collective-permute-start.46 = (f32[96,384]{1,0:T(8,128)S(1)}, f32[96,384]{1,0:T(8,128)S(1)}, u32[]{:S(2)}, u32[]{:S(2)}) collective-permute-start(f32[96,384]{1,0:T(8,128)S(1)} %get-tuple-element.108.refs_0_), channel_id=1, source_target_pairs={{0,12},{1,13},{2,14},{3,15},{4,8},{5,9},{6,10},{7,11},{8,4},{9,5},... | collective-permute-start | bytes 442376 | tf_op jit(solution)/shard_map/ppermute | solution.py:381
  (30 other events, 132.9 us)

commit v5 on v3

--- a/solution.py
+++ b/solution.py
@@ -24,7 +24,7 @@
 DIMS = (("sector", 1), ("term", 0), ("term", 1))
 CORE = ("sector", 0)
 ORDERS = ((0, 1, 2), (2, 1, 0))
-START_ORDER = (4, 2, 1, 6, 5, 3, 7)
+START_ORDER = (6, 5, 4, 2, 1, 3)
 
 
 def matmul_cost(pairs, rows, b):
@@ -285,6 +285,20 @@
         out_shape=jax.ShapeDtypeStruct(parts[0].shape, F32),
         compiler_params=grant(4),
     )(*parts)
+
+
+def pick_kernel(even_ref, odd_ref, out_ref):
+    out_ref[...] = jnp.where(bit_of(*CORE) == 0, even_ref[...], odd_ref[...])
+
+
+def pick(even, odd):
+    return pl.pallas_call(
+        pick_kernel,
+        in_specs=[VMEM] * 2,
+        out_specs=VMEM,
+        out_shape=jax.ShapeDtypeStruct(even.shape, F32),
+        compiler_params=grant(4),
+    )(even, odd)
 
 
 def update_kernel(*refs):
@@ -430,6 +444,8 @@
             zero = zero_tile(energy)
             for k in away:
                 got[k] = swap(vec, dims_of(k))
+            near = pick(got[5], got[6])
+            got[7] = swap(near, [DIMS[1]], [DIMS[2]])
             pieces = []
             for k in range(8):
                 pieces += [got[k], swap(got[k], [CORE])]

time: 123 us -> 121 us (0.984)
  waiting for transfers between devices: 41.4 us -> 34.2 us
  starting transfers between devices: 46.9 us -> 51.8 us
    ppermute x47, waiting for transfers between devices: 41.4 us -> 34.2 us  [swap(): lax.ppermute(x, AXES, flips(mesh_shape, even, even if odd is None else odd))]
    ppermute x47, starting transfers between devices: 46.9 us -> 51.8 us  [swap(): lax.ppermute(x, AXES, flips(mesh_shape, even, even if odd is None else odd))]
  transfers between devices with their start and end apart: 47 -> 47, of which waited for: 24 -> 21; matrix products, arithmetic and copies ran while one was open for 2% -> 2% of each run, Pallas kernels for 4% -> 4%
where the time goes in v5:
time: 121 us; the launch traced here: 120 us
  starting transfers between devices  51.8 us (43%)
  waiting for transfers between devices  34.2 us (28%)
  Pallas kernels  23.4 us (19%)
  local copies, waits for them, and re-layouts  7.67 us (6%)
  other arithmetic  1.85 us (2%)
  between operations  1.55 us (1%)
    ppermute x47, starting transfers between devices, swap(): lax.ppermute(x, AXES, flips(mesh_shape, even, even if odd is None else odd))  51.8 us
    ppermute x47, waiting for transfers between devices, swap(): lax.ppermute(x, AXES, flips(mesh_shape, even, even if odd is None else odd))  34.2 us
    pallas_call x4, Pallas kernels, outer(): pl.pallas_call(functools.partial(outer_kernel, first, chunk, cells, len(p...  11.1 us
    pallas_call x3, Pallas kernels, inner(): pl.pallas_call(functools.partial(inner_kernel, first, half, cells, len(pi...  9.73 us
    unnamed x14, local copies, waits for them, and re-layouts  5.47 us
  transfers between devices with their start and end apart: 47, of which 21 were waited for; matrix products, arithmetic and copies ran while one was open for 2% of the time, Pallas kernels for 4%

profile of v5, /device:TPU:0, one launch (start us, length us, event | category | flops | bytes accessed | tf_op | source)
XLA Modules:
  0.0 120.5 jit_solution(4734709911100900846)
XLA Ops:
  1.8 3.1 %collective-permute-start.1 = (f32[192,384]{1,0:T(8,128)S(1)}, f32[192,384]{1,0:T(8,128)S(1)}, u32[]{:S(2)}, u32[]{:S(2)}) collective-permute-start(f32[192,384]{1,0:T(8,128)S(1)} %get-tuple-element.111), channel_id=1, source_target_pairs={{0,2},{1,3},{2,0},{3,1},{4,6},{5,7},{6,4},{7,5},{8,10},{9,11},{10,... | collective-permute-start | bytes 884744 | tf_op jit(solution)/shard_map/ppermute | solution.py:386
  12.7 5.5 %collective-permute-done.3.refs_4_.refs_6_ = f32[192,384]{1,0:T(8,128)S(1)} collective-permute-done((f32[192,384]{1,0:T(8,128)S(1)}, f32[192,384]{1,0:T(8,128)S(1)}, u32[]{:S(2)}, u32[]{:S(2)}) %collective-permute-start.3) | collective-permute-done | bytes 294944 | tf_op jit(solution)/shard_map/ppermute | solution.py:386
  18.9 2.9 %shard_map.87 = (bf16[4,192,384]{2,1,0:T(8,128)(2,1)S(1)}, bf16[4,192,384]{2,1,0:T(8,128)(2,1)S(1)}, f32[8,384]{1,0:T(8,128)S(1)}) custom-call(s32[1,4]{1,0:T(1,128)S(1)} %copy-done.6, s32[1]{0:T(128)S(6)} %copy.9.refs_1_, f32[384,384]{1,0:T(8,128)S(1)} %bitcast.8, f32[384,384]{1,0:T(8,128)S(1)} %collective-permute-done.refs_3_, ...), custom_call_target="tpu_custom_call" | custom-call | flops 679477248 | bytes 4718592 | tf_op jit(solution)/shard_map/pallas_call | solution.py:182
  21.8 3.0 %shard_map.88 = (bf16[4,1152,384]{2,1,0:T(8,128)(2,1)S(1)}, f32[8,384]{1,0:T(8,128)S(1)}) custom-call(s32[1,4]{1,0:T(1,128)S(1)} %copy-done.6, s32[1]{0:T(128)S(6)} %copy.9.refs_1_, f32[384,384]{1,0:T(8,128)S(1)} %bitcast.9, f32[384,384]{1,0:T(8,128)S(1)} %collective-permute-done.refs_3_, f32[192,384]{1,0:T(8,128)S(1)} %collective-permute-done.3.refs_4_.refs_6_, ...), custom_call_target="tpu_custom_call" | custom-call | flops 679477248 | bytes 4718592 | tf_op jit(solution)/shard_map/pallas_call | solution.py:182
  24.8 2.5 %shard_map.89 = (f32[1152,128]{1,0:T(8,128)S(1)}, f32[1152,128]{1,0:T(8,128)S(1)}, f32[8,128]{1,0:T(8,128)S(1)}) custom-call(s32[1,4]{1,0:T(1,128)S(1)} %copy-done.5, s32[1]{0:T(128)S(6)} %copy.9.refs_1_, f32[384,384]{1,0:T(8,128)S(1)} %bitcast.10, f32[384,384]{1,0:T(8,128)S(1)} %collective-permute-done.refs_3_, ...), custom_call_target="tpu_custom_call" | custom-call | flops 679477248 | bytes 4718592 | tf_op jit(solution)/shard_map/pallas_call | solution.py:241
  27.3 3.1 %shard_map.93 = (f32[1160,128]{1,0:T(8,128)S(1)}, f32[1160,128]{1,0:T(8,128)S(1)}, f32[8,128]{1,0:T(8,128)}) custom-call(s32[1,4]{1,0:T(1,128)S(1)} %copy-done.5, s32[1]{0:T(128)S(6)} %copy.9.refs_1_, f32[384,384]{1,0:T(8,128)S(1)} %bitcast.11, f32[384,384]{1,0:T(8,128)S(1)} %collective-permute-done.refs_3_, f32[192,384]{1,0:T(8,128)S(1)} %collective-permute-done.1.refs_4_, ...), custom_call_target="tpu_custom_call" | custom-call | flops 679477248 | bytes 4718592 | tf_op jit(solution)/shard_map/pallas_call | solution.py:241
  34.6 4.6 %collective-permute-done.12.recv_ref = f32[584,128]{1,0:T(8,128)S(1)} collective-permute-done((f32[584,128]{1,0:T(8,128)S(1)}, f32[584,128]{1,0:T(8,128)S(1)}, u32[]{:S(2)}, u32[]{:S(2)}) %collective-permute-start.12) | collective-permute-done | bytes 299040 | tf_op jit(solution)/shard_map/ppermute | solution.py:386
  39.3 2.9 %collective-permute-start.13 = (f32[152,128]{1,0:T(8,128)S(1)}, f32[152,128]{1,0:T(8,128)S(1)}, u32[]{:S(2)}, u32[]{:S(2)}) collective-permute-start(f32[152,128]{1,0:T(8,128)S(1)} %get-tuple-element.82), channel_id=1, source_target_pairs={{0,12},{1,7},{2,14},{3,5},{4,8},{5,3},{6,10},{7,1},{8,4},{9,15},{1... | collective-permute-start | bytes 233480 | tf_op jit(solution)/shard_map/ppermute | solution.py:386
  42.9 2.9 %collective-permute-start.7 = (f32[144,128]{1,0:T(8,128)S(1)}, f32[144,128]{1,0:T(8,128)S(1)}, u32[]{:S(2)}, u32[]{:S(2)}) collective-permute-start(f32[144,128]{1,0:T(8,128)S(1)} %get-tuple-element.73), channel_id=1, source_target_pairs={{0,12},{1,7},{2,14},{3,5},{4,8},{5,3},{6,10},{7,1},{8,4},{9,15},{1... | collective-permute-start | bytes 221192 | tf_op jit(solution)/shard_map/ppermute | solution.py:386
  47.5 2.5 %collective-permute-start.16 = (f32[152,128]{1,0:T(8,128)S(1)}, f32[152,128]{1,0:T(8,128)S(1)}, u32[]{:S(2)}, u32[]{:S(2)}) collective-permute-start(f32[152,128]{1,0:T(8,128)S(1)} %shard_map.96.refs_2_), channel_id=1, source_target_pairs={{0,16},{1,17},{2,18},{3,19},{4,20},{5,21},{6,22},{7,23},{8,24},{9,... | collective-permute-start | bytes 233480 | tf_op jit(solution)/shard_map/ppermute | solution.py:386
  50.7 3.5 %collective-permute-start.10 = (f32[144,128]{1,0:T(8,128)S(1)}, f32[144,128]{1,0:T(8,128)S(1)}, u32[]{:S(2)}, u32[]{:S(2)}) collective-permute-start(f32[144,128]{1,0:T(8,128)S(1)} %shard_map.92.refs_0_), channel_id=1, source_target_pairs={{0,16},{1,17},{2,18},{3,19},{4,20},{5,21},{6,22},{7,23},{8,24},{9,... | collective-permute-start | bytes 221192 | tf_op jit(solution)/shard_map/ppermute | solution.py:386
  54.3 3.0 %collective-permute-done.10.refs_1_ = f32[144,128]{1,0:T(8,128)S(1)} collective-permute-done((f32[144,128]{1,0:T(8,128)S(1)}, f32[144,128]{1,0:T(8,128)S(1)}, u32[]{:S(2)}, u32[]{:S(2)}) %collective-permute-start.10) | collective-permute-done | bytes 73760 | tf_op jit(solution)/shard_map/ppermute | solution.py:386
  58.7 1.9 %collective-permute-start.26 = (f32[96,384]{1,0:T(8,128)S(1)}, f32[96,384]{1,0:T(8,128)S(1)}, u32[]{:S(2)}, u32[]{:S(2)}) collective-permute-start(f32[96,384]{1,0:T(8,128)S(1)} %get-tuple-element.87.refs_2_.refs_4_), channel_id=1, source_target_pairs={{0,10},{1,11},{2,8},{3,9},{4,14},{5,15},{6,12},{7,13},{8,2},{9,3},... | collective-permute-start | bytes 442376 | tf_op jit(solution)/shard_map/ppermute | solution.py:386
  67.0 4.9 %collective-permute-start.30 = (f32[96,384]{1,0:T(8,128)S(1)}, f32[96,384]{1,0:T(8,128)S(1)}, u32[]{:S(2)}, u32[]{:S(2)}) collective-permute-start(f32[96,384]{1,0:T(8,128)S(1)} %shard_map.98), channel_id=1, source_target_pairs={{0,4},{1,9},{2,6},{3,11},{4,0},{5,13},{6,2},{7,15},{8,12},{9,1},{1... | collective-permute-start | bytes 442376 | tf_op jit(solution)/shard_map/ppermute | solution.py:386
  73.0 2.1 %collective-permute-done.30.refs_16_ = f32[96,384]{1,0:T(8,128)S(1)} collective-permute-done((f32[96,384]{1,0:T(8,128)S(1)}, f32[96,384]{1,0:T(8,128)S(1)}, u32[]{:S(2)}, u32[]{:S(2)}) %collective-permute-start.30) | collective-permute-done | bytes 147488 | tf_op jit(solution)/shard_map/ppermute | solution.py:386
  76.4 3.9 %shard_map.99 = (bf16[4,1152,384]{2,1,0:T(8,128)(2,1)S(1)}, f32[8,384]{1,0:T(8,128)S(1)}) custom-call(s32[1,4]{1,0:T(1,128)S(1)} %copy-done.6, s32[1]{0:T(128)S(6)} %copy.9.refs_1_, f32[96,384]{1,0:T(8,128)S(1)} %get-tuple-element.87.refs_2_.refs_4_, f32[96,384]{1,0:T(8,128)S(1)} %collective-permute-done.17.refs_3_, ...), custom_call_target="tpu_custom_call" | custom-call | flops 1358954496 | bytes 4718592 | tf_op jit(solution)/shard_map/pallas_call | solution.py:182
  80.3 2.5 %shard_map.101 = (f32[1152,128]{1,0:T(8,128)S(1)}, f32[1152,128]{1,0:T(8,128)S(1)}, f32[8,128]{1,0:T(8,128)S(1)}) custom-call(s32[1,4]{1,0:T(1,128)S(1)} %copy-done.5, s32[1]{0:T(128)S(6)} %copy.9.refs_1_, f32[96,384]{1,0:T(8,128)S(1)} %get-tuple-element.87.refs_2_.refs_4_, f32[96,384]{1,0:T(8,128)S(1)} %collective-permute-done.17.refs_3_, ...), custom_call_target="tpu_custom_call" | custom-call | flops 679477248 | bytes 4718592 | tf_op jit(solution)/shard_map/pallas_call | solution.py:241
  82.8 3.1 %shard_map.105 = (f32[1160,128]{1,0:T(8,128)S(1)}, f32[1160,128]{1,0:T(8,128)S(1)}, f32[8,128]{1,0:T(8,128)}) custom-call(s32[1,4]{1,0:T(1,128)S(1)} %copy-done.5, s32[1]{0:T(128)S(6)} %copy.9.refs_1_, f32[96,384]{1,0:T(8,128)S(1)} %get-tuple-element.87.refs_2_.refs_4_, f32[96,384]{1,0:T(8,128)S(1)} %collective-permute-done.17.refs_3_, ...), custom_call_target="tpu_custom_call" | custom-call | flops 679477248 | bytes 4718592 | tf_op jit(solution)/shard_map/pallas_call | solution.py:241
  90.2 4.6 %collective-permute-done.39.recv_ref = f32[584,128]{1,0:T(8,128)S(1)} collective-permute-done((f32[584,128]{1,0:T(8,128)S(1)}, f32[584,128]{1,0:T(8,128)S(1)}, u32[]{:S(2)}, u32[]{:S(2)}) %collective-permute-start.39) | collective-permute-done | bytes 299040 | tf_op jit(solution)/shard_map/ppermute | solution.py:386
  102.6 2.6 %collective-permute-start.43 = (f32[152,128]{1,0:T(8,128)S(1)}, f32[152,128]{1,0:T(8,128)S(1)}, u32[]{:S(2)}, u32[]{:S(2)}) collective-permute-start(f32[152,128]{1,0:T(8,128)S(1)} %shard_map.108.refs_2_), channel_id=1, source_target_pairs={{0,16},{1,17},{2,18},{3,19},{4,20},{5,21},{6,22},{7,23},{8,24},{9,... | collective-permute-start | bytes 233480 | tf_op jit(solution)/shard_map/ppermute | solution.py:386
  105.6 4.2 %collective-permute-start.37 = (f32[144,128]{1,0:T(8,128)S(1)}, f32[144,128]{1,0:T(8,128)S(1)}, u32[]{:S(2)}, u32[]{:S(2)}) collective-permute-start(f32[144,128]{1,0:T(8,128)S(1)} %shard_map.104.refs_0_), channel_id=1, source_target_pairs={{0,16},{1,17},{2,18},{3,19},{4,20},{5,21},{6,22},{7,23},{8,24},{9,... | collective-permute-start | bytes 221192 | tf_op jit(solution)/shard_map/ppermute | solution.py:386
  109.8 2.9 %collective-permute-done.37.refs_1_ = f32[144,128]{1,0:T(8,128)S(1)} collective-permute-done((f32[144,128]{1,0:T(8,128)S(1)}, f32[144,128]{1,0:T(8,128)S(1)}, u32[]{:S(2)}, u32[]{:S(2)}) %collective-permute-start.37) | collective-permute-done | bytes 73760 | tf_op jit(solution)/shard_map/ppermute | solution.py:386
  113.4 2.9 %collective-permute-start.46 = (f32[96,384]{1,0:T(8,128)S(1)}, f32[96,384]{1,0:T(8,128)S(1)}, u32[]{:S(2)}, u32[]{:S(2)}) collective-permute-start(f32[96,384]{1,0:T(8,128)S(1)} %get-tuple-element.108.refs_0_), channel_id=1, source_target_pairs={{0,12},{1,13},{2,14},{3,15},{4,8},{5,9},{6,10},{7,11},{8,4},{9,5},... | collective-permute-start | bytes 442376 | tf_op jit(solution)/shard_map/ppermute | solution.py:386
  117.3 1.8 %pad_maximum_fusion = f32[2]{0:T(128)} fusion(f32[1]{0:T(128)} %bitcast.4, f32[1]{0:T(128)} %bitcast.3), kind=kLoop, calls=%fused_computation.2 | loop fusion | flops 2 | bytes 16 | tf_op jit(solution)/shard_map/stack | solution.py:454
  (114 shorter events, 42.3 us)
Async XLA Ops:
  1.8 10.9 %collective-permute-start.1 = (f32[192,384]{1,0:T(8,128)S(1)}, f32[192,384]{1,0:T(8,128)S(1)}, u32[]{:S(2)}, u32[]{:S(2)}) collective-permute-start(f32[192,384]{1,0:T(8,128)S(1)} %get-tuple-element.111), channel_id=1, source_target_pairs={{0,2},{1,3},{2,0},{3,1},{4,6},{5,7},{6,4},{7,5},{8,10},{9,11},{10,... | collective-permute-start | bytes 884744 | tf_op jit(solution)/shard_map/ppermute | solution.py:386
  4.9 14.0 %collective-permute-start = (f32[384,384]{1,0:T(8,128)}, f32[384,384]{1,0:T(8,128)S(1)}, u32[]{:S(2)}, u32[]{:S(2)}) collective-permute-start(f32[384,384]{1,0:T(8,128)} %bitcast.7), channel_id=1, source_target_pairs={{0,1},{1,0},{2,3},{3,2},{4,5},{5,4},{6,7},{7,6},{8,9},{9,8},{10,11... | collective-permute-start | bytes 1769480 | tf_op jit(solution)/shard_map/ppermute | solution.py:386
  4.9 13.3 %collective-permute-start.3 = (f32[192,384]{1,0:T(8,128)S(1)}, f32[192,384]{1,0:T(8,128)S(1)}, u32[]{:S(2)}, u32[]{:S(2)}) collective-permute-start(f32[192,384]{1,0:T(8,128)S(1)} %get-tuple-element.110), channel_id=1, source_target_pairs={{0,2},{1,3},{2,0},{3,1},{4,6},{5,7},{6,4},{7,5},{8,10},{9,11},{10,... | collective-permute-start | bytes 884744 | tf_op jit(solution)/shard_map/ppermute | solution.py:386
  32.4 6.8 %collective-permute-start.12 = (f32[584,128]{1,0:T(8,128)S(1)}, f32[584,128]{1,0:T(8,128)S(1)}, u32[]{:S(2)}, u32[]{:S(2)}) collective-permute-start(f32[584,128]{1,0:T(8,128)S(1)} %get-tuple-element.80), channel_id=1, source_target_pairs={{0,2},{1,9},{2,0},{3,11},{4,6},{5,13},{6,4},{7,15},{8,10},{9,1},{1... | collective-permute-start | bytes 897032 | tf_op jit(solution)/shard_map/ppermute | solution.py:386
  33.2 9.6 %collective-permute-start.6 = (f32[576,128]{1,0:T(8,128)S(1)}, f32[576,128]{1,0:T(8,128)S(1)}, u32[]{:S(2)}, u32[]{:S(2)}) collective-permute-start(f32[576,128]{1,0:T(8,128)S(1)} %get-tuple-element.71), channel_id=1, source_target_pairs={{0,2},{1,9},{2,0},{3,11},{4,6},{5,13},{6,4},{7,15},{8,10},{9,1},{1... | collective-permute-start | bytes 884744 | tf_op jit(solution)/shard_map/ppermute | solution.py:386
  39.3 7.1 %collective-permute-start.13 = (f32[152,128]{1,0:T(8,128)S(1)}, f32[152,128]{1,0:T(8,128)S(1)}, u32[]{:S(2)}, u32[]{:S(2)}) collective-permute-start(f32[152,128]{1,0:T(8,128)S(1)} %get-tuple-element.82), channel_id=1, source_target_pairs={{0,12},{1,7},{2,14},{3,5},{4,8},{5,3},{6,10},{7,1},{8,4},{9,15},{1... | collective-permute-start | bytes 233480 | tf_op jit(solution)/shard_map/ppermute | solution.py:386
  42.9 7.1 %collective-permute-start.7 = (f32[144,128]{1,0:T(8,128)S(1)}, f32[144,128]{1,0:T(8,128)S(1)}, u32[]{:S(2)}, u32[]{:S(2)}) collective-permute-start(f32[144,128]{1,0:T(8,128)S(1)} %get-tuple-element.73), channel_id=1, source_target_pairs={{0,12},{1,7},{2,14},{3,5},{4,8},{5,3},{6,10},{7,1},{8,4},{9,15},{1... | collective-permute-start | bytes 221192 | tf_op jit(solution)/shard_map/ppermute | solution.py:386
  47.5 9.8 %collective-permute-start.16 = (f32[152,128]{1,0:T(8,128)S(1)}, f32[152,128]{1,0:T(8,128)S(1)}, u32[]{:S(2)}, u32[]{:S(2)}) collective-permute-start(f32[152,128]{1,0:T(8,128)S(1)} %shard_map.96.refs_2_), channel_id=1, source_target_pairs={{0,16},{1,17},{2,18},{3,19},{4,20},{5,21},{6,22},{7,23},{8,24},{9,... | collective-permute-start | bytes 233480 | tf_op jit(solution)/shard_map/ppermute | solution.py:386
  50.7 6.5 %collective-permute-start.10 = (f32[144,128]{1,0:T(8,128)S(1)}, f32[144,128]{1,0:T(8,128)S(1)}, u32[]{:S(2)}, u32[]{:S(2)}) collective-permute-start(f32[144,128]{1,0:T(8,128)S(1)} %shard_map.92.refs_0_), channel_id=1, source_target_pairs={{0,16},{1,17},{2,18},{3,19},{4,20},{5,21},{6,22},{7,23},{8,24},{9,... | collective-permute-start | bytes 221192 | tf_op jit(solution)/shard_map/ppermute | solution.py:386
  57.4 6.3 %collective-permute-start.20 = (f32[96,384]{1,0:T(8,128)S(1)}, f32[96,384]{1,0:T(8,128)S(1)}, u32[]{:S(2)}, u32[]{:S(2)}) collective-permute-start(f32[96,384]{1,0:T(8,128)S(1)} %get-tuple-element.87.refs_2_.refs_4_), channel_id=1, source_target_pairs={{0,4},{1,5},{2,6},{3,7},{4,0},{5,1},{6,2},{7,3},{8,12},{9,13},{10,... | collective-permute-start | bytes 442376 | tf_op jit(solution)/shard_map/ppermute | solution.py:386
  58.7 6.8 %collective-permute-start.26 = (f32[96,384]{1,0:T(8,128)S(1)}, f32[96,384]{1,0:T(8,128)S(1)}, u32[]{:S(2)}, u32[]{:S(2)}) collective-permute-start(f32[96,384]{1,0:T(8,128)S(1)} %get-tuple-element.87.refs_2_.refs_4_), channel_id=1, source_target_pairs={{0,10},{1,11},{2,8},{3,9},{4,14},{5,15},{6,12},{7,13},{8,2},{9,3},... | collective-permute-start | bytes 442376 | tf_op jit(solution)/shard_map/ppermute | solution.py:386
  60.6 6.4 %collective-permute-start.28 = (f32[96,384]{1,0:T(8,128)S(1)}, f32[96,384]{1,0:T(8,128)S(1)}, u32[]{:S(2)}, u32[]{:S(2)}) collective-permute-start(f32[96,384]{1,0:T(8,128)S(1)} %get-tuple-element.87.refs_2_.refs_4_), channel_id=1, source_target_pairs={{0,6},{1,7},{2,4},{3,5},{4,2},{5,3},{6,0},{7,1},{8,14},{9,15},{10,... | collective-permute-start | bytes 442376 | tf_op jit(solution)/shard_map/ppermute | solution.py:386
  62.6 9.4 %collective-permute-start.22 = (f32[96,384]{1,0:T(8,128)S(1)}, f32[96,384]{1,0:T(8,128)S(1)}, u32[]{:S(2)}, u32[]{:S(2)}) collective-permute-start(f32[96,384]{1,0:T(8,128)S(1)} %get-tuple-element.87.refs_2_.refs_4_), channel_id=1, source_target_pairs={{0,12},{1,13},{2,14},{3,15},{4,8},{5,9},{6,10},{7,11},{8,4},{9,5},... | collective-permute-start | bytes 442376 | tf_op jit(solution)/shard_map/ppermute | solution.py:386
  63.8 8.2 %collective-permute-start.24 = (f32[96,384]{1,0:T(8,128)S(1)}, f32[96,384]{1,0:T(8,128)S(1)}, u32[]{:S(2)}, u32[]{:S(2)}) collective-permute-start(f32[96,384]{1,0:T(8,128)S(1)} %get-tuple-element.87.refs_2_.refs_4_), channel_id=1, source_target_pairs={{0,2},{1,3},{2,0},{3,1},{4,6},{5,7},{6,4},{7,5},{8,10},{9,11},{10,... | collective-permute-start | bytes 442376 | tf_op jit(solution)/shard_map/ppermute | solution.py:386
  65.5 6.9 %collective-permute-start.19 = (f32[96,384]{1,0:T(8,128)S(1)}, f32[96,384]{1,0:T(8,128)S(1)}, u32[]{:S(2)}, u32[]{:S(2)}) collective-permute-start(f32[96,384]{1,0:T(8,128)S(1)} %collective-permute-done.18.refs_4_), channel_id=1, source_target_pairs={{0,1},{1,0},{2,3},{3,2},{4,5},{5,4},{6,7},{7,6},{8,9},{9,8},{10,11... | collective-permute-start | bytes 442376 | tf_op jit(solution)/shard_map/ppermute | solution.py:386
  67.0 8.0 %collective-permute-start.30 = (f32[96,384]{1,0:T(8,128)S(1)}, f32[96,384]{1,0:T(8,128)S(1)}, u32[]{:S(2)}, u32[]{:S(2)}) collective-permute-start(f32[96,384]{1,0:T(8,128)S(1)} %shard_map.98), channel_id=1, source_target_pairs={{0,4},{1,9},{2,6},{3,11},{4,0},{5,13},{6,2},{7,15},{8,12},{9,1},{1... | collective-permute-start | bytes 442376 | tf_op jit(solution)/shard_map/ppermute | solution.py:386
  88.0 6.8 %collective-permute-start.39 = (f32[584,128]{1,0:T(8,128)S(1)}, f32[584,128]{1,0:T(8,128)S(1)}, u32[]{:S(2)}, u32[]{:S(2)}) collective-permute-start(f32[584,128]{1,0:T(8,128)S(1)} %get-tuple-element.103), channel_id=1, source_target_pairs={{0,2},{1,9},{2,0},{3,11},{4,6},{5,13},{6,4},{7,15},{8,10},{9,1},{1... | collective-permute-start | bytes 897032 | tf_op jit(solution)/shard_map/ppermute | solution.py:386
  88.8 10.2 %collective-permute-start.33 = (f32[576,128]{1,0:T(8,128)S(1)}, f32[576,128]{1,0:T(8,128)S(1)}, u32[]{:S(2)}, u32[]{:S(2)}) collective-permute-start(f32[576,128]{1,0:T(8,128)S(1)} %get-tuple-element.94), channel_id=1, source_target_pairs={{0,2},{1,9},{2,0},{3,11},{4,6},{5,13},{6,4},{7,15},{8,10},{9,1},{1... | collective-permute-start | bytes 884744 | tf_op jit(solution)/shard_map/ppermute | solution.py:386
  94.8 6.4 %collective-permute-start.40 = (f32[152,128]{1,0:T(8,128)S(1)}, f32[152,128]{1,0:T(8,128)S(1)}, u32[]{:S(2)}, u32[]{:S(2)}) collective-permute-start(f32[152,128]{1,0:T(8,128)S(1)} %get-tuple-element.105), channel_id=1, source_target_pairs={{0,12},{1,7},{2,14},{3,5},{4,8},{5,3},{6,10},{7,1},{8,4},{9,15},{1... | collective-permute-start | bytes 233480 | tf_op jit(solution)/shard_map/ppermute | solution.py:386
  102.6 10.1 %collective-permute-start.43 = (f32[152,128]{1,0:T(8,128)S(1)}, f32[152,128]{1,0:T(8,128)S(1)}, u32[]{:S(2)}, u32[]{:S(2)}) collective-permute-start(f32[152,128]{1,0:T(8,128)S(1)} %shard_map.108.refs_2_), channel_id=1, source_target_pairs={{0,16},{1,17},{2,18},{3,19},{4,20},{5,21},{6,22},{7,23},{8,24},{9,... | collective-permute-start | bytes 233480 | tf_op jit(solution)/shard_map/ppermute | solution.py:386
  105.6 7.0 %collective-permute-start.37 = (f32[144,128]{1,0:T(8,128)S(1)}, f32[144,128]{1,0:T(8,128)S(1)}, u32[]{:S(2)}, u32[]{:S(2)}) collective-permute-start(f32[144,128]{1,0:T(8,128)S(1)} %shard_map.104.refs_0_), channel_id=1, source_target_pairs={{0,16},{1,17},{2,18},{3,19},{4,20},{5,21},{6,22},{7,23},{8,24},{9,... | collective-permute-start | bytes 221192 | tf_op jit(solution)/shard_map/ppermute | solution.py:386
  112.7 6.4 %collective-permute-start.44 = (f32[96,384]{1,0:T(8,128)S(1)}, f32[96,384]{1,0:T(8,128)S(1)}, u32[]{:S(2)}, u32[]{:S(2)}) collective-permute-start(f32[96,384]{1,0:T(8,128)S(1)} %get-tuple-element.108.refs_0_), channel_id=1, source_target_pairs={{0,8},{1,9},{2,10},{3,11},{4,12},{5,13},{6,14},{7,15},{8,0},{9,1},... | collective-permute-start | bytes 442376 | tf_op jit(solution)/shard_map/ppermute | solution.py:386
  112.8 6.4 %collective-permute-start.45 = (f32[96,384]{1,0:T(8,128)S(1)}, f32[96,384]{1,0:T(8,128)S(1)}, u32[]{:S(2)}, u32[]{:S(2)}) collective-permute-start(f32[96,384]{1,0:T(8,128)S(1)} %get-tuple-element.108.refs_0_), channel_id=1, source_target_pairs={{0,4},{1,5},{2,6},{3,7},{4,0},{5,1},{6,2},{7,3},{8,12},{9,13},{10,... | collective-permute-start | bytes 442376 | tf_op jit(solution)/shard_map/ppermute | solution.py:386
  113.4 6.2 %collective-permute-start.46 = (f32[96,384]{1,0:T(8,128)S(1)}, f32[96,384]{1,0:T(8,128)S(1)}, u32[]{:S(2)}, u32[]{:S(2)}) collective-permute-start(f32[96,384]{1,0:T(8,128)S(1)} %get-tuple-element.108.refs_0_), channel_id=1, source_target_pairs={{0,12},{1,13},{2,14},{3,15},{4,8},{5,9},{6,10},{7,11},{8,4},{9,5},... | collective-permute-start | bytes 442376 | tf_op jit(solution)/shard_map/ppermute | solution.py:386
  (30 other events, 137.8 us)

commit v6 on v5

--- a/solution.py
+++ b/solution.py
@@ -23,7 +23,7 @@
 
 DIMS = (("sector", 1), ("term", 0), ("term", 1))
 CORE = ("sector", 0)
-ORDERS = ((0, 1, 2), (2, 1, 0))
+ORDERS = (((0, 1, 2), (2, 1, 0)), ((1, 0, 2), (2, 1, 0)))
 START_ORDER = (6, 5, 4, 2, 1, 3)
 
 
@@ -49,8 +49,8 @@
     return place([bit_of(*dim) ^ ((k >> (2 - i)) & 1) for i, dim in enumerate(DIMS)], parity, rows)
 
 
-def slot_of(parity, masks):
-    a, b = (sum(masks[dim] << (2 - i) for i, dim in enumerate(order)) for order in ORDERS)
+def slot_of(chunk, parity, masks):
+    a, b = (sum(masks[dim] << (2 - i) for i, dim in enumerate(order)) for order in ORDERS[chunk])
     return jnp.where(parity == 0, a, b)
 
 
@@ -223,7 +223,7 @@
                     masks = tuple((number >> (3 - i)) & 1 for i in range(3))
                     here = pl.ds(row, shard)
                 x = acc[sector, here, :] * scale
-                slot = slot_of(core ^ side, masks)
+                slot = slot_of(chunk, core ^ side, masks)
                 store_wide(dest, pl.multiple_of(slot * wide, 8), x)
                 rho += jnp.sum(x * piece[start + q * shard:start + (q + 1) * shard, :], axis=0, keepdims=True)
     rho = jnp.broadcast_to(jnp.sum(rho * scale, axis=1, keepdims=True), TILE) / cells + before_ref[...]
@@ -331,6 +331,23 @@
     )(*sums, vec, inv, diag)
 
 
+def take_kernel(first, x_ref, out_ref, sem):
+    copy = pltpu.make_async_copy(x_ref.at[0, pl.ds(first, out_ref.shape[0]), :], out_ref, sem)
+    copy.start()
+    copy.wait()
+
+
+def take(x, first, rows):
+    return pl.pallas_call(
+        functools.partial(take_kernel, first),
+        in_specs=[pl.BlockSpec(memory_space=pl.ANY)],
+        out_specs=VMEM,
+        out_shape=jax.ShapeDtypeStruct((rows, x.shape[-1]), x.dtype),
+        scratch_shapes=[pltpu.SemaphoreType.DMA],
+        compiler_params=grant(4),
+    )(x)
+
+
 def zero_tile(tile):
     def kernel(in_ref, out_ref):
         out_ref[...] = jnp.zeros_like(out_ref)
@@ -395,7 +412,7 @@
     rows = b // CHUNKS
     far = []
     for h in range(CHUNKS):
-        far.append(swap(own[h * rows:(h + 1) * rows], [DIMS[0]]))
+        far.append(swap(take(psi_start, h * rows, rows), [DIMS[0]]))
     beside = swap(own, [CORE])
     left, right, vec, diag = prepare(left_ops, right_ops, psi_start, diagonal)
     far[0], left, right, vec, diag = lax.optimization_barrier((far[0], left, right, vec, diag))
@@ -419,16 +436,17 @@
             send, keep, rho = outer(first, h, cells, sectors, pair_out, pair_count, pieces, (left, cat), inv, rho)
             keeps.append(keep)
             recvs.append(swap(send, [CORE]))
-        first_dims, second, third = ([[DIMS[dim]] for dim in step] for step in zip(*ORDERS))
+        orders = [[[[DIMS[dim]] for dim in step] for step in zip(*order)] for order in ORDERS]
         for h in range(CHUNKS):
             extra = TILE[0] if h == CHUNKS - 1 else 0
             keeps[h], send = cut(keeps[h], recvs[h], extra, 2)
-            recvs[h] = swap(send, *first_dims)
-        both = [a + b for a, b in zip(second, third)]
+            recvs[h] = swap(send, *orders[h][0])
         for h in range(CHUNKS):
             extra = TILE[0] if h == CHUNKS - 1 else 0
             slots = cut(keeps[h], recvs[h], extra, 4)
             parts = [slots[0]]
+            _, second, third = orders[h]
+            both = [a + b for a, b in zip(second, third)]
             for k, dims in ((3, both), (2, second), (1, third)):
                 parts.append(swap(slots[k], *dims))
             keeps[h] = parts

time: 121 us -> 125 us (1.033)
  waiting for transfers between devices: 34.2 us -> 42.8 us
  starting transfers between devices: 51.8 us -> 43.9 us
  Pallas kernels: 23.4 us -> 28.5 us
  local copies, waits for them, and re-layouts: 7.67 us -> 5.49 us
    ppermute x47, waiting for transfers between devices: 34.2 us -> 42.8 us  [swap(): lax.ppermute(x, AXES, flips(mesh_shape, even, even if odd is None else odd))]
    ppermute x47, starting transfers between devices: 51.8 us -> 43.9 us  [swap(): lax.ppermute(x, AXES, flips(mesh_shape, even, even if odd is None else odd))]
    pallas_call x0 -> x2, Pallas kernels: none -> 1.94 us  [take(): pl.pallas_call(functools.partial(take_kernel, first), in_specs=[pl.BlockS...]
    unnamed x14 -> x10, local copies, waits for them, and re-layouts: 5.47 us -> 4.41 us
  transfers between devices with their start and end apart: 47 -> 47, of which waited for: 21 -> 22; matrix products, arithmetic and copies ran while one was open for 2% -> 2% of each run, Pallas kernels for 4% -> 6%
where the time goes in v6:
time: 125 us; the launch traced here: 124 us
  starting transfers between devices  43.9 us (35%)
  waiting for transfers between devices  42.8 us (34%)
  Pallas kernels  28.5 us (23%)
  local copies, waits for them, and re-layouts  5.49 us (4%)
  other arithmetic  1.85 us (1%)
  between operations  1.55 us (1%)
    ppermute x47, starting transfers between devices, swap(): lax.ppermute(x, AXES, flips(mesh_shape, even, even if odd is None else odd))  43.9 us
    ppermute x47, waiting for transfers between devices, swap(): lax.ppermute(x, AXES, flips(mesh_shape, even, even if odd is None else odd))  42.8 us
    pallas_call x4, Pallas kernels, outer(): pl.pallas_call(functools.partial(outer_kernel, first, chunk, cells, len(p...  12.1 us
    pallas_call x3, Pallas kernels, inner(): pl.pallas_call(functools.partial(inner_kernel, first, half, cells, len(pi...  10.8 us
    unnamed x10, local copies, waits for them, and re-layouts  4.41 us
  transfers between devices with their start and end apart: 47, of which 22 were waited for; matrix products, arithmetic and copies ran while one was open for 2% of the time, Pallas kernels for 6%

profile of v6, /device:TPU:0, one launch (start us, length us, event | category | flops | bytes accessed | tf_op | source)
XLA Modules:
  0.0 124.0 jit_solution(12197905463021569016)
XLA Ops:
  1.6 3.1 %collective-permute-start.1 = (f32[192,384]{1,0:T(8,128)S(1)}, f32[192,384]{1,0:T(8,128)S(1)}, u32[]{:S(2)}, u32[]{:S(2)}) collective-permute-start(f32[192,384]{1,0:T(8,128)S(1)} %shard_map.86), channel_id=1, source_target_pairs={{0,2},{1,3},{2,0},{3,1},{4,6},{5,7},{6,4},{7,5},{8,10},{9,11},{10,... | collective-permute-start | bytes 884744 | tf_op jit(solution)/shard_map/ppermute | solution.py:403
  10.2 2.1 %shard_map.87 = (bf16[4,384,1152]{2,1,0:T(8,128)(2,1)S(1)}, bf16[4,384,1152]{2,1,0:T(8,128)(2,1)S(1)}, f32[96,384]{1,0:T(8,128)S(1)}, f32[96,384]{1,0:T(8,128)S(1)}) custom-call(f32[4,384,384]{2,1,0:T(8,128)S(1)} %copy-done, f32[4,384,384]{2,1,0:T(8,128)S(1)} %copy-done.1, f32[1,384,384]{2,1,0:T(8,128)} %x_ref.3, f32[1,384,384]{2,1,0:T(8,128)S(1)} %copy-done.2), custom_call_target="tpu_custom_call" | custom-call | flops 2359296 | bytes 11796480 | tf_op jit(solution)/shard_map/pallas_call | solution.py:99
  12.8 5.2 %collective-permute-done.3.refs_4_.refs_6_ = f32[192,384]{1,0:T(8,128)S(1)} collective-permute-done((f32[192,384]{1,0:T(8,128)S(1)}, f32[192,384]{1,0:T(8,128)S(1)}, u32[]{:S(2)}, u32[]{:S(2)}) %collective-permute-start.3) | collective-permute-done | bytes 294944 | tf_op jit(solution)/shard_map/ppermute | solution.py:403
  18.7 3.4 %shard_map.89 = (bf16[4,192,384]{2,1,0:T(8,128)(2,1)S(1)}, bf16[4,192,384]{2,1,0:T(8,128)(2,1)S(1)}, f32[8,384]{1,0:T(8,128)S(1)}) custom-call(s32[1,4]{1,0:T(1,128)S(1)} %copy-done.4, s32[1]{0:T(128)S(6)} %copy.9.refs_1_, f32[384,384]{1,0:T(8,128)} %bitcast.refs_2_, f32[384,384]{1,0:T(8,128)S(1)} %collective-permute-done.refs_3_, ...), custom_call_target="tpu_custom_call" | custom-call | flops 679477248 | bytes 4718592 | tf_op jit(solution)/shard_map/pallas_call | solution.py:182
  22.1 3.5 %shard_map.90 = (bf16[4,1152,384]{2,1,0:T(8,128)(2,1)S(1)}, f32[8,384]{1,0:T(8,128)S(1)}) custom-call(s32[1,4]{1,0:T(1,128)S(1)} %copy-done.4, s32[1]{0:T(128)S(6)} %copy.9.refs_1_, f32[384,384]{1,0:T(8,128)} %bitcast.refs_2_, f32[384,384]{1,0:T(8,128)S(1)} %collective-permute-done.refs_3_, f32[192,384]{1,0:T(8,128)S(1)} %collective-permute-done.3.refs_4_.refs_6_, ...), custom_call_target="tpu_custom_call" | custom-call | flops 679477248 | bytes 4718592 | tf_op jit(solution)/shard_map/pallas_call | solution.py:182
  25.7 3.0 %shard_map.91 = (f32[1152,128]{1,0:T(8,128)S(1)}, f32[1152,128]{1,0:T(8,128)S(1)}, f32[8,128]{1,0:T(8,128)S(1)}) custom-call(s32[1,4]{1,0:T(1,128)S(1)} %copy-done.3, s32[1]{0:T(128)S(6)} %copy.9.refs_1_, f32[384,384]{1,0:T(8,128)} %bitcast.refs_2_, f32[384,384]{1,0:T(8,128)S(1)} %collective-permute-done.refs_3_, ...), custom_call_target="tpu_custom_call" | custom-call | flops 679477248 | bytes 4718592 | tf_op jit(solution)/shard_map/pallas_call | solution.py:241
  28.7 3.6 %shard_map.95 = (f32[1160,128]{1,0:T(8,128)S(1)}, f32[1160,128]{1,0:T(8,128)S(1)}, f32[8,128]{1,0:T(8,128)}) custom-call(s32[1,4]{1,0:T(1,128)S(1)} %copy-done.3, s32[1]{0:T(128)S(6)} %copy.9.refs_1_, f32[384,384]{1,0:T(8,128)} %bitcast.refs_2_, f32[384,384]{1,0:T(8,128)S(1)} %collective-permute-done.refs_3_, f32[192,384]{1,0:T(8,128)S(1)} %collective-permute-done.1.refs_4_, ...), custom_call_target="tpu_custom_call" | custom-call | flops 679477248 | bytes 4718592 | tf_op jit(solution)/shard_map/pallas_call | solution.py:241
  35.4 5.8 %collective-permute-done.12.recv_ref = f32[584,128]{1,0:T(8,128)S(1)} collective-permute-done((f32[584,128]{1,0:T(8,128)S(1)}, f32[584,128]{1,0:T(8,128)S(1)}, u32[]{:S(2)}, u32[]{:S(2)}) %collective-permute-start.12) | collective-permute-done | bytes 299040 | tf_op jit(solution)/shard_map/ppermute | solution.py:403
  41.2 2.8 %collective-permute-start.13 = (f32[152,128]{1,0:T(8,128)S(1)}, f32[152,128]{1,0:T(8,128)S(1)}, u32[]{:S(2)}, u32[]{:S(2)}) collective-permute-start(f32[152,128]{1,0:T(8,128)S(1)} %get-tuple-element.82), channel_id=1, source_target_pairs={{0,10},{1,7},{2,8},{3,5},{4,14},{5,3},{6,12},{7,1},{8,2},{9,15},{1... | collective-permute-start | bytes 233480 | tf_op jit(solution)/shard_map/ppermute | solution.py:403
  44.8 2.9 %collective-permute-start.7 = (f32[144,128]{1,0:T(8,128)S(1)}, f32[144,128]{1,0:T(8,128)S(1)}, u32[]{:S(2)}, u32[]{:S(2)}) collective-permute-start(f32[144,128]{1,0:T(8,128)S(1)} %get-tuple-element.73), channel_id=1, source_target_pairs={{0,12},{1,7},{2,14},{3,5},{4,8},{5,3},{6,10},{7,1},{8,4},{9,15},{1... | collective-permute-start | bytes 221192 | tf_op jit(solution)/shard_map/ppermute | solution.py:403
  49.5 2.2 %collective-permute-start.16 = (f32[152,128]{1,0:T(8,128)S(1)}, f32[152,128]{1,0:T(8,128)S(1)}, u32[]{:S(2)}, u32[]{:S(2)}) collective-permute-start(f32[152,128]{1,0:T(8,128)S(1)} %shard_map.98.refs_2_), channel_id=1, source_target_pairs={{0,16},{1,17},{2,18},{3,19},{4,20},{5,21},{6,22},{7,23},{8,24},{9,... | collective-permute-start | bytes 233480 | tf_op jit(solution)/shard_map/ppermute | solution.py:403
  53.0 3.0 %collective-permute-start.10 = (f32[144,128]{1,0:T(8,128)S(1)}, f32[144,128]{1,0:T(8,128)S(1)}, u32[]{:S(2)}, u32[]{:S(2)}) collective-permute-start(f32[144,128]{1,0:T(8,128)S(1)} %shard_map.94.refs_0_), channel_id=1, source_target_pairs={{0,16},{1,17},{2,18},{3,19},{4,20},{5,21},{6,22},{7,23},{8,24},{9,... | collective-permute-start | bytes 221192 | tf_op jit(solution)/shard_map/ppermute | solution.py:403
  56.0 3.0 %collective-permute-done.10.refs_1_ = f32[144,128]{1,0:T(8,128)S(1)} collective-permute-done((f32[144,128]{1,0:T(8,128)S(1)}, f32[144,128]{1,0:T(8,128)S(1)}, u32[]{:S(2)}, u32[]{:S(2)}) %collective-permute-start.10) | collective-permute-done | bytes 73760 | tf_op jit(solution)/shard_map/ppermute | solution.py:403
  67.3 2.6 %collective-permute-done.26.even_ref.refs_12_ = f32[96,384]{1,0:T(8,128)S(1)} collective-permute-done((f32[96,384]{1,0:T(8,128)S(1)}, f32[96,384]{1,0:T(8,128)S(1)}, u32[]{:S(2)}, u32[]{:S(2)}) %collective-permute-start.26) | collective-permute-done | bytes 147488 | tf_op jit(solution)/shard_map/ppermute | solution.py:403
  71.1 2.7 %collective-permute-start.30 = (f32[96,384]{1,0:T(8,128)S(1)}, f32[96,384]{1,0:T(8,128)S(1)}, u32[]{:S(2)}, u32[]{:S(2)}) collective-permute-start(f32[96,384]{1,0:T(8,128)S(1)} %shard_map.100), channel_id=1, source_target_pairs={{0,4},{1,9},{2,6},{3,11},{4,0},{5,13},{6,2},{7,15},{8,12},{9,1},{1... | collective-permute-start | bytes 442376 | tf_op jit(solution)/shard_map/ppermute | solution.py:403
  74.9 2.1 %collective-permute-done.30.refs_16_ = f32[96,384]{1,0:T(8,128)S(1)} collective-permute-done((f32[96,384]{1,0:T(8,128)S(1)}, f32[96,384]{1,0:T(8,128)S(1)}, u32[]{:S(2)}, u32[]{:S(2)}) %collective-permute-start.30) | collective-permute-done | bytes 147488 | tf_op jit(solution)/shard_map/ppermute | solution.py:403
  78.4 3.9 %shard_map.101 = (bf16[4,1152,384]{2,1,0:T(8,128)(2,1)S(1)}, f32[8,384]{1,0:T(8,128)S(1)}) custom-call(s32[1,4]{1,0:T(1,128)S(1)} %copy-done.4, s32[1]{0:T(128)S(6)} %copy.9.refs_1_, f32[96,384]{1,0:T(8,128)S(1)} %get-tuple-element.87.refs_2_.refs_4_, f32[96,384]{1,0:T(8,128)S(1)} %collective-permute-done.17.refs_3_, ...), custom_call_target="tpu_custom_call" | custom-call | flops 1358954496 | bytes 4718592 | tf_op jit(solution)/shard_map/pallas_call | solution.py:182
  82.2 2.5 %shard_map.103 = (f32[1152,128]{1,0:T(8,128)S(1)}, f32[1152,128]{1,0:T(8,128)S(1)}, f32[8,128]{1,0:T(8,128)S(1)}) custom-call(s32[1,4]{1,0:T(1,128)S(1)} %copy-done.3, s32[1]{0:T(128)S(6)} %copy.9.refs_1_, f32[96,384]{1,0:T(8,128)S(1)} %get-tuple-element.87.refs_2_.refs_4_, f32[96,384]{1,0:T(8,128)S(1)} %collective-permute-done.17.refs_3_, ...), custom_call_target="tpu_custom_call" | custom-call | flops 679477248 | bytes 4718592 | tf_op jit(solution)/shard_map/pallas_call | solution.py:241
  84.7 3.1 %shard_map.107 = (f32[1160,128]{1,0:T(8,128)S(1)}, f32[1160,128]{1,0:T(8,128)S(1)}, f32[8,128]{1,0:T(8,128)}) custom-call(s32[1,4]{1,0:T(1,128)S(1)} %copy-done.3, s32[1]{0:T(128)S(6)} %copy.9.refs_1_, f32[96,384]{1,0:T(8,128)S(1)} %get-tuple-element.87.refs_2_.refs_4_, f32[96,384]{1,0:T(8,128)S(1)} %collective-permute-done.17.refs_3_, ...), custom_call_target="tpu_custom_call" | custom-call | flops 679477248 | bytes 4718592 | tf_op jit(solution)/shard_map/pallas_call | solution.py:241
  91.4 5.3 %collective-permute-done.39.recv_ref = f32[584,128]{1,0:T(8,128)S(1)} collective-permute-done((f32[584,128]{1,0:T(8,128)S(1)}, f32[584,128]{1,0:T(8,128)S(1)}, u32[]{:S(2)}, u32[]{:S(2)}) %collective-permute-start.39) | collective-permute-done | bytes 299040 | tf_op jit(solution)/shard_map/ppermute | solution.py:403
  96.7 2.3 %collective-permute-start.40 = (f32[152,128]{1,0:T(8,128)S(1)}, f32[152,128]{1,0:T(8,128)S(1)}, u32[]{:S(2)}, u32[]{:S(2)}) collective-permute-start(f32[152,128]{1,0:T(8,128)S(1)} %get-tuple-element.105), channel_id=1, source_target_pairs={{0,10},{1,7},{2,8},{3,5},{4,14},{5,3},{6,12},{7,1},{8,2},{9,15},{1... | collective-permute-start | bytes 233480 | tf_op jit(solution)/shard_map/ppermute | solution.py:403
  108.4 2.6 %collective-permute-start.37 = (f32[144,128]{1,0:T(8,128)S(1)}, f32[144,128]{1,0:T(8,128)S(1)}, u32[]{:S(2)}, u32[]{:S(2)}) collective-permute-start(f32[144,128]{1,0:T(8,128)S(1)} %shard_map.106.refs_0_), channel_id=1, source_target_pairs={{0,16},{1,17},{2,18},{3,19},{4,20},{5,21},{6,22},{7,23},{8,24},{9,... | collective-permute-start | bytes 221192 | tf_op jit(solution)/shard_map/ppermute | solution.py:403
  111.1 3.5 %collective-permute-done.37.refs_1_ = f32[144,128]{1,0:T(8,128)S(1)} collective-permute-done((f32[144,128]{1,0:T(8,128)S(1)}, f32[144,128]{1,0:T(8,128)S(1)}, u32[]{:S(2)}, u32[]{:S(2)}) %collective-permute-start.37) | collective-permute-done | bytes 73760 | tf_op jit(solution)/shard_map/ppermute | solution.py:403
  115.5 2.7 %collective-permute-start.46 = (f32[96,384]{1,0:T(8,128)S(1)}, f32[96,384]{1,0:T(8,128)S(1)}, u32[]{:S(2)}, u32[]{:S(2)}) collective-permute-start(f32[96,384]{1,0:T(8,128)S(1)} %get-tuple-element.108.refs_0_), channel_id=1, source_target_pairs={{0,12},{1,13},{2,14},{3,15},{4,8},{5,9},{6,10},{7,11},{8,4},{9,5},... | collective-permute-start | bytes 442376 | tf_op jit(solution)/shard_map/ppermute | solution.py:403
  (111 shorter events, 45.6 us)
Async XLA Ops:
  1.6 10.9 %collective-permute-start.1 = (f32[192,384]{1,0:T(8,128)S(1)}, f32[192,384]{1,0:T(8,128)S(1)}, u32[]{:S(2)}, u32[]{:S(2)}) collective-permute-start(f32[192,384]{1,0:T(8,128)S(1)} %shard_map.86), channel_id=1, source_target_pairs={{0,2},{1,3},{2,0},{3,1},{4,6},{5,7},{6,4},{7,5},{8,10},{9,11},{10,... | collective-permute-start | bytes 884744 | tf_op jit(solution)/shard_map/ppermute | solution.py:403
  4.7 14.0 %collective-permute-start = (f32[384,384]{1,0:T(8,128)}, f32[384,384]{1,0:T(8,128)S(1)}, u32[]{:S(2)}, u32[]{:S(2)}) collective-permute-start(f32[384,384]{1,0:T(8,128)} %bitcast.refs_2_), channel_id=1, source_target_pairs={{0,1},{1,0},{2,3},{3,2},{4,5},{5,4},{6,7},{7,6},{8,9},{9,8},{10,11... | collective-permute-start | bytes 1769480 | tf_op jit(solution)/shard_map/ppermute | solution.py:403
  5.7 12.3 %collective-permute-start.3 = (f32[192,384]{1,0:T(8,128)S(1)}, f32[192,384]{1,0:T(8,128)S(1)}, u32[]{:S(2)}, u32[]{:S(2)}) collective-permute-start(f32[192,384]{1,0:T(8,128)S(1)} %shard_map.88), channel_id=1, source_target_pairs={{0,2},{1,3},{2,0},{3,1},{4,6},{5,7},{6,4},{7,5},{8,10},{9,11},{10,... | collective-permute-start | bytes 884744 | tf_op jit(solution)/shard_map/ppermute | solution.py:403
  34.4 6.8 %collective-permute-start.12 = (f32[584,128]{1,0:T(8,128)S(1)}, f32[584,128]{1,0:T(8,128)S(1)}, u32[]{:S(2)}, u32[]{:S(2)}) collective-permute-start(f32[584,128]{1,0:T(8,128)S(1)} %get-tuple-element.80), channel_id=1, source_target_pairs={{0,4},{1,9},{2,6},{3,11},{4,0},{5,13},{6,2},{7,15},{8,12},{9,1},{1... | collective-permute-start | bytes 897032 | tf_op jit(solution)/shard_map/ppermute | solution.py:403
  35.2 9.6 %collective-permute-start.6 = (f32[576,128]{1,0:T(8,128)S(1)}, f32[576,128]{1,0:T(8,128)S(1)}, u32[]{:S(2)}, u32[]{:S(2)}) collective-permute-start(f32[576,128]{1,0:T(8,128)S(1)} %get-tuple-element.71), channel_id=1, source_target_pairs={{0,2},{1,9},{2,0},{3,11},{4,6},{5,13},{6,4},{7,15},{8,10},{9,1},{1... | collective-permute-start | bytes 884744 | tf_op jit(solution)/shard_map/ppermute | solution.py:403
  41.2 7.1 %collective-permute-start.13 = (f32[152,128]{1,0:T(8,128)S(1)}, f32[152,128]{1,0:T(8,128)S(1)}, u32[]{:S(2)}, u32[]{:S(2)}) collective-permute-start(f32[152,128]{1,0:T(8,128)S(1)} %get-tuple-element.82), channel_id=1, source_target_pairs={{0,10},{1,7},{2,8},{3,5},{4,14},{5,3},{6,12},{7,1},{8,2},{9,15},{1... | collective-permute-start | bytes 233480 | tf_op jit(solution)/shard_map/ppermute | solution.py:403
  44.8 6.8 %collective-permute-start.7 = (f32[144,128]{1,0:T(8,128)S(1)}, f32[144,128]{1,0:T(8,128)S(1)}, u32[]{:S(2)}, u32[]{:S(2)}) collective-permute-start(f32[144,128]{1,0:T(8,128)S(1)} %get-tuple-element.73), channel_id=1, source_target_pairs={{0,12},{1,7},{2,14},{3,5},{4,8},{5,3},{6,10},{7,1},{8,4},{9,15},{1... | collective-permute-start | bytes 221192 | tf_op jit(solution)/shard_map/ppermute | solution.py:403
  49.5 9.5 %collective-permute-start.16 = (f32[152,128]{1,0:T(8,128)S(1)}, f32[152,128]{1,0:T(8,128)S(1)}, u32[]{:S(2)}, u32[]{:S(2)}) collective-permute-start(f32[152,128]{1,0:T(8,128)S(1)} %shard_map.98.refs_2_), channel_id=1, source_target_pairs={{0,16},{1,17},{2,18},{3,19},{4,20},{5,21},{6,22},{7,23},{8,24},{9,... | collective-permute-start | bytes 233480 | tf_op jit(solution)/shard_map/ppermute | solution.py:403
  59.1 6.5 %collective-permute-start.18 = (f32[96,384]{1,0:T(8,128)S(1)}, f32[96,384]{1,0:T(8,128)S(1)}, u32[]{:S(2)}, u32[]{:S(2)}) collective-permute-start(f32[96,384]{1,0:T(8,128)S(1)} %get-tuple-element.87.refs_2_.refs_4_), channel_id=1, source_target_pairs={{0,8},{1,9},{2,10},{3,11},{4,12},{5,13},{6,14},{7,15},{8,0},{9,1},... | collective-permute-start | bytes 442376 | tf_op jit(solution)/shard_map/ppermute | solution.py:403
  59.2 7.3 %collective-permute-start.20 = (f32[96,384]{1,0:T(8,128)S(1)}, f32[96,384]{1,0:T(8,128)S(1)}, u32[]{:S(2)}, u32[]{:S(2)}) collective-permute-start(f32[96,384]{1,0:T(8,128)S(1)} %get-tuple-element.87.refs_2_.refs_4_), channel_id=1, source_target_pairs={{0,4},{1,5},{2,6},{3,7},{4,0},{5,1},{6,2},{7,3},{8,12},{9,13},{10,... | collective-permute-start | bytes 442376 | tf_op jit(solution)/shard_map/ppermute | solution.py:403
  60.8 9.1 %collective-permute-start.26 = (f32[96,384]{1,0:T(8,128)S(1)}, f32[96,384]{1,0:T(8,128)S(1)}, u32[]{:S(2)}, u32[]{:S(2)}) collective-permute-start(f32[96,384]{1,0:T(8,128)S(1)} %get-tuple-element.87.refs_2_.refs_4_), channel_id=1, source_target_pairs={{0,10},{1,11},{2,8},{3,9},{4,14},{5,15},{6,12},{7,13},{8,2},{9,3},... | collective-permute-start | bytes 442376 | tf_op jit(solution)/shard_map/ppermute | solution.py:403
  62.8 8.3 %collective-permute-start.28 = (f32[96,384]{1,0:T(8,128)S(1)}, f32[96,384]{1,0:T(8,128)S(1)}, u32[]{:S(2)}, u32[]{:S(2)}) collective-permute-start(f32[96,384]{1,0:T(8,128)S(1)} %get-tuple-element.87.refs_2_.refs_4_), channel_id=1, source_target_pairs={{0,6},{1,7},{2,4},{3,5},{4,2},{5,3},{6,0},{7,1},{8,14},{9,15},{10,... | collective-permute-start | bytes 442376 | tf_op jit(solution)/shard_map/ppermute | solution.py:403
  64.1 7.0 %collective-permute-start.17 = (f32[96,384]{1,0:T(8,128)S(1)}, f32[96,384]{1,0:T(8,128)S(1)}, u32[]{:S(2)}, u32[]{:S(2)}) collective-permute-start(f32[96,384]{1,0:T(8,128)S(1)} %get-tuple-element.87.refs_2_.refs_4_), channel_id=1, source_target_pairs={{0,1},{1,0},{2,3},{3,2},{4,5},{5,4},{6,7},{7,6},{8,9},{9,8},{10,11... | collective-permute-start | bytes 442376 | tf_op jit(solution)/shard_map/ppermute | solution.py:403
  65.6 8.3 %collective-permute-start.22 = (f32[96,384]{1,0:T(8,128)S(1)}, f32[96,384]{1,0:T(8,128)S(1)}, u32[]{:S(2)}, u32[]{:S(2)}) collective-permute-start(f32[96,384]{1,0:T(8,128)S(1)} %get-tuple-element.87.refs_2_.refs_4_), channel_id=1, source_target_pairs={{0,12},{1,13},{2,14},{3,15},{4,8},{5,9},{6,10},{7,11},{8,4},{9,5},... | collective-permute-start | bytes 442376 | tf_op jit(solution)/shard_map/ppermute | solution.py:403
  66.4 7.4 %collective-permute-start.24 = (f32[96,384]{1,0:T(8,128)S(1)}, f32[96,384]{1,0:T(8,128)S(1)}, u32[]{:S(2)}, u32[]{:S(2)}) collective-permute-start(f32[96,384]{1,0:T(8,128)S(1)} %get-tuple-element.87.refs_2_.refs_4_), channel_id=1, source_target_pairs={{0,2},{1,3},{2,0},{3,1},{4,6},{5,7},{6,4},{7,5},{8,10},{9,11},{10,... | collective-permute-start | bytes 442376 | tf_op jit(solution)/shard_map/ppermute | solution.py:403
  89.9 6.8 %collective-permute-start.39 = (f32[584,128]{1,0:T(8,128)S(1)}, f32[584,128]{1,0:T(8,128)S(1)}, u32[]{:S(2)}, u32[]{:S(2)}) collective-permute-start(f32[584,128]{1,0:T(8,128)S(1)} %get-tuple-element.103), channel_id=1, source_target_pairs={{0,4},{1,9},{2,6},{3,11},{4,0},{5,13},{6,2},{7,15},{8,12},{9,1},{1... | collective-permute-start | bytes 897032 | tf_op jit(solution)/shard_map/ppermute | solution.py:403
  90.7 9.6 %collective-permute-start.33 = (f32[576,128]{1,0:T(8,128)S(1)}, f32[576,128]{1,0:T(8,128)S(1)}, u32[]{:S(2)}, u32[]{:S(2)}) collective-permute-start(f32[576,128]{1,0:T(8,128)S(1)} %get-tuple-element.94), channel_id=1, source_target_pairs={{0,2},{1,9},{2,0},{3,11},{4,6},{5,13},{6,4},{7,15},{8,10},{9,1},{1... | collective-permute-start | bytes 884744 | tf_op jit(solution)/shard_map/ppermute | solution.py:403
  96.7 6.5 %collective-permute-start.40 = (f32[152,128]{1,0:T(8,128)S(1)}, f32[152,128]{1,0:T(8,128)S(1)}, u32[]{:S(2)}, u32[]{:S(2)}) collective-permute-start(f32[152,128]{1,0:T(8,128)S(1)} %get-tuple-element.105), channel_id=1, source_target_pairs={{0,10},{1,7},{2,8},{3,5},{4,14},{5,3},{6,12},{7,1},{8,2},{9,15},{1... | collective-permute-start | bytes 233480 | tf_op jit(solution)/shard_map/ppermute | solution.py:403
  100.3 6.4 %collective-permute-start.34 = (f32[144,128]{1,0:T(8,128)S(1)}, f32[144,128]{1,0:T(8,128)S(1)}, u32[]{:S(2)}, u32[]{:S(2)}) collective-permute-start(f32[144,128]{1,0:T(8,128)S(1)} %get-tuple-element.96), channel_id=1, source_target_pairs={{0,12},{1,7},{2,14},{3,5},{4,8},{5,3},{6,10},{7,1},{8,4},{9,15},{1... | collective-permute-start | bytes 221192 | tf_op jit(solution)/shard_map/ppermute | solution.py:403
  104.7 9.9 %collective-permute-start.43 = (f32[152,128]{1,0:T(8,128)S(1)}, f32[152,128]{1,0:T(8,128)S(1)}, u32[]{:S(2)}, u32[]{:S(2)}) collective-permute-start(f32[152,128]{1,0:T(8,128)S(1)} %shard_map.110.refs_2_), channel_id=1, source_target_pairs={{0,16},{1,17},{2,18},{3,19},{4,20},{5,21},{6,22},{7,23},{8,24},{9,... | collective-permute-start | bytes 233480 | tf_op jit(solution)/shard_map/ppermute | solution.py:403
  108.4 6.2 %collective-permute-start.37 = (f32[144,128]{1,0:T(8,128)S(1)}, f32[144,128]{1,0:T(8,128)S(1)}, u32[]{:S(2)}, u32[]{:S(2)}) collective-permute-start(f32[144,128]{1,0:T(8,128)S(1)} %shard_map.106.refs_0_), channel_id=1, source_target_pairs={{0,16},{1,17},{2,18},{3,19},{4,20},{5,21},{6,22},{7,23},{8,24},{9,... | collective-permute-start | bytes 221192 | tf_op jit(solution)/shard_map/ppermute | solution.py:403
  114.7 6.8 %collective-permute-start.44 = (f32[96,384]{1,0:T(8,128)S(1)}, f32[96,384]{1,0:T(8,128)S(1)}, u32[]{:S(2)}, u32[]{:S(2)}) collective-permute-start(f32[96,384]{1,0:T(8,128)S(1)} %get-tuple-element.108.refs_0_), channel_id=1, source_target_pairs={{0,8},{1,9},{2,10},{3,11},{4,12},{5,13},{6,14},{7,15},{8,0},{9,1},... | collective-permute-start | bytes 442376 | tf_op jit(solution)/shard_map/ppermute | solution.py:403
  114.7 8.4 %collective-permute-start.45 = (f32[96,384]{1,0:T(8,128)S(1)}, f32[96,384]{1,0:T(8,128)S(1)}, u32[]{:S(2)}, u32[]{:S(2)}) collective-permute-start(f32[96,384]{1,0:T(8,128)S(1)} %get-tuple-element.108.refs_0_), channel_id=1, source_target_pairs={{0,4},{1,5},{2,6},{3,7},{4,0},{5,1},{6,2},{7,3},{8,12},{9,13},{10,... | collective-permute-start | bytes 442376 | tf_op jit(solution)/shard_map/ppermute | solution.py:403
  115.5 7.6 %collective-permute-start.46 = (f32[96,384]{1,0:T(8,128)S(1)}, f32[96,384]{1,0:T(8,128)S(1)}, u32[]{:S(2)}, u32[]{:S(2)}) collective-permute-start(f32[96,384]{1,0:T(8,128)S(1)} %get-tuple-element.108.refs_0_), channel_id=1, source_target_pairs={{0,12},{1,13},{2,14},{3,15},{4,8},{5,9},{6,10},{7,11},{8,4},{9,5},... | collective-permute-start | bytes 442376 | tf_op jit(solution)/shard_map/ppermute | solution.py:403
  (28 other events, 117.0 us)

commit v7 on v6

--- a/solution.py
+++ b/solution.py
@@ -331,23 +331,6 @@
     )(*sums, vec, inv, diag)
 
 
-def take_kernel(first, x_ref, out_ref, sem):
-    copy = pltpu.make_async_copy(x_ref.at[0, pl.ds(first, out_ref.shape[0]), :], out_ref, sem)
-    copy.start()
-    copy.wait()
-
-
-def take(x, first, rows):
-    return pl.pallas_call(
-        functools.partial(take_kernel, first),
-        in_specs=[pl.BlockSpec(memory_space=pl.ANY)],
-        out_specs=VMEM,
-        out_shape=jax.ShapeDtypeStruct((rows, x.shape[-1]), x.dtype),
-        scratch_shapes=[pltpu.SemaphoreType.DMA],
-        compiler_params=grant(4),
-    )(x)
-
-
 def zero_tile(tile):
     def kernel(in_ref, out_ref):
         out_ref[...] = jnp.zeros_like(out_ref)
@@ -412,7 +395,8 @@
     rows = b // CHUNKS
     far = []
     for h in range(CHUNKS):
-        far.append(swap(take(psi_start, h * rows, rows), [DIMS[0]]))
+        block = own if h == 0 else lax.optimization_barrier(own)
+        far.append(swap(block[h * rows:(h + 1) * rows], [DIMS[0]]))
     beside = swap(own, [CORE])
     left, right, vec, diag = prepare(left_ops, right_ops, psi_start, diagonal)
     far[0], left, right, vec, diag = lax.optimization_barrier((far[0], left, right, vec, diag))

time: 125 us -> 122 us (0.976)
  Pallas kernels: 28.5 us -> 23.4 us
  local copies, waits for them, and re-layouts: 5.49 us -> 8.58 us
    slice x0 -> x2, local copies, waits for them, and re-layouts: none -> 2.02 us  [shards(): far.append(swap(block[h * rows:(h + 1) * rows], [DIMS[0]]))]
    pallas_call x2 -> x0, Pallas kernels: 1.94 us -> none  [take(): pl.pallas_call(functools.partial(take_kernel, first), in_specs=[pl.BlockS...]
    unnamed x10 -> x14, local copies, waits for them, and re-layouts: 4.41 us -> 5.47 us
  transfers between devices with their start and end apart: 47 -> 47, of which waited for: 22 -> 22; matrix products, arithmetic and copies ran while one was open for 2% -> 3% of each run, Pallas kernels for 6% -> 4%
where the time goes in v7:
time: 122 us
  starting transfers between devices  43.8 us (36%)
  waiting for transfers between devices  42.8 us (35%)
  Pallas kernels  23.4 us (19%)
  local copies, waits for them, and re-layouts  8.58 us (7%)
  other arithmetic  1.85 us (2%)
  between operations  1.56 us (1%)
    ppermute x47, starting transfers between devices, swap(): lax.ppermute(x, AXES, flips(mesh_shape, even, even if odd is None else odd))  43.8 us
    ppermute x47, waiting for transfers between devices, swap(): lax.ppermute(x, AXES, flips(mesh_shape, even, even if odd is None else odd))  42.8 us
    pallas_call x4, Pallas kernels, outer(): pl.pallas_call(functools.partial(outer_kernel, first, chunk, cells, len(p...  11.1 us
    pallas_call x3, Pallas kernels, inner(): pl.pallas_call(functools.partial(inner_kernel, first, half, cells, len(pi...  9.73 us
    unnamed x14, local copies, waits for them, and re-layouts  5.47 us
  transfers between devices with their start and end apart: 47, of which 22 were waited for; matrix products, arithmetic and copies ran while one was open for 3% of the time, Pallas kernels for 4%

profile of v7, /device:TPU:0, one launch (start us, length us, event | category | flops | bytes accessed | tf_op | source)
XLA Modules:
  0.0 122.0 jit_solution(4203860591286879470)
XLA Ops:
  1.7 3.1 %collective-permute-start.1 = (f32[192,384]{1,0:T(8,128)S(1)}, f32[192,384]{1,0:T(8,128)S(1)}, u32[]{:S(2)}, u32[]{:S(2)}) collective-permute-start(f32[192,384]{1,0:T(8,128)S(1)} %slice_bitcast_fusion), channel_id=1, source_target_pairs={{0,2},{1,3},{2,0},{3,1},{4,6},{5,7},{6,4},{7,5},{8,10},{9,11},{10,... | collective-permute-start | bytes 884744 | tf_op jit(solution)/shard_map/ppermute | solution.py:386
  12.9 5.2 %collective-permute-done.3.refs_4_.refs_6_ = f32[192,384]{1,0:T(8,128)S(1)} collective-permute-done((f32[192,384]{1,0:T(8,128)S(1)}, f32[192,384]{1,0:T(8,128)S(1)}, u32[]{:S(2)}, u32[]{:S(2)}) %collective-permute-start.3) | collective-permute-done | bytes 294944 | tf_op jit(solution)/shard_map/ppermute | solution.py:386
  18.8 2.9 %shard_map.87 = (bf16[4,192,384]{2,1,0:T(8,128)(2,1)S(1)}, bf16[4,192,384]{2,1,0:T(8,128)(2,1)S(1)}, f32[8,384]{1,0:T(8,128)S(1)}) custom-call(s32[1,4]{1,0:T(1,128)S(1)} %copy-done.6, s32[1]{0:T(128)S(6)} %copy.9.refs_1_, f32[384,384]{1,0:T(8,128)S(1)} %bitcast.7, f32[384,384]{1,0:T(8,128)S(1)} %collective-permute-done.refs_3_, ...), custom_call_target="tpu_custom_call" | custom-call | flops 679477248 | bytes 4718592 | tf_op jit(solution)/shard_map/pallas_call | solution.py:182
  21.7 3.0 %shard_map.88 = (bf16[4,1152,384]{2,1,0:T(8,128)(2,1)S(1)}, f32[8,384]{1,0:T(8,128)S(1)}) custom-call(s32[1,4]{1,0:T(1,128)S(1)} %copy-done.6, s32[1]{0:T(128)S(6)} %copy.9.refs_1_, f32[384,384]{1,0:T(8,128)S(1)} %bitcast.8, f32[384,384]{1,0:T(8,128)S(1)} %collective-permute-done.refs_3_, f32[192,384]{1,0:T(8,128)S(1)} %collective-permute-done.3.refs_4_.refs_6_, ...), custom_call_target="tpu_custom_call" | custom-call | flops 679477248 | bytes 4718592 | tf_op jit(solution)/shard_map/pallas_call | solution.py:182
  24.7 2.5 %shard_map.89 = (f32[1152,128]{1,0:T(8,128)S(1)}, f32[1152,128]{1,0:T(8,128)S(1)}, f32[8,128]{1,0:T(8,128)S(1)}) custom-call(s32[1,4]{1,0:T(1,128)S(1)} %copy-done.5, s32[1]{0:T(128)S(6)} %copy.9.refs_1_, f32[384,384]{1,0:T(8,128)S(1)} %bitcast.9, f32[384,384]{1,0:T(8,128)S(1)} %collective-permute-done.refs_3_, ...), custom_call_target="tpu_custom_call" | custom-call | flops 679477248 | bytes 4718592 | tf_op jit(solution)/shard_map/pallas_call | solution.py:241
  27.2 3.1 %shard_map.93 = (f32[1160,128]{1,0:T(8,128)S(1)}, f32[1160,128]{1,0:T(8,128)S(1)}, f32[8,128]{1,0:T(8,128)}) custom-call(s32[1,4]{1,0:T(1,128)S(1)} %copy-done.5, s32[1]{0:T(128)S(6)} %copy.9.refs_1_, f32[384,384]{1,0:T(8,128)S(1)} %bitcast.10, f32[384,384]{1,0:T(8,128)S(1)} %collective-permute-done.refs_3_, f32[192,384]{1,0:T(8,128)S(1)} %collective-permute-done.1.refs_4_, ...), custom_call_target="tpu_custom_call" | custom-call | flops 679477248 | bytes 4718592 | tf_op jit(solution)/shard_map/pallas_call | solution.py:241
  33.3 5.8 %collective-permute-done.12.recv_ref = f32[584,128]{1,0:T(8,128)S(1)} collective-permute-done((f32[584,128]{1,0:T(8,128)S(1)}, f32[584,128]{1,0:T(8,128)S(1)}, u32[]{:S(2)}, u32[]{:S(2)}) %collective-permute-start.12) | collective-permute-done | bytes 299040 | tf_op jit(solution)/shard_map/ppermute | solution.py:386
  39.2 2.8 %collective-permute-start.13 = (f32[152,128]{1,0:T(8,128)S(1)}, f32[152,128]{1,0:T(8,128)S(1)}, u32[]{:S(2)}, u32[]{:S(2)}) collective-permute-start(f32[152,128]{1,0:T(8,128)S(1)} %get-tuple-element.82), channel_id=1, source_target_pairs={{0,10},{1,7},{2,8},{3,5},{4,14},{5,3},{6,12},{7,1},{8,2},{9,15},{1... | collective-permute-start | bytes 233480 | tf_op jit(solution)/shard_map/ppermute | solution.py:386
  42.8 2.9 %collective-permute-start.7 = (f32[144,128]{1,0:T(8,128)S(1)}, f32[144,128]{1,0:T(8,128)S(1)}, u32[]{:S(2)}, u32[]{:S(2)}) collective-permute-start(f32[144,128]{1,0:T(8,128)S(1)} %get-tuple-element.73), channel_id=1, source_target_pairs={{0,12},{1,7},{2,14},{3,5},{4,8},{5,3},{6,10},{7,1},{8,4},{9,15},{1... | collective-permute-start | bytes 221192 | tf_op jit(solution)/shard_map/ppermute | solution.py:386
  47.4 2.1 %collective-permute-start.16 = (f32[152,128]{1,0:T(8,128)S(1)}, f32[152,128]{1,0:T(8,128)S(1)}, u32[]{:S(2)}, u32[]{:S(2)}) collective-permute-start(f32[152,128]{1,0:T(8,128)S(1)} %shard_map.96.refs_2_), channel_id=1, source_target_pairs={{0,16},{1,17},{2,18},{3,19},{4,20},{5,21},{6,22},{7,23},{8,24},{9,... | collective-permute-start | bytes 233480 | tf_op jit(solution)/shard_map/ppermute | solution.py:386
  50.9 3.0 %collective-permute-start.10 = (f32[144,128]{1,0:T(8,128)S(1)}, f32[144,128]{1,0:T(8,128)S(1)}, u32[]{:S(2)}, u32[]{:S(2)}) collective-permute-start(f32[144,128]{1,0:T(8,128)S(1)} %shard_map.92.refs_0_), channel_id=1, source_target_pairs={{0,16},{1,17},{2,18},{3,19},{4,20},{5,21},{6,22},{7,23},{8,24},{9,... | collective-permute-start | bytes 221192 | tf_op jit(solution)/shard_map/ppermute | solution.py:386
  53.9 3.0 %collective-permute-done.10.refs_1_ = f32[144,128]{1,0:T(8,128)S(1)} collective-permute-done((f32[144,128]{1,0:T(8,128)S(1)}, f32[144,128]{1,0:T(8,128)S(1)}, u32[]{:S(2)}, u32[]{:S(2)}) %collective-permute-start.10) | collective-permute-done | bytes 73760 | tf_op jit(solution)/shard_map/ppermute | solution.py:386
  65.2 2.6 %collective-permute-done.26.even_ref.refs_12_ = f32[96,384]{1,0:T(8,128)S(1)} collective-permute-done((f32[96,384]{1,0:T(8,128)S(1)}, f32[96,384]{1,0:T(8,128)S(1)}, u32[]{:S(2)}, u32[]{:S(2)}) %collective-permute-start.26) | collective-permute-done | bytes 147488 | tf_op jit(solution)/shard_map/ppermute | solution.py:386
  69.1 2.7 %collective-permute-start.30 = (f32[96,384]{1,0:T(8,128)S(1)}, f32[96,384]{1,0:T(8,128)S(1)}, u32[]{:S(2)}, u32[]{:S(2)}) collective-permute-start(f32[96,384]{1,0:T(8,128)S(1)} %shard_map.98), channel_id=1, source_target_pairs={{0,4},{1,9},{2,6},{3,11},{4,0},{5,13},{6,2},{7,15},{8,12},{9,1},{1... | collective-permute-start | bytes 442376 | tf_op jit(solution)/shard_map/ppermute | solution.py:386
  72.8 2.1 %collective-permute-done.30.refs_16_ = f32[96,384]{1,0:T(8,128)S(1)} collective-permute-done((f32[96,384]{1,0:T(8,128)S(1)}, f32[96,384]{1,0:T(8,128)S(1)}, u32[]{:S(2)}, u32[]{:S(2)}) %collective-permute-start.30) | collective-permute-done | bytes 147488 | tf_op jit(solution)/shard_map/ppermute | solution.py:386
  76.3 3.9 %shard_map.99 = (bf16[4,1152,384]{2,1,0:T(8,128)(2,1)S(1)}, f32[8,384]{1,0:T(8,128)S(1)}) custom-call(s32[1,4]{1,0:T(1,128)S(1)} %copy-done.6, s32[1]{0:T(128)S(6)} %copy.9.refs_1_, f32[96,384]{1,0:T(8,128)S(1)} %get-tuple-element.87.refs_2_.refs_4_, f32[96,384]{1,0:T(8,128)S(1)} %collective-permute-done.17.refs_3_, ...), custom_call_target="tpu_custom_call" | custom-call | flops 1358954496 | bytes 4718592 | tf_op jit(solution)/shard_map/pallas_call | solution.py:182
  80.2 2.5 %shard_map.101 = (f32[1152,128]{1,0:T(8,128)S(1)}, f32[1152,128]{1,0:T(8,128)S(1)}, f32[8,128]{1,0:T(8,128)S(1)}) custom-call(s32[1,4]{1,0:T(1,128)S(1)} %copy-done.5, s32[1]{0:T(128)S(6)} %copy.9.refs_1_, f32[96,384]{1,0:T(8,128)S(1)} %get-tuple-element.87.refs_2_.refs_4_, f32[96,384]{1,0:T(8,128)S(1)} %collective-permute-done.17.refs_3_, ...), custom_call_target="tpu_custom_call" | custom-call | flops 679477248 | bytes 4718592 | tf_op jit(solution)/shard_map/pallas_call | solution.py:241
  82.7 3.1 %shard_map.105 = (f32[1160,128]{1,0:T(8,128)S(1)}, f32[1160,128]{1,0:T(8,128)S(1)}, f32[8,128]{1,0:T(8,128)}) custom-call(s32[1,4]{1,0:T(1,128)S(1)} %copy-done.5, s32[1]{0:T(128)S(6)} %copy.9.refs_1_, f32[96,384]{1,0:T(8,128)S(1)} %get-tuple-element.87.refs_2_.refs_4_, f32[96,384]{1,0:T(8,128)S(1)} %collective-permute-done.17.refs_3_, ...), custom_call_target="tpu_custom_call" | custom-call | flops 679477248 | bytes 4718592 | tf_op jit(solution)/shard_map/pallas_call | solution.py:241
  89.3 5.3 %collective-permute-done.39.recv_ref = f32[584,128]{1,0:T(8,128)S(1)} collective-permute-done((f32[584,128]{1,0:T(8,128)S(1)}, f32[584,128]{1,0:T(8,128)S(1)}, u32[]{:S(2)}, u32[]{:S(2)}) %collective-permute-start.39) | collective-permute-done | bytes 299040 | tf_op jit(solution)/shard_map/ppermute | solution.py:386
  94.7 2.3 %collective-permute-start.40 = (f32[152,128]{1,0:T(8,128)S(1)}, f32[152,128]{1,0:T(8,128)S(1)}, u32[]{:S(2)}, u32[]{:S(2)}) collective-permute-start(f32[152,128]{1,0:T(8,128)S(1)} %get-tuple-element.105), channel_id=1, source_target_pairs={{0,10},{1,7},{2,8},{3,5},{4,14},{5,3},{6,12},{7,1},{8,2},{9,15},{1... | collective-permute-start | bytes 233480 | tf_op jit(solution)/shard_map/ppermute | solution.py:386
  102.6 2.0 %collective-permute-start.43 = (f32[152,128]{1,0:T(8,128)S(1)}, f32[152,128]{1,0:T(8,128)S(1)}, u32[]{:S(2)}, u32[]{:S(2)}) collective-permute-start(f32[152,128]{1,0:T(8,128)S(1)} %shard_map.108.refs_2_), channel_id=1, source_target_pairs={{0,16},{1,17},{2,18},{3,19},{4,20},{5,21},{6,22},{7,23},{8,24},{9,... | collective-permute-start | bytes 233480 | tf_op jit(solution)/shard_map/ppermute | solution.py:386
  106.4 2.6 %collective-permute-start.37 = (f32[144,128]{1,0:T(8,128)S(1)}, f32[144,128]{1,0:T(8,128)S(1)}, u32[]{:S(2)}, u32[]{:S(2)}) collective-permute-start(f32[144,128]{1,0:T(8,128)S(1)} %shard_map.104.refs_0_), channel_id=1, source_target_pairs={{0,16},{1,17},{2,18},{3,19},{4,20},{5,21},{6,22},{7,23},{8,24},{9,... | collective-permute-start | bytes 221192 | tf_op jit(solution)/shard_map/ppermute | solution.py:386
  109.0 3.5 %collective-permute-done.37.refs_1_ = f32[144,128]{1,0:T(8,128)S(1)} collective-permute-done((f32[144,128]{1,0:T(8,128)S(1)}, f32[144,128]{1,0:T(8,128)S(1)}, u32[]{:S(2)}, u32[]{:S(2)}) %collective-permute-start.37) | collective-permute-done | bytes 73760 | tf_op jit(solution)/shard_map/ppermute | solution.py:386
  113.5 2.7 %collective-permute-start.46 = (f32[96,384]{1,0:T(8,128)S(1)}, f32[96,384]{1,0:T(8,128)S(1)}, u32[]{:S(2)}, u32[]{:S(2)}) collective-permute-start(f32[96,384]{1,0:T(8,128)S(1)} %get-tuple-element.108.refs_0_), channel_id=1, source_target_pairs={{0,12},{1,13},{2,14},{3,15},{4,8},{5,9},{6,10},{7,11},{8,4},{9,5},... | collective-permute-start | bytes 442376 | tf_op jit(solution)/shard_map/ppermute | solution.py:386
  (115 shorter events, 45.6 us)
Async XLA Ops:
  1.7 10.9 %collective-permute-start.1 = (f32[192,384]{1,0:T(8,128)S(1)}, f32[192,384]{1,0:T(8,128)S(1)}, u32[]{:S(2)}, u32[]{:S(2)}) collective-permute-start(f32[192,384]{1,0:T(8,128)S(1)} %slice_bitcast_fusion), channel_id=1, source_target_pairs={{0,2},{1,3},{2,0},{3,1},{4,6},{5,7},{6,4},{7,5},{8,10},{9,11},{10,... | collective-permute-start | bytes 884744 | tf_op jit(solution)/shard_map/ppermute | solution.py:386
  4.8 14.0 %collective-permute-start = (f32[384,384]{1,0:T(8,128)}, f32[384,384]{1,0:T(8,128)S(1)}, u32[]{:S(2)}, u32[]{:S(2)}) collective-permute-start(f32[384,384]{1,0:T(8,128)} %bitcast.5), channel_id=1, source_target_pairs={{0,1},{1,0},{2,3},{3,2},{4,5},{5,4},{6,7},{7,6},{8,9},{9,8},{10,11... | collective-permute-start | bytes 1769480 | tf_op jit(solution)/shard_map/ppermute | solution.py:386
  5.7 12.3 %collective-permute-start.3 = (f32[192,384]{1,0:T(8,128)S(1)}, f32[192,384]{1,0:T(8,128)S(1)}, u32[]{:S(2)}, u32[]{:S(2)}) collective-permute-start(f32[192,384]{1,0:T(8,128)S(1)} %slice.20), channel_id=1, source_target_pairs={{0,2},{1,3},{2,0},{3,1},{4,6},{5,7},{6,4},{7,5},{8,10},{9,11},{10,... | collective-permute-start | bytes 884744 | tf_op jit(solution)/shard_map/ppermute | solution.py:386
  32.3 6.8 %collective-permute-start.12 = (f32[584,128]{1,0:T(8,128)S(1)}, f32[584,128]{1,0:T(8,128)S(1)}, u32[]{:S(2)}, u32[]{:S(2)}) collective-permute-start(f32[584,128]{1,0:T(8,128)S(1)} %get-tuple-element.80), channel_id=1, source_target_pairs={{0,4},{1,9},{2,6},{3,11},{4,0},{5,13},{6,2},{7,15},{8,12},{9,1},{1... | collective-permute-start | bytes 897032 | tf_op jit(solution)/shard_map/ppermute | solution.py:386
  33.1 9.6 %collective-permute-start.6 = (f32[576,128]{1,0:T(8,128)S(1)}, f32[576,128]{1,0:T(8,128)S(1)}, u32[]{:S(2)}, u32[]{:S(2)}) collective-permute-start(f32[576,128]{1,0:T(8,128)S(1)} %get-tuple-element.71), channel_id=1, source_target_pairs={{0,2},{1,9},{2,0},{3,11},{4,6},{5,13},{6,4},{7,15},{8,10},{9,1},{1... | collective-permute-start | bytes 884744 | tf_op jit(solution)/shard_map/ppermute | solution.py:386
  39.2 7.1 %collective-permute-start.13 = (f32[152,128]{1,0:T(8,128)S(1)}, f32[152,128]{1,0:T(8,128)S(1)}, u32[]{:S(2)}, u32[]{:S(2)}) collective-permute-start(f32[152,128]{1,0:T(8,128)S(1)} %get-tuple-element.82), channel_id=1, source_target_pairs={{0,10},{1,7},{2,8},{3,5},{4,14},{5,3},{6,12},{7,1},{8,2},{9,15},{1... | collective-permute-start | bytes 233480 | tf_op jit(solution)/shard_map/ppermute | solution.py:386
  42.8 6.8 %collective-permute-start.7 = (f32[144,128]{1,0:T(8,128)S(1)}, f32[144,128]{1,0:T(8,128)S(1)}, u32[]{:S(2)}, u32[]{:S(2)}) collective-permute-start(f32[144,128]{1,0:T(8,128)S(1)} %get-tuple-element.73), channel_id=1, source_target_pairs={{0,12},{1,7},{2,14},{3,5},{4,8},{5,3},{6,10},{7,1},{8,4},{9,15},{1... | collective-permute-start | bytes 221192 | tf_op jit(solution)/shard_map/ppermute | solution.py:386
  47.4 9.5 %collective-permute-start.16 = (f32[152,128]{1,0:T(8,128)S(1)}, f32[152,128]{1,0:T(8,128)S(1)}, u32[]{:S(2)}, u32[]{:S(2)}) collective-permute-start(f32[152,128]{1,0:T(8,128)S(1)} %shard_map.96.refs_2_), channel_id=1, source_target_pairs={{0,16},{1,17},{2,18},{3,19},{4,20},{5,21},{6,22},{7,23},{8,24},{9,... | collective-permute-start | bytes 233480 | tf_op jit(solution)/shard_map/ppermute | solution.py:386
  57.0 6.5 %collective-permute-start.18 = (f32[96,384]{1,0:T(8,128)S(1)}, f32[96,384]{1,0:T(8,128)S(1)}, u32[]{:S(2)}, u32[]{:S(2)}) collective-permute-start(f32[96,384]{1,0:T(8,128)S(1)} %get-tuple-element.87.refs_2_.refs_4_), channel_id=1, source_target_pairs={{0,8},{1,9},{2,10},{3,11},{4,12},{5,13},{6,14},{7,15},{8,0},{9,1},... | collective-permute-start | bytes 442376 | tf_op jit(solution)/shard_map/ppermute | solution.py:386
  57.1 7.3 %collective-permute-start.20 = (f32[96,384]{1,0:T(8,128)S(1)}, f32[96,384]{1,0:T(8,128)S(1)}, u32[]{:S(2)}, u32[]{:S(2)}) collective-permute-start(f32[96,384]{1,0:T(8,128)S(1)} %get-tuple-element.87.refs_2_.refs_4_), channel_id=1, source_target_pairs={{0,4},{1,5},{2,6},{3,7},{4,0},{5,1},{6,2},{7,3},{8,12},{9,13},{10,... | collective-permute-start | bytes 442376 | tf_op jit(solution)/shard_map/ppermute | solution.py:386
  58.8 9.1 %collective-permute-start.26 = (f32[96,384]{1,0:T(8,128)S(1)}, f32[96,384]{1,0:T(8,128)S(1)}, u32[]{:S(2)}, u32[]{:S(2)}) collective-permute-start(f32[96,384]{1,0:T(8,128)S(1)} %get-tuple-element.87.refs_2_.refs_4_), channel_id=1, source_target_pairs={{0,10},{1,11},{2,8},{3,9},{4,14},{5,15},{6,12},{7,13},{8,2},{9,3},... | collective-permute-start | bytes 442376 | tf_op jit(solution)/shard_map/ppermute | solution.py:386
  60.8 8.3 %collective-permute-start.28 = (f32[96,384]{1,0:T(8,128)S(1)}, f32[96,384]{1,0:T(8,128)S(1)}, u32[]{:S(2)}, u32[]{:S(2)}) collective-permute-start(f32[96,384]{1,0:T(8,128)S(1)} %get-tuple-element.87.refs_2_.refs_4_), channel_id=1, source_target_pairs={{0,6},{1,7},{2,4},{3,5},{4,2},{5,3},{6,0},{7,1},{8,14},{9,15},{10,... | collective-permute-start | bytes 442376 | tf_op jit(solution)/shard_map/ppermute | solution.py:386
  62.0 7.0 %collective-permute-start.17 = (f32[96,384]{1,0:T(8,128)S(1)}, f32[96,384]{1,0:T(8,128)S(1)}, u32[]{:S(2)}, u32[]{:S(2)}) collective-permute-start(f32[96,384]{1,0:T(8,128)S(1)} %get-tuple-element.87.refs_2_.refs_4_), channel_id=1, source_target_pairs={{0,1},{1,0},{2,3},{3,2},{4,5},{5,4},{6,7},{7,6},{8,9},{9,8},{10,11... | collective-permute-start | bytes 442376 | tf_op jit(solution)/shard_map/ppermute | solution.py:386
  63.5 8.3 %collective-permute-start.22 = (f32[96,384]{1,0:T(8,128)S(1)}, f32[96,384]{1,0:T(8,128)S(1)}, u32[]{:S(2)}, u32[]{:S(2)}) collective-permute-start(f32[96,384]{1,0:T(8,128)S(1)} %get-tuple-element.87.refs_2_.refs_4_), channel_id=1, source_target_pairs={{0,12},{1,13},{2,14},{3,15},{4,8},{5,9},{6,10},{7,11},{8,4},{9,5},... | collective-permute-start | bytes 442376 | tf_op jit(solution)/shard_map/ppermute | solution.py:386
  64.4 7.4 %collective-permute-start.24 = (f32[96,384]{1,0:T(8,128)S(1)}, f32[96,384]{1,0:T(8,128)S(1)}, u32[]{:S(2)}, u32[]{:S(2)}) collective-permute-start(f32[96,384]{1,0:T(8,128)S(1)} %get-tuple-element.87.refs_2_.refs_4_), channel_id=1, source_target_pairs={{0,2},{1,3},{2,0},{3,1},{4,6},{5,7},{6,4},{7,5},{8,10},{9,11},{10,... | collective-permute-start | bytes 442376 | tf_op jit(solution)/shard_map/ppermute | solution.py:386
  87.8 6.8 %collective-permute-start.39 = (f32[584,128]{1,0:T(8,128)S(1)}, f32[584,128]{1,0:T(8,128)S(1)}, u32[]{:S(2)}, u32[]{:S(2)}) collective-permute-start(f32[584,128]{1,0:T(8,128)S(1)} %get-tuple-element.103), channel_id=1, source_target_pairs={{0,4},{1,9},{2,6},{3,11},{4,0},{5,13},{6,2},{7,15},{8,12},{9,1},{1... | collective-permute-start | bytes 897032 | tf_op jit(solution)/shard_map/ppermute | solution.py:386
  88.7 9.6 %collective-permute-start.33 = (f32[576,128]{1,0:T(8,128)S(1)}, f32[576,128]{1,0:T(8,128)S(1)}, u32[]{:S(2)}, u32[]{:S(2)}) collective-permute-start(f32[576,128]{1,0:T(8,128)S(1)} %get-tuple-element.94), channel_id=1, source_target_pairs={{0,2},{1,9},{2,0},{3,11},{4,6},{5,13},{6,4},{7,15},{8,10},{9,1},{1... | collective-permute-start | bytes 884744 | tf_op jit(solution)/shard_map/ppermute | solution.py:386
  94.7 6.5 %collective-permute-start.40 = (f32[152,128]{1,0:T(8,128)S(1)}, f32[152,128]{1,0:T(8,128)S(1)}, u32[]{:S(2)}, u32[]{:S(2)}) collective-permute-start(f32[152,128]{1,0:T(8,128)S(1)} %get-tuple-element.105), channel_id=1, source_target_pairs={{0,10},{1,7},{2,8},{3,5},{4,14},{5,3},{6,12},{7,1},{8,2},{9,15},{1... | collective-permute-start | bytes 233480 | tf_op jit(solution)/shard_map/ppermute | solution.py:386
  98.3 6.4 %collective-permute-start.34 = (f32[144,128]{1,0:T(8,128)S(1)}, f32[144,128]{1,0:T(8,128)S(1)}, u32[]{:S(2)}, u32[]{:S(2)}) collective-permute-start(f32[144,128]{1,0:T(8,128)S(1)} %get-tuple-element.96), channel_id=1, source_target_pairs={{0,12},{1,7},{2,14},{3,5},{4,8},{5,3},{6,10},{7,1},{8,4},{9,15},{1... | collective-permute-start | bytes 221192 | tf_op jit(solution)/shard_map/ppermute | solution.py:386
  102.6 9.9 %collective-permute-start.43 = (f32[152,128]{1,0:T(8,128)S(1)}, f32[152,128]{1,0:T(8,128)S(1)}, u32[]{:S(2)}, u32[]{:S(2)}) collective-permute-start(f32[152,128]{1,0:T(8,128)S(1)} %shard_map.108.refs_2_), channel_id=1, source_target_pairs={{0,16},{1,17},{2,18},{3,19},{4,20},{5,21},{6,22},{7,23},{8,24},{9,... | collective-permute-start | bytes 233480 | tf_op jit(solution)/shard_map/ppermute | solution.py:386
  106.4 6.2 %collective-permute-start.37 = (f32[144,128]{1,0:T(8,128)S(1)}, f32[144,128]{1,0:T(8,128)S(1)}, u32[]{:S(2)}, u32[]{:S(2)}) collective-permute-start(f32[144,128]{1,0:T(8,128)S(1)} %shard_map.104.refs_0_), channel_id=1, source_target_pairs={{0,16},{1,17},{2,18},{3,19},{4,20},{5,21},{6,22},{7,23},{8,24},{9,... | collective-permute-start | bytes 221192 | tf_op jit(solution)/shard_map/ppermute | solution.py:386
  112.6 6.8 %collective-permute-start.44 = (f32[96,384]{1,0:T(8,128)S(1)}, f32[96,384]{1,0:T(8,128)S(1)}, u32[]{:S(2)}, u32[]{:S(2)}) collective-permute-start(f32[96,384]{1,0:T(8,128)S(1)} %get-tuple-element.108.refs_0_), channel_id=1, source_target_pairs={{0,8},{1,9},{2,10},{3,11},{4,12},{5,13},{6,14},{7,15},{8,0},{9,1},... | collective-permute-start | bytes 442376 | tf_op jit(solution)/shard_map/ppermute | solution.py:386
  112.7 8.4 %collective-permute-start.45 = (f32[96,384]{1,0:T(8,128)S(1)}, f32[96,384]{1,0:T(8,128)S(1)}, u32[]{:S(2)}, u32[]{:S(2)}) collective-permute-start(f32[96,384]{1,0:T(8,128)S(1)} %get-tuple-element.108.refs_0_), channel_id=1, source_target_pairs={{0,4},{1,5},{2,6},{3,7},{4,0},{5,1},{6,2},{7,3},{8,12},{9,13},{10,... | collective-permute-start | bytes 442376 | tf_op jit(solution)/shard_map/ppermute | solution.py:386
  113.5 7.6 %collective-permute-start.46 = (f32[96,384]{1,0:T(8,128)S(1)}, f32[96,384]{1,0:T(8,128)S(1)}, u32[]{:S(2)}, u32[]{:S(2)}) collective-permute-start(f32[96,384]{1,0:T(8,128)S(1)} %get-tuple-element.108.refs_0_), channel_id=1, source_target_pairs={{0,12},{1,13},{2,14},{3,15},{4,8},{5,9},{6,10},{7,11},{8,4},{9,5},... | collective-permute-start | bytes 442376 | tf_op jit(solution)/shard_map/ppermute | solution.py:386
  (30 other events, 136.1 us)

commit v8 on v7

--- a/solution.py
+++ b/solution.py
@@ -395,8 +395,7 @@
     rows = b // CHUNKS
     far = []
     for h in range(CHUNKS):
-        block = own if h == 0 else lax.optimization_barrier(own)
-        far.append(swap(block[h * rows:(h + 1) * rows], [DIMS[0]]))
+        far.append(swap(own[h * rows:(h + 1) * rows], [DIMS[0]]))
     beside = swap(own, [CORE])
     left, right, vec, diag = prepare(left_ops, right_ops, psi_start, diagonal)
     far[0], left, right, vec, diag = lax.optimization_barrier((far[0], left, right, vec, diag))
@@ -451,7 +450,7 @@
             pieces = []
             for k in range(8):
                 pieces += [got[k], swap(got[k], [CORE])]
-    got = {k: swap(vec, dims_of(k)) for k in (3, 2, 1)}
+    got = {k: swap(vec, dims_of(k)) for k in (2, 3, 1)}
     block = join([vec, got[1], got[2], got[3]])
     return block, jnp.stack(energies)
 

time: 122 us -> 122 us (level)
    ppermute x47, waiting for transfers between devices: 42.8 us -> 44 us  [swap(): lax.ppermute(x, AXES, flips(mesh_shape, even, even if odd is None else odd))]
  transfers between devices with their start and end apart: 47 -> 47, of which waited for: 22 -> 22; matrix products, arithmetic and copies ran while one was open for 3% -> 2% of each run, Pallas kernels for 4% -> 4%
where the time goes in v8:
time: 122 us
  waiting for transfers between devices  44 us (36%)
  starting transfers between devices  43.6 us (36%)
  Pallas kernels  23.4 us (19%)
  local copies, waits for them, and re-layouts  7.67 us (6%)
  other arithmetic  1.85 us (2%)
  between operations  1.56 us (1%)
    ppermute x47, waiting for transfers between devices, swap(): lax.ppermute(x, AXES, flips(mesh_shape, even, even if odd is None else odd))  44 us
    ppermute x47, starting transfers between devices, swap(): lax.ppermute(x, AXES, flips(mesh_shape, even, even if odd is None else odd))  43.6 us
    pallas_call x4, Pallas kernels, outer(): pl.pallas_call(functools.partial(outer_kernel, first, chunk, cells, len(p...  11.1 us
    pallas_call x3, Pallas kernels, inner(): pl.pallas_call(functools.partial(inner_kernel, first, half, cells, len(pi...  9.73 us
    unnamed x14, local copies, waits for them, and re-layouts  5.47 us
  transfers between devices with their start and end apart: 47, of which 22 were waited for; matrix products, arithmetic and copies ran while one was open for 2% of the time, Pallas kernels for 4%

profile of v8, /device:TPU:0, one launch (start us, length us, event | category | flops | bytes accessed | tf_op | source)
XLA Modules:
  0.0 122.1 jit_solution(152162268396266030)
XLA Ops:
  1.8 3.1 %collective-permute-start.1 = (f32[192,384]{1,0:T(8,128)S(1)}, f32[192,384]{1,0:T(8,128)S(1)}, u32[]{:S(2)}, u32[]{:S(2)}) collective-permute-start(f32[192,384]{1,0:T(8,128)S(1)} %get-tuple-element.111), channel_id=1, source_target_pairs={{0,2},{1,3},{2,0},{3,1},{4,6},{5,7},{6,4},{7,5},{8,10},{9,11},{10,... | collective-permute-start | bytes 884744 | tf_op jit(solution)/shard_map/ppermute | solution.py:386
  12.7 5.5 %collective-permute-done.3.refs_4_.refs_6_ = f32[192,384]{1,0:T(8,128)S(1)} collective-permute-done((f32[192,384]{1,0:T(8,128)S(1)}, f32[192,384]{1,0:T(8,128)S(1)}, u32[]{:S(2)}, u32[]{:S(2)}) %collective-permute-start.3) | collective-permute-done | bytes 294944 | tf_op jit(solution)/shard_map/ppermute | solution.py:386
  18.9 2.9 %shard_map.87 = (bf16[4,192,384]{2,1,0:T(8,128)(2,1)S(1)}, bf16[4,192,384]{2,1,0:T(8,128)(2,1)S(1)}, f32[8,384]{1,0:T(8,128)S(1)}) custom-call(s32[1,4]{1,0:T(1,128)S(1)} %copy-done.6, s32[1]{0:T(128)S(6)} %copy.9.refs_1_, f32[384,384]{1,0:T(8,128)S(1)} %bitcast.8, f32[384,384]{1,0:T(8,128)S(1)} %collective-permute-done.refs_3_, ...), custom_call_target="tpu_custom_call" | custom-call | flops 679477248 | bytes 4718592 | tf_op jit(solution)/shard_map/pallas_call | solution.py:182
  21.8 3.0 %shard_map.88 = (bf16[4,1152,384]{2,1,0:T(8,128)(2,1)S(1)}, f32[8,384]{1,0:T(8,128)S(1)}) custom-call(s32[1,4]{1,0:T(1,128)S(1)} %copy-done.6, s32[1]{0:T(128)S(6)} %copy.9.refs_1_, f32[384,384]{1,0:T(8,128)S(1)} %bitcast.9, f32[384,384]{1,0:T(8,128)S(1)} %collective-permute-done.refs_3_, f32[192,384]{1,0:T(8,128)S(1)} %collective-permute-done.3.refs_4_.refs_6_, ...), custom_call_target="tpu_custom_call" | custom-call | flops 679477248 | bytes 4718592 | tf_op jit(solution)/shard_map/pallas_call | solution.py:182
  24.8 2.5 %shard_map.89 = (f32[1152,128]{1,0:T(8,128)S(1)}, f32[1152,128]{1,0:T(8,128)S(1)}, f32[8,128]{1,0:T(8,128)S(1)}) custom-call(s32[1,4]{1,0:T(1,128)S(1)} %copy-done.5, s32[1]{0:T(128)S(6)} %copy.9.refs_1_, f32[384,384]{1,0:T(8,128)S(1)} %bitcast.10, f32[384,384]{1,0:T(8,128)S(1)} %collective-permute-done.refs_3_, ...), custom_call_target="tpu_custom_call" | custom-call | flops 679477248 | bytes 4718592 | tf_op jit(solution)/shard_map/pallas_call | solution.py:241
  27.3 3.1 %shard_map.93 = (f32[1160,128]{1,0:T(8,128)S(1)}, f32[1160,128]{1,0:T(8,128)S(1)}, f32[8,128]{1,0:T(8,128)}) custom-call(s32[1,4]{1,0:T(1,128)S(1)} %copy-done.5, s32[1]{0:T(128)S(6)} %copy.9.refs_1_, f32[384,384]{1,0:T(8,128)S(1)} %bitcast.11, f32[384,384]{1,0:T(8,128)S(1)} %collective-permute-done.refs_3_, f32[192,384]{1,0:T(8,128)S(1)} %collective-permute-done.1.refs_4_, ...), custom_call_target="tpu_custom_call" | custom-call | flops 679477248 | bytes 4718592 | tf_op jit(solution)/shard_map/pallas_call | solution.py:241
  33.4 5.8 %collective-permute-done.12.recv_ref = f32[584,128]{1,0:T(8,128)S(1)} collective-permute-done((f32[584,128]{1,0:T(8,128)S(1)}, f32[584,128]{1,0:T(8,128)S(1)}, u32[]{:S(2)}, u32[]{:S(2)}) %collective-permute-start.12) | collective-permute-done | bytes 299040 | tf_op jit(solution)/shard_map/ppermute | solution.py:386
  39.3 2.8 %collective-permute-start.13 = (f32[152,128]{1,0:T(8,128)S(1)}, f32[152,128]{1,0:T(8,128)S(1)}, u32[]{:S(2)}, u32[]{:S(2)}) collective-permute-start(f32[152,128]{1,0:T(8,128)S(1)} %get-tuple-element.82), channel_id=1, source_target_pairs={{0,10},{1,7},{2,8},{3,5},{4,14},{5,3},{6,12},{7,1},{8,2},{9,15},{1... | collective-permute-start | bytes 233480 | tf_op jit(solution)/shard_map/ppermute | solution.py:386
  42.9 2.9 %collective-permute-start.7 = (f32[144,128]{1,0:T(8,128)S(1)}, f32[144,128]{1,0:T(8,128)S(1)}, u32[]{:S(2)}, u32[]{:S(2)}) collective-permute-start(f32[144,128]{1,0:T(8,128)S(1)} %get-tuple-element.73), channel_id=1, source_target_pairs={{0,12},{1,7},{2,14},{3,5},{4,8},{5,3},{6,10},{7,1},{8,4},{9,15},{1... | collective-permute-start | bytes 221192 | tf_op jit(solution)/shard_map/ppermute | solution.py:386
  47.5 2.2 %collective-permute-start.16 = (f32[152,128]{1,0:T(8,128)S(1)}, f32[152,128]{1,0:T(8,128)S(1)}, u32[]{:S(2)}, u32[]{:S(2)}) collective-permute-start(f32[152,128]{1,0:T(8,128)S(1)} %shard_map.96.refs_2_), channel_id=1, source_target_pairs={{0,16},{1,17},{2,18},{3,19},{4,20},{5,21},{6,22},{7,23},{8,24},{9,... | collective-permute-start | bytes 233480 | tf_op jit(solution)/shard_map/ppermute | solution.py:386
  51.0 3.0 %collective-permute-start.10 = (f32[144,128]{1,0:T(8,128)S(1)}, f32[144,128]{1,0:T(8,128)S(1)}, u32[]{:S(2)}, u32[]{:S(2)}) collective-permute-start(f32[144,128]{1,0:T(8,128)S(1)} %shard_map.92.refs_0_), channel_id=1, source_target_pairs={{0,16},{1,17},{2,18},{3,19},{4,20},{5,21},{6,22},{7,23},{8,24},{9,... | collective-permute-start | bytes 221192 | tf_op jit(solution)/shard_map/ppermute | solution.py:386
  54.0 3.0 %collective-permute-done.10.refs_1_ = f32[144,128]{1,0:T(8,128)S(1)} collective-permute-done((f32[144,128]{1,0:T(8,128)S(1)}, f32[144,128]{1,0:T(8,128)S(1)}, u32[]{:S(2)}, u32[]{:S(2)}) %collective-permute-start.10) | collective-permute-done | bytes 73760 | tf_op jit(solution)/shard_map/ppermute | solution.py:386
  65.3 2.6 %collective-permute-done.26.even_ref.refs_12_ = f32[96,384]{1,0:T(8,128)S(1)} collective-permute-done((f32[96,384]{1,0:T(8,128)S(1)}, f32[96,384]{1,0:T(8,128)S(1)}, u32[]{:S(2)}, u32[]{:S(2)}) %collective-permute-start.26) | collective-permute-done | bytes 147488 | tf_op jit(solution)/shard_map/ppermute | solution.py:386
  69.2 2.7 %collective-permute-start.30 = (f32[96,384]{1,0:T(8,128)S(1)}, f32[96,384]{1,0:T(8,128)S(1)}, u32[]{:S(2)}, u32[]{:S(2)}) collective-permute-start(f32[96,384]{1,0:T(8,128)S(1)} %shard_map.98), channel_id=1, source_target_pairs={{0,4},{1,9},{2,6},{3,11},{4,0},{5,13},{6,2},{7,15},{8,12},{9,1},{1... | collective-permute-start | bytes 442376 | tf_op jit(solution)/shard_map/ppermute | solution.py:386
  73.0 2.1 %collective-permute-done.30.refs_16_ = f32[96,384]{1,0:T(8,128)S(1)} collective-permute-done((f32[96,384]{1,0:T(8,128)S(1)}, f32[96,384]{1,0:T(8,128)S(1)}, u32[]{:S(2)}, u32[]{:S(2)}) %collective-permute-start.30) | collective-permute-done | bytes 147488 | tf_op jit(solution)/shard_map/ppermute | solution.py:386
  76.4 3.9 %shard_map.99 = (bf16[4,1152,384]{2,1,0:T(8,128)(2,1)S(1)}, f32[8,384]{1,0:T(8,128)S(1)}) custom-call(s32[1,4]{1,0:T(1,128)S(1)} %copy-done.6, s32[1]{0:T(128)S(6)} %copy.9.refs_1_, f32[96,384]{1,0:T(8,128)S(1)} %get-tuple-element.87.refs_2_.refs_4_, f32[96,384]{1,0:T(8,128)S(1)} %collective-permute-done.17.refs_3_, ...), custom_call_target="tpu_custom_call" | custom-call | flops 1358954496 | bytes 4718592 | tf_op jit(solution)/shard_map/pallas_call | solution.py:182
  80.3 2.5 %shard_map.101 = (f32[1152,128]{1,0:T(8,128)S(1)}, f32[1152,128]{1,0:T(8,128)S(1)}, f32[8,128]{1,0:T(8,128)S(1)}) custom-call(s32[1,4]{1,0:T(1,128)S(1)} %copy-done.5, s32[1]{0:T(128)S(6)} %copy.9.refs_1_, f32[96,384]{1,0:T(8,128)S(1)} %get-tuple-element.87.refs_2_.refs_4_, f32[96,384]{1,0:T(8,128)S(1)} %collective-permute-done.17.refs_3_, ...), custom_call_target="tpu_custom_call" | custom-call | flops 679477248 | bytes 4718592 | tf_op jit(solution)/shard_map/pallas_call | solution.py:241
  82.8 3.1 %shard_map.105 = (f32[1160,128]{1,0:T(8,128)S(1)}, f32[1160,128]{1,0:T(8,128)S(1)}, f32[8,128]{1,0:T(8,128)}) custom-call(s32[1,4]{1,0:T(1,128)S(1)} %copy-done.5, s32[1]{0:T(128)S(6)} %copy.9.refs_1_, f32[96,384]{1,0:T(8,128)S(1)} %get-tuple-element.87.refs_2_.refs_4_, f32[96,384]{1,0:T(8,128)S(1)} %collective-permute-done.17.refs_3_, ...), custom_call_target="tpu_custom_call" | custom-call | flops 679477248 | bytes 4718592 | tf_op jit(solution)/shard_map/pallas_call | solution.py:241
  89.4 5.3 %collective-permute-done.39.recv_ref = f32[584,128]{1,0:T(8,128)S(1)} collective-permute-done((f32[584,128]{1,0:T(8,128)S(1)}, f32[584,128]{1,0:T(8,128)S(1)}, u32[]{:S(2)}, u32[]{:S(2)}) %collective-permute-start.39) | collective-permute-done | bytes 299040 | tf_op jit(solution)/shard_map/ppermute | solution.py:386
  94.8 2.3 %collective-permute-start.40 = (f32[152,128]{1,0:T(8,128)S(1)}, f32[152,128]{1,0:T(8,128)S(1)}, u32[]{:S(2)}, u32[]{:S(2)}) collective-permute-start(f32[152,128]{1,0:T(8,128)S(1)} %get-tuple-element.105), channel_id=1, source_target_pairs={{0,10},{1,7},{2,8},{3,5},{4,14},{5,3},{6,12},{7,1},{8,2},{9,15},{1... | collective-permute-start | bytes 233480 | tf_op jit(solution)/shard_map/ppermute | solution.py:386
  102.7 2.1 %collective-permute-start.43 = (f32[152,128]{1,0:T(8,128)S(1)}, f32[152,128]{1,0:T(8,128)S(1)}, u32[]{:S(2)}, u32[]{:S(2)}) collective-permute-start(f32[152,128]{1,0:T(8,128)S(1)} %shard_map.108.refs_2_), channel_id=1, source_target_pairs={{0,16},{1,17},{2,18},{3,19},{4,20},{5,21},{6,22},{7,23},{8,24},{9,... | collective-permute-start | bytes 233480 | tf_op jit(solution)/shard_map/ppermute | solution.py:386
  106.5 2.7 %collective-permute-start.37 = (f32[144,128]{1,0:T(8,128)S(1)}, f32[144,128]{1,0:T(8,128)S(1)}, u32[]{:S(2)}, u32[]{:S(2)}) collective-permute-start(f32[144,128]{1,0:T(8,128)S(1)} %shard_map.104.refs_0_), channel_id=1, source_target_pairs={{0,16},{1,17},{2,18},{3,19},{4,20},{5,21},{6,22},{7,23},{8,24},{9,... | collective-permute-start | bytes 221192 | tf_op jit(solution)/shard_map/ppermute | solution.py:386
  109.1 3.5 %collective-permute-done.37.refs_1_ = f32[144,128]{1,0:T(8,128)S(1)} collective-permute-done((f32[144,128]{1,0:T(8,128)S(1)}, f32[144,128]{1,0:T(8,128)S(1)}, u32[]{:S(2)}, u32[]{:S(2)}) %collective-permute-start.37) | collective-permute-done | bytes 73760 | tf_op jit(solution)/shard_map/ppermute | solution.py:386
  113.6 2.7 %collective-permute-start.46 = (f32[96,384]{1,0:T(8,128)S(1)}, f32[96,384]{1,0:T(8,128)S(1)}, u32[]{:S(2)}, u32[]{:S(2)}) collective-permute-start(f32[96,384]{1,0:T(8,128)S(1)} %get-tuple-element.108.refs_0_), channel_id=1, source_target_pairs={{0,12},{1,13},{2,14},{3,15},{4,8},{5,9},{6,10},{7,11},{8,4},{9,5},... | collective-permute-start | bytes 442376 | tf_op jit(solution)/shard_map/ppermute | solution.py:386
  (114 shorter events, 45.4 us)
Async XLA Ops:
  1.8 10.9 %collective-permute-start.1 = (f32[192,384]{1,0:T(8,128)S(1)}, f32[192,384]{1,0:T(8,128)S(1)}, u32[]{:S(2)}, u32[]{:S(2)}) collective-permute-start(f32[192,384]{1,0:T(8,128)S(1)} %get-tuple-element.111), channel_id=1, source_target_pairs={{0,2},{1,3},{2,0},{3,1},{4,6},{5,7},{6,4},{7,5},{8,10},{9,11},{10,... | collective-permute-start | bytes 884744 | tf_op jit(solution)/shard_map/ppermute | solution.py:386
  4.9 14.0 %collective-permute-start = (f32[384,384]{1,0:T(8,128)}, f32[384,384]{1,0:T(8,128)S(1)}, u32[]{:S(2)}, u32[]{:S(2)}) collective-permute-start(f32[384,384]{1,0:T(8,128)} %bitcast.7), channel_id=1, source_target_pairs={{0,1},{1,0},{2,3},{3,2},{4,5},{5,4},{6,7},{7,6},{8,9},{9,8},{10,11... | collective-permute-start | bytes 1769480 | tf_op jit(solution)/shard_map/ppermute | solution.py:386
  4.9 13.3 %collective-permute-start.3 = (f32[192,384]{1,0:T(8,128)S(1)}, f32[192,384]{1,0:T(8,128)S(1)}, u32[]{:S(2)}, u32[]{:S(2)}) collective-permute-start(f32[192,384]{1,0:T(8,128)S(1)} %get-tuple-element.110), channel_id=1, source_target_pairs={{0,2},{1,3},{2,0},{3,1},{4,6},{5,7},{6,4},{7,5},{8,10},{9,11},{10,... | collective-permute-start | bytes 884744 | tf_op jit(solution)/shard_map/ppermute | solution.py:386
  32.4 6.8 %collective-permute-start.12 = (f32[584,128]{1,0:T(8,128)S(1)}, f32[584,128]{1,0:T(8,128)S(1)}, u32[]{:S(2)}, u32[]{:S(2)}) collective-permute-start(f32[584,128]{1,0:T(8,128)S(1)} %get-tuple-element.80), channel_id=1, source_target_pairs={{0,4},{1,9},{2,6},{3,11},{4,0},{5,13},{6,2},{7,15},{8,12},{9,1},{1... | collective-permute-start | bytes 897032 | tf_op jit(solution)/shard_map/ppermute | solution.py:386
  33.2 9.6 %collective-permute-start.6 = (f32[576,128]{1,0:T(8,128)S(1)}, f32[576,128]{1,0:T(8,128)S(1)}, u32[]{:S(2)}, u32[]{:S(2)}) collective-permute-start(f32[576,128]{1,0:T(8,128)S(1)} %get-tuple-element.71), channel_id=1, source_target_pairs={{0,2},{1,9},{2,0},{3,11},{4,6},{5,13},{6,4},{7,15},{8,10},{9,1},{1... | collective-permute-start | bytes 884744 | tf_op jit(solution)/shard_map/ppermute | solution.py:386
  39.3 7.1 %collective-permute-start.13 = (f32[152,128]{1,0:T(8,128)S(1)}, f32[152,128]{1,0:T(8,128)S(1)}, u32[]{:S(2)}, u32[]{:S(2)}) collective-permute-start(f32[152,128]{1,0:T(8,128)S(1)} %get-tuple-element.82), channel_id=1, source_target_pairs={{0,10},{1,7},{2,8},{3,5},{4,14},{5,3},{6,12},{7,1},{8,2},{9,15},{1... | collective-permute-start | bytes 233480 | tf_op jit(solution)/shard_map/ppermute | solution.py:386
  42.9 6.8 %collective-permute-start.7 = (f32[144,128]{1,0:T(8,128)S(1)}, f32[144,128]{1,0:T(8,128)S(1)}, u32[]{:S(2)}, u32[]{:S(2)}) collective-permute-start(f32[144,128]{1,0:T(8,128)S(1)} %get-tuple-element.73), channel_id=1, source_target_pairs={{0,12},{1,7},{2,14},{3,5},{4,8},{5,3},{6,10},{7,1},{8,4},{9,15},{1... | collective-permute-start | bytes 221192 | tf_op jit(solution)/shard_map/ppermute | solution.py:386
  47.5 9.5 %collective-permute-start.16 = (f32[152,128]{1,0:T(8,128)S(1)}, f32[152,128]{1,0:T(8,128)S(1)}, u32[]{:S(2)}, u32[]{:S(2)}) collective-permute-start(f32[152,128]{1,0:T(8,128)S(1)} %shard_map.96.refs_2_), channel_id=1, source_target_pairs={{0,16},{1,17},{2,18},{3,19},{4,20},{5,21},{6,22},{7,23},{8,24},{9,... | collective-permute-start | bytes 233480 | tf_op jit(solution)/shard_map/ppermute | solution.py:386
  57.1 6.5 %collective-permute-start.18 = (f32[96,384]{1,0:T(8,128)S(1)}, f32[96,384]{1,0:T(8,128)S(1)}, u32[]{:S(2)}, u32[]{:S(2)}) collective-permute-start(f32[96,384]{1,0:T(8,128)S(1)} %get-tuple-element.87.refs_2_.refs_4_), channel_id=1, source_target_pairs={{0,8},{1,9},{2,10},{3,11},{4,12},{5,13},{6,14},{7,15},{8,0},{9,1},... | collective-permute-start | bytes 442376 | tf_op jit(solution)/shard_map/ppermute | solution.py:386
  57.2 7.3 %collective-permute-start.20 = (f32[96,384]{1,0:T(8,128)S(1)}, f32[96,384]{1,0:T(8,128)S(1)}, u32[]{:S(2)}, u32[]{:S(2)}) collective-permute-start(f32[96,384]{1,0:T(8,128)S(1)} %get-tuple-element.87.refs_2_.refs_4_), channel_id=1, source_target_pairs={{0,4},{1,5},{2,6},{3,7},{4,0},{5,1},{6,2},{7,3},{8,12},{9,13},{10,... | collective-permute-start | bytes 442376 | tf_op jit(solution)/shard_map/ppermute | solution.py:386
  58.9 9.1 %collective-permute-start.26 = (f32[96,384]{1,0:T(8,128)S(1)}, f32[96,384]{1,0:T(8,128)S(1)}, u32[]{:S(2)}, u32[]{:S(2)}) collective-permute-start(f32[96,384]{1,0:T(8,128)S(1)} %get-tuple-element.87.refs_2_.refs_4_), channel_id=1, source_target_pairs={{0,10},{1,11},{2,8},{3,9},{4,14},{5,15},{6,12},{7,13},{8,2},{9,3},... | collective-permute-start | bytes 442376 | tf_op jit(solution)/shard_map/ppermute | solution.py:386
  60.9 8.3 %collective-permute-start.28 = (f32[96,384]{1,0:T(8,128)S(1)}, f32[96,384]{1,0:T(8,128)S(1)}, u32[]{:S(2)}, u32[]{:S(2)}) collective-permute-start(f32[96,384]{1,0:T(8,128)S(1)} %get-tuple-element.87.refs_2_.refs_4_), channel_id=1, source_target_pairs={{0,6},{1,7},{2,4},{3,5},{4,2},{5,3},{6,0},{7,1},{8,14},{9,15},{10,... | collective-permute-start | bytes 442376 | tf_op jit(solution)/shard_map/ppermute | solution.py:386
  62.2 7.0 %collective-permute-start.17 = (f32[96,384]{1,0:T(8,128)S(1)}, f32[96,384]{1,0:T(8,128)S(1)}, u32[]{:S(2)}, u32[]{:S(2)}) collective-permute-start(f32[96,384]{1,0:T(8,128)S(1)} %get-tuple-element.87.refs_2_.refs_4_), channel_id=1, source_target_pairs={{0,1},{1,0},{2,3},{3,2},{4,5},{5,4},{6,7},{7,6},{8,9},{9,8},{10,11... | collective-permute-start | bytes 442376 | tf_op jit(solution)/shard_map/ppermute | solution.py:386
  63.7 8.3 %collective-permute-start.22 = (f32[96,384]{1,0:T(8,128)S(1)}, f32[96,384]{1,0:T(8,128)S(1)}, u32[]{:S(2)}, u32[]{:S(2)}) collective-permute-start(f32[96,384]{1,0:T(8,128)S(1)} %get-tuple-element.87.refs_2_.refs_4_), channel_id=1, source_target_pairs={{0,12},{1,13},{2,14},{3,15},{4,8},{5,9},{6,10},{7,11},{8,4},{9,5},... | collective-permute-start | bytes 442376 | tf_op jit(solution)/shard_map/ppermute | solution.py:386
  64.5 7.4 %collective-permute-start.24 = (f32[96,384]{1,0:T(8,128)S(1)}, f32[96,384]{1,0:T(8,128)S(1)}, u32[]{:S(2)}, u32[]{:S(2)}) collective-permute-start(f32[96,384]{1,0:T(8,128)S(1)} %get-tuple-element.87.refs_2_.refs_4_), channel_id=1, source_target_pairs={{0,2},{1,3},{2,0},{3,1},{4,6},{5,7},{6,4},{7,5},{8,10},{9,11},{10,... | collective-permute-start | bytes 442376 | tf_op jit(solution)/shard_map/ppermute | solution.py:386
  87.9 6.8 %collective-permute-start.39 = (f32[584,128]{1,0:T(8,128)S(1)}, f32[584,128]{1,0:T(8,128)S(1)}, u32[]{:S(2)}, u32[]{:S(2)}) collective-permute-start(f32[584,128]{1,0:T(8,128)S(1)} %get-tuple-element.103), channel_id=1, source_target_pairs={{0,4},{1,9},{2,6},{3,11},{4,0},{5,13},{6,2},{7,15},{8,12},{9,1},{1... | collective-permute-start | bytes 897032 | tf_op jit(solution)/shard_map/ppermute | solution.py:386
  88.8 9.6 %collective-permute-start.33 = (f32[576,128]{1,0:T(8,128)S(1)}, f32[576,128]{1,0:T(8,128)S(1)}, u32[]{:S(2)}, u32[]{:S(2)}) collective-permute-start(f32[576,128]{1,0:T(8,128)S(1)} %get-tuple-element.94), channel_id=1, source_target_pairs={{0,2},{1,9},{2,0},{3,11},{4,6},{5,13},{6,4},{7,15},{8,10},{9,1},{1... | collective-permute-start | bytes 884744 | tf_op jit(solution)/shard_map/ppermute | solution.py:386
  94.8 6.5 %collective-permute-start.40 = (f32[152,128]{1,0:T(8,128)S(1)}, f32[152,128]{1,0:T(8,128)S(1)}, u32[]{:S(2)}, u32[]{:S(2)}) collective-permute-start(f32[152,128]{1,0:T(8,128)S(1)} %get-tuple-element.105), channel_id=1, source_target_pairs={{0,10},{1,7},{2,8},{3,5},{4,14},{5,3},{6,12},{7,1},{8,2},{9,15},{1... | collective-permute-start | bytes 233480 | tf_op jit(solution)/shard_map/ppermute | solution.py:386
  98.4 6.4 %collective-permute-start.34 = (f32[144,128]{1,0:T(8,128)S(1)}, f32[144,128]{1,0:T(8,128)S(1)}, u32[]{:S(2)}, u32[]{:S(2)}) collective-permute-start(f32[144,128]{1,0:T(8,128)S(1)} %get-tuple-element.96), channel_id=1, source_target_pairs={{0,12},{1,7},{2,14},{3,5},{4,8},{5,3},{6,10},{7,1},{8,4},{9,15},{1... | collective-permute-start | bytes 221192 | tf_op jit(solution)/shard_map/ppermute | solution.py:386
  102.7 9.9 %collective-permute-start.43 = (f32[152,128]{1,0:T(8,128)S(1)}, f32[152,128]{1,0:T(8,128)S(1)}, u32[]{:S(2)}, u32[]{:S(2)}) collective-permute-start(f32[152,128]{1,0:T(8,128)S(1)} %shard_map.108.refs_2_), channel_id=1, source_target_pairs={{0,16},{1,17},{2,18},{3,19},{4,20},{5,21},{6,22},{7,23},{8,24},{9,... | collective-permute-start | bytes 233480 | tf_op jit(solution)/shard_map/ppermute | solution.py:386
  106.5 6.1 %collective-permute-start.37 = (f32[144,128]{1,0:T(8,128)S(1)}, f32[144,128]{1,0:T(8,128)S(1)}, u32[]{:S(2)}, u32[]{:S(2)}) collective-permute-start(f32[144,128]{1,0:T(8,128)S(1)} %shard_map.104.refs_0_), channel_id=1, source_target_pairs={{0,16},{1,17},{2,18},{3,19},{4,20},{5,21},{6,22},{7,23},{8,24},{9,... | collective-permute-start | bytes 221192 | tf_op jit(solution)/shard_map/ppermute | solution.py:386
  112.7 6.8 %collective-permute-start.44 = (f32[96,384]{1,0:T(8,128)S(1)}, f32[96,384]{1,0:T(8,128)S(1)}, u32[]{:S(2)}, u32[]{:S(2)}) collective-permute-start(f32[96,384]{1,0:T(8,128)S(1)} %get-tuple-element.108.refs_0_), channel_id=1, source_target_pairs={{0,8},{1,9},{2,10},{3,11},{4,12},{5,13},{6,14},{7,15},{8,0},{9,1},... | collective-permute-start | bytes 442376 | tf_op jit(solution)/shard_map/ppermute | solution.py:386
  112.8 8.4 %collective-permute-start.45 = (f32[96,384]{1,0:T(8,128)S(1)}, f32[96,384]{1,0:T(8,128)S(1)}, u32[]{:S(2)}, u32[]{:S(2)}) collective-permute-start(f32[96,384]{1,0:T(8,128)S(1)} %get-tuple-element.108.refs_0_), channel_id=1, source_target_pairs={{0,4},{1,5},{2,6},{3,7},{4,0},{5,1},{6,2},{7,3},{8,12},{9,13},{10,... | collective-permute-start | bytes 442376 | tf_op jit(solution)/shard_map/ppermute | solution.py:386
  113.6 7.6 %collective-permute-start.46 = (f32[96,384]{1,0:T(8,128)S(1)}, f32[96,384]{1,0:T(8,128)S(1)}, u32[]{:S(2)}, u32[]{:S(2)}) collective-permute-start(f32[96,384]{1,0:T(8,128)S(1)} %get-tuple-element.108.refs_0_), channel_id=1, source_target_pairs={{0,12},{1,13},{2,14},{3,15},{4,8},{5,9},{6,10},{7,11},{8,4},{9,5},... | collective-permute-start | bytes 442376 | tf_op jit(solution)/shard_map/ppermute | solution.py:386
  (30 other events, 136.3 us)
